TPU v7x, 256 devices: a whole 4x4x8 slice. The times are simulated.
256 devices in a mesh: sector: 32 (over z, y), mpo: 8 (over x, core).
Axes of the slice: x: 4, y: 4, z: 8, core: 2. Of those that a mesh axis runs over, the one named last changes fastest.
Arguments:
- guess: float32 [512, 128, 128], P('sector'), may hold values from -64 to 64
- diag_shift: float32 [512, 128, 128], P('sector'), may hold values from 0 to 6
- block_rows: int32 [512], P('sector'), may hold values from 64 to 128
- block_cols: int32 [512], P('sector'), may hold values from 64 to 128
- left_env: bfloat16 [64, 512, 128, 128], P('mpo', 'sector'), may hold values from -2 to 2
- right_env: bfloat16 [64, 512, 128, 128], P('mpo', 'sector'), may hold values from -2 to 2
- edge_input: int32 [1024], P('sector'), may hold values from 0 to 15
- edge_left: int32 [1024], P('sector'), may hold values from 0 to 15
- edge_right: int32 [1024], P('sector'), may hold values from 0 to 15
- edge_owner: int32 [1024, 1], P('sector'), may hold values from 0 to 31, as said below
- edge_slot: int32 [1024], P('sector'), may hold values from 0 to 15, as said below
Outputs:
- images: float32 [3, 512, 128, 128], P(None, 'sector', 'mpo')
- next_basis: float32 [512, 128, 128], P('sector', 'mpo')
- ritz: float32 [3], replicated
Inputs may be any that keep to these rules, and one draw needn't show every extreme that they name: `edge_owner`: among the 32 couplings of one index of sector, at most 2 name the same owner, and some owner is named by exactly 2. No coupling names the index of sector that holds it. `edge_slot`: couplings come in mirrored pairs: for every coupling e there is a coupling f with in_f = out_e and out_f = in_e.
All inputs are finite; a program needn't handle non-finite values.
Results may differ from a plain program's by a relative error of at most 0.025.
Values may be sent and summed in bfloat16 or wider, within the bound.
No kernel may reach another device: no remote copies, remote signals or barrier semaphores. Data moves between devices by JAX's collectives and lax.ppermute only.
A program may use at most 64 MiB of HBM per device.

v0:
```python
import jax
import jax.numpy as jnp
from jax import lax
from jax.sharding import PartitionSpec as P

APPLIES = 3


def per_device(
    guess,
    diag_shift,
    block_rows,
    block_cols,
    left_env,
    right_env,
    edge_input,
    edge_left,
    edge_right,
    edge_owner,
    edge_slot,
):
    slots, size, _ = guess.shape
    sectors = lax.axis_size("sector")
    terms_count = lax.axis_size("mpo")
    edges = edge_input.shape[0]
    capacity = max(2, 2 * edges // sectors)
    share = size // terms_count
    first_row = lax.axis_index("mpo") * share
    owner = edge_owner[:, 0]
    order = jnp.arange(edges, dtype=jnp.int32)
    earlier = (owner[:, None] == owner[None, :]) & (order[None, :] < order[:, None])
    rank = jnp.sum(earlier.astype(jnp.int32), axis=1)
    where_to = owner * capacity + rank
    place_hits = where_to[None, :] == jnp.arange(sectors * capacity, dtype=jnp.int32)[:, None]
    placing = place_hits.astype(jnp.bfloat16)
    slot_ids = (jnp.sum(jnp.where(place_hits, edge_slot[None, :] + 1, 0), axis=1) - 1).reshape(
        sectors, capacity
    )
    rows_index = lax.broadcasted_iota(jnp.int32, guess.shape, 1)
    cols_index = lax.broadcasted_iota(jnp.int32, guess.shape, 2)
    mask = (
        (rows_index < block_rows[:, None, None]) & (cols_index < block_cols[:, None, None])
    ).astype(jnp.float32)

    def own_rows(values, axis):
        return lax.dynamic_slice_in_dim(values, first_row, share, axis)

    def add_up(values):
        return lax.psum(values, "sector")

    def to_input(vector):
        return vector.astype(jnp.bfloat16)

    def deliver(total):
        rounded = total.astype(jnp.bfloat16)
        whole = lax.all_gather(rounded, "mpo", axis=1, tiled=True)
        packed = jnp.dot(
            placing, whole.reshape(edges, size * size), preferred_element_type=jnp.float32
        )
        packed = packed.astype(jnp.bfloat16).reshape(sectors, capacity, size, size)
        return (
            lax.all_to_all(packed, "sector", split_axis=0, concat_axis=0, tiled=True),
            lax.all_to_all(slot_ids, "sector", split_axis=0, concat_axis=0, tiled=True),
        )

    def apply_hamiltonian(vector):
        xin = to_input(vector)
        picked = xin[edge_input]

        def one_term(total, envs):
            left_term, right_term = envs
            half = jnp.einsum(
                "eij,ejk->eik", picked, right_term[edge_right], preferred_element_type=jnp.float32
            )
            half = half.astype(jnp.bfloat16)
            return (
                total
                + jnp.einsum(
                    "eij,ejk->eik", left_term[edge_left], half, preferred_element_type=jnp.float32
                ),
                None,
            )

        partial_sum, _ = lax.scan(
            one_term, jnp.zeros((edges, size, size), jnp.float32), (left_env, right_env)
        )
        rounded_terms = partial_sum.astype(jnp.bfloat16).astype(jnp.float32)
        total = lax.psum_scatter(
            rounded_terms.astype(jnp.bfloat16), "mpo", scatter_dimension=1, tiled=True
        ).astype(jnp.float32)
        arrived, arrived_ids = deliver(total)
        taking = (
            arrived_ids.reshape(-1)[None, :] == jnp.arange(slots, dtype=jnp.int32)[:, None]
        ).astype(jnp.bfloat16)
        gathered = jnp.dot(
            taking, arrived.reshape(sectors * capacity, -1), preferred_element_type=jnp.float32
        )
        return gathered.reshape(mask.shape) * mask

    start = mask * guess
    basis = [start / jnp.sqrt(add_up(jnp.sum(start * start)) + 1e-06)]
    image_list = []
    ritz_list = []
    for step in range(APPLIES):
        current = basis[-1]
        image = apply_hamiltonian(current)
        image_list.append(image)
        theta = add_up(jnp.sum(current * image))
        ritz_list.append(theta)
        corr = mask * (image - theta * current) / jnp.maximum(jnp.abs(diag_shift - theta), 1.0)
        projections = add_up(tuple((jnp.sum(vector * corr) for vector in basis)))
        ortho = corr
        for weight, vector in zip(projections, basis):
            ortho = ortho - weight * vector
        length = add_up(jnp.sum(ortho * ortho))
        basis.append(ortho / jnp.sqrt(length + 1e-06))
    stacked = jnp.stack(image_list)
    final = basis[-1]
    stacked = own_rows(stacked, 2)
    final = own_rows(final, 1)
    return (stacked, final, jnp.stack(ritz_list))


def solution(mesh):
    return jax.shard_map(
        per_device,
        mesh=mesh,
        in_specs=(
            P("sector", None, None),
            P("sector", None, None),
            P("sector"),
            P("sector"),
            P("mpo", "sector", None, None),
            P("mpo", "sector", None, None),
            P("sector"),
            P("sector"),
            P("sector"),
            P("sector", None),
            P("sector"),
        ),
        out_specs=(P(None, "sector", "mpo", None), P("sector", "mpo", None), P()),
        check_vma=False,
    )
```

profile of v0, /device:TPU:4, one launch (start us, length us, event | category | flops | bytes accessed | tf_op | source)
XLA Modules:
  0.0 1359.3 jit_solution(13275661166807130471)
XLA Ops:
  9.8 78.5 %psum.91 = f32[]{:T(128)} all-reduce(f32[]{:T(128)} %multiply_reduce_fusion.12), channel_id=1, replica_groups=mesh['sector'=32,'mpo'=8] {'sector'}, use_global_device_ids=true, to_apply=%region_3.4 | all-reduce | flops 1 | bytes 8 | tf_op jit(solution)/shard_map/psum | solution.py:49
  92.8 61.1 %while.33 = (s32[]{:T(128)}, f32[32,128,128]{2,1,0:T(8,128)}, bf16[8,16,128,128]{3,2,1,0:T(8,128)(2,1)}, s32[32]{0:T(128)S(1)}, bf16[8,16,128,128]{3,2,1,0:T(8,1...) while((s32[]{:T(128)}, f32[32,128,128]{2,1,0:T(8,128)}, ...), condition=%wide.region_5.6_spmd.clone, body=%wide.region_4.5_spmd.clone.sunk | while | flops 270010560 | bytes 13640811 | solution.py:84
  110.4 4.9 select_add_fusion.6
  118.1 4.9 select_add_fusion.6
  156.8 24.4 %reduce-scatter.4.cloned.1.call-done = bf16[32,16,128]{2,1,0:T(8,128)(2,1)} async-done(((bf16[32,128,128]{2,1,0:T(8,128)(2,1)}), bf16[32,16,128]{2,1,0:T(8,128)(2,1)}) %reduce-scatter.4.cloned.1.call-update) | async-done | bytes 131088 | tf_op jit(solution)/shard_map/reduce_scatter | solution.py:88
  182.2 9.9 all-to-all-start
  192.1 20.3 %all-gather.4.cloned.1.call-done = bf16[32,128,128]{2,1,0:T(8,128)(2,1)} async-done(((bf16[32,16,128]{2,1,0:T(8,128)(2,1)}), bf16[32,128,128]{2,1,0:T(8,128)(2,1)}) %all-gather.4.cloned.1.call-update) | async-done | bytes 1048592 | tf_op jit(solution)/shard_map/all_gather | solution.py:56
  216.4 10.0 all-to-all-start.1
  227.8 49.2 %all-to-all-done.1 = bf16[32,2,128,128]{3,2,1,0:T(8,128)(2,1)S(1)} async-done(((bf16[32,2,128,128]{3,2,1,0:T(8,128)(2,1)}), bf16[32,2,128,128]{3,2,1,0:T(8,128)(2,1)S(1)}, u32[]{:S(2)}, u32[]{:S(2)}) %all-to-all-start.1) | async-done | bytes 2097184 | tf_op jit(solution)/shard_map/all_to_all | solution.py:62
  282.4 72.4 %psum.92 = f32[]{:T(128)} all-reduce(f32[]{:T(128)} %get-tuple-element.297), channel_id=1, replica_groups=mesh['sector'=32,'mpo'=8] {'sector'}, use_global_device_ids=true, to_apply=%region_8.9 | all-reduce | flops 1 | bytes 8 | tf_op jit(solution)/shard_map/psum | solution.py:49
  357.4 70.2 %psum.93 = f32[]{:T(128)} all-reduce(f32[]{:T(128)} %multiply_reduce_fusion.10), channel_id=1, replica_groups=mesh['sector'=32,'mpo'=8] {'sector'}, use_global_device_ids=true, to_apply=%region_10.11 | all-reduce | flops 1 | bytes 8 | tf_op jit(solution)/shard_map/psum | solution.py:49
  430.9 72.4 %psum.94 = f32[]{:T(128)} all-reduce(f32[]{:T(128)} %multiply_reduce_fusion.9), channel_id=1, replica_groups=mesh['sector'=32,'mpo'=8] {'sector'}, use_global_device_ids=true, to_apply=%region_12.13 | all-reduce | flops 1 | bytes 8 | tf_op jit(solution)/shard_map/psum | solution.py:49
  509.5 61.1 %while.34 = (s32[]{:T(128)}, f32[32,128,128]{2,1,0:T(8,128)}, bf16[8,16,128,128]{3,2,1,0:T(8,128)(2,1)}, s32[32]{0:T(128)S(1)}, bf16[8,16,128,128]{3,2,1,0:T(8,1...) while((s32[]{:T(128)}, f32[32,128,128]{2,1,0:T(8,128)}, ...), condition=%wide.region_14.15_spmd.clone, body=%wide.region_13.14_spmd.clone.sunk | while | flops 270010560 | bytes 13640811 | solution.py:84
  534.8 4.9 select_add_fusion.7
  542.6 4.9 select_add_fusion.7
  573.4 26.6 %reduce-scatter.6.cloned.1.call-done = bf16[32,16,128]{2,1,0:T(8,128)(2,1)} async-done(((bf16[32,128,128]{2,1,0:T(8,128)(2,1)}), bf16[32,16,128]{2,1,0:T(8,128)(2,1)}) %reduce-scatter.6.cloned.1.call-update) | async-done | bytes 131088 | tf_op jit(solution)/shard_map/reduce_scatter | solution.py:88
  600.0 31.1 %all-gather.6.cloned.1.call-done = bf16[32,128,128]{2,1,0:T(8,128)(2,1)} async-done(((bf16[32,16,128]{2,1,0:T(8,128)(2,1)}), bf16[32,128,128]{2,1,0:T(8,128)(2,1)}) %all-gather.6.cloned.1.call-update) | async-done | bytes 1048592 | tf_op jit(solution)/shard_map/all_gather | solution.py:56
  635.1 10.0 all-to-all-start.2
  645.1 50.5 %all-to-all-done.2 = bf16[32,2,128,128]{3,2,1,0:T(8,128)(2,1)S(1)} async-done(((bf16[32,2,128,128]{3,2,1,0:T(8,128)(2,1)}), bf16[32,2,128,128]{3,2,1,0:T(8,128)(2,1)S(1)}, u32[]{:S(2)}, u32[]{:S(2)}) %all-to-all-start.2) | async-done | bytes 2097184 | tf_op jit(solution)/shard_map/all_to_all | solution.py:62
  701.6 72.3 %psum.95 = f32[]{:T(128)} all-reduce(f32[]{:T(128)} %get-tuple-element.299), channel_id=1, replica_groups=mesh['sector'=32,'mpo'=8] {'sector'}, use_global_device_ids=true, to_apply=%region_17.18 | all-reduce | flops 1 | bytes 8 | tf_op jit(solution)/shard_map/psum | solution.py:49
  778.6 70.3 %all-reduce.1 = (f32[]{:T(128)}, f32[]{:T(128)}) all-reduce(f32[]{:T(128)} %get-tuple-element.229, f32[]{:T(128)} %get-tuple-element.228), channel_id=1, replica_groups=mesh['sector'=32,'mpo'=8] {'sector'}, use_global_device_ids=true, to_apply=%region_21.22 | all-reduce | flops 2 | bytes 16 | tf_op jit(solution)/shard_map/psum | solution.py:49
  852.7 72.3 %psum.98 = f32[]{:T(128)} all-reduce(f32[]{:T(128)} %get-tuple-element.280), channel_id=1, replica_groups=mesh['sector'=32,'mpo'=8] {'sector'}, use_global_device_ids=true, to_apply=%region_23.24 | all-reduce | flops 1 | bytes 8 | tf_op jit(solution)/shard_map/psum | solution.py:49
  927.6 61.1 %while.35 = (s32[]{:T(128)}, f32[32,128,128]{2,1,0:T(8,128)}, bf16[8,16,128,128]{3,2,1,0:T(8,128)(2,1)}, s32[32]{0:T(128)S(1)}, bf16[8,16,128,128]{3,2,1,0:T(8,1...) while((s32[]{:T(128)}, f32[32,128,128]{2,1,0:T(8,128)}, ...), condition=%wide.region_25.26_spmd.clone, body=%wide.region_24.25_spmd.clone.sunk | while | flops 270010560 | bytes 13640811 | solution.py:84
  991.7 26.3 %reduce-scatter.8.cloned.1.call-done = bf16[32,16,128]{2,1,0:T(8,128)(2,1)} async-done(((bf16[32,128,128]{2,1,0:T(8,128)(2,1)}), bf16[32,16,128]{2,1,0:T(8,128)(2,1)}) %reduce-scatter.8.cloned.1.call-update) | async-done | bytes 131088 | tf_op jit(solution)/shard_map/reduce_scatter | solution.py:88
  1018.1 31.0 %all-gather.8.cloned.1.call-done = bf16[32,128,128]{2,1,0:T(8,128)(2,1)} async-done(((bf16[32,16,128]{2,1,0:T(8,128)(2,1)}), bf16[32,128,128]{2,1,0:T(8,128)(2,1)}) %all-gather.8.cloned.1.call-update) | async-done | bytes 1048592 | tf_op jit(solution)/shard_map/all_gather | solution.py:56
  1053.1 9.8 all-to-all-start.3
  1063.0 50.6 %all-to-all-done.3 = bf16[32,2,128,128]{3,2,1,0:T(8,128)(2,1)S(1)} async-done(((bf16[32,2,128,128]{3,2,1,0:T(8,128)(2,1)}), bf16[32,2,128,128]{3,2,1,0:T(8,128)(2,1)S(1)}, u32[]{:S(2)}, u32[]{:S(2)}) %all-to-all-start.3) | async-done | bytes 2097184 | tf_op jit(solution)/shard_map/all_to_all | solution.py:62
  1119.8 72.4 %psum.99 = f32[]{:T(128)} all-reduce(f32[]{:T(128)} %get-tuple-element.301), channel_id=1, replica_groups=mesh['sector'=32,'mpo'=8] {'sector'}, use_global_device_ids=true, to_apply=%region_28.29 | all-reduce | flops 1 | bytes 8 | tf_op jit(solution)/shard_map/psum | solution.py:49
  1192.1 5.2 multiply_reduce_fusion.3
  1197.4 70.3 %all-reduce = (f32[]{:T(128)}, f32[]{:T(128)}, f32[]{:T(128)}) all-reduce(f32[]{:T(128)} %get-tuple-element.226, f32[]{:T(128)} %get-tuple-element.227, f32[]{:T(128)} %get-tuple-element.225), channel_id=1, replica_groups=mesh['sector'=32,'mpo'=8] {'sector'}, use_global_device_ids=true, to_apply=%region_34.35 | all-reduce | flops 3 | bytes 24 | tf_op jit(solution)/shard_map/psum | solution.py:49
  1267.6 5.9 multiply_reduce_fusion
  1273.6 72.1 %psum.103 = f32[]{:T(128)} all-reduce(f32[]{:T(128)} %get-tuple-element.277), channel_id=1, replica_groups=mesh['sector'=32,'mpo'=8] {'sector'}, use_global_device_ids=true, to_apply=%region_36.37 | all-reduce | flops 1 | bytes 8 | tf_op jit(solution)/shard_map/psum | solution.py:49
  (264 shorter events, 237.5 us)
Async XLA Ops:
  7.2 84.0 %copy-start.18 = (s32[32]{0:T(128)S(1)}, s32[32]{0:T(128)}, u32[]{:S(2)}) copy-start(s32[32]{0:T(128)} %param.23) | copy-start | bytes 388
  7.2 174.0 %reduce-scatter.4.cloned.1.call-start = ((), (), s32[]{:S(2)}) async-start(), calls=%async_computation.7 | async-start | bytes 1179648 | tf_op jit(solution)/shard_map/reduce_scatter | solution.py:88
  89.0 3.8 copy-start.14
  89.0 3.8 copy-start.15
  153.9 27.3 %copy-start.20 = (s32[32,1]{0,1:T(1,128)S(1)}, s32[32,1]{0,1:T(1,128)}, u32[]{:S(2)}) copy-start(s32[32,1]{0,1:T(1,128)} %param.26) | copy-start | bytes 388
  153.9 27.5 %copy-start.19 = (s32[32]{0:T(128)S(1)}, s32[32]{0:T(128)}, u32[]{:S(2)}) copy-start(s32[32]{0:T(128)} %param.27) | copy-start | bytes 388
  156.7 55.6 %all-gather.4.cloned.1.call-start = ((), (), s32[]{:S(2)}) async-start(), calls=%async_computation.8 | async-start | bytes 1179648 | tf_op jit(solution)/shard_map/all_gather | solution.py:56
  182.2 34.2 %all-to-all-start = ((s32[32,1,2]{2,1,0:T(1,128)}), s32[32,1,2]{2,1,0:T(1,128)S(1)}, u32[]{:S(2)}, u32[]{:S(2)}) async-start(s32[32,1,2]{2,1,0:T(1,128)} %bitcast.1), calls=%async_computation | async-start | bytes 32768 | tf_op jit(solution)/shard_map/all_to_all | solution.py:63
  216.4 61.9 %copy-start = (f32[16,128,128]{2,1,0:T(8,128)S(1)}, f32[16,128,128]{2,1,0:T(8,128)}, u32[]{:S(2)}) copy-start(f32[16,128,128]{2,1,0:T(8,128)} %param.17) | copy-start | bytes 3145732
  216.4 61.9 %copy-start.16 = (s32[16]{0:T(128)S(1)}, s32[16]{0:T(128)}, u32[]{:S(2)}) copy-start(s32[16]{0:T(128)} %param.20) | copy-start | bytes 196
  216.4 61.9 %copy-start.17 = (s32[16]{0:T(128)S(1)}, s32[16]{0:T(128)}, u32[]{:S(2)}) copy-start(s32[16]{0:T(128)} %param.19) | copy-start | bytes 196
  216.4 60.6 %all-to-all-start.1 = ((bf16[32,2,128,128]{3,2,1,0:T(8,128)(2,1)}), bf16[32,2,128,128]{3,2,1,0:T(8,128)(2,1)S(1)}, u32[]{:S(2)}, u32[]{:S(2)}) async-start(bf16[32,2,128,128]{3,2,1,0:T(8,128)(2,1)} %bitcast.40), calls=%async_computation.2 | async-start | bytes 4194304 | tf_op jit(solution)/shard_map/all_to_all | solution.py:62
  226.4 373.6 %reduce-scatter.6.cloned.1.call-start = ((), (), s32[]{:S(2)}) async-start(), calls=%async_computation.9 | async-start | bytes 1179648 | tf_op jit(solution)/shard_map/reduce_scatter | solution.py:88
  277.0 1.4 copy-start.12
  278.3 76.4 %copy-start.3 = (f32[16,128,128]{2,1,0:T(8,128)S(1)}, f32[16,128,128]{2,1,0:T(8,128)}, u32[]{:S(2)}) copy-start(f32[16,128,128]{2,1,0:T(8,128)} %param.18) | copy-start | bytes 3145732
  282.4 221.6 %copy-start.8 = (f32[16,128,128]{2,0,1:T(8,128)}, f32[16,128,128]{2,0,1:T(8,128)S(1)}, u32[]{:S(2)}) copy-start(f32[16,128,128]{2,0,1:T(8,128)S(1)} %get-tuple-element.298) | copy-start | bytes 3145732
  573.4 57.7 %all-gather.6.cloned.1.call-start = ((), (), s32[]{:S(2)}) async-start(), calls=%async_computation.10 | async-start | bytes 1179648 | tf_op jit(solution)/shard_map/all_gather | solution.py:56
  635.1 61.8 %copy-start.6 = (f32[16,128,128]{2,0,1:T(8,128)S(1)}, f32[16,128,128]{2,0,1:T(8,128)}, u32[]{:S(2)}) copy-start(f32[16,128,128]{2,0,1:T(8,128)} %get-tuple-element.284) | copy-start | bytes 3145732
  635.1 60.5 %all-to-all-start.2 = ((bf16[32,2,128,128]{3,2,1,0:T(8,128)(2,1)}), bf16[32,2,128,128]{3,2,1,0:T(8,128)(2,1)S(1)}, u32[]{:S(2)}, u32[]{:S(2)}) async-start(bf16[32,2,128,128]{3,2,1,0:T(8,128)(2,1)} %bitcast.48), calls=%async_computation.4 | async-start | bytes 4194304 | tf_op jit(solution)/shard_map/all_to_all | solution.py:62
  645.1 373.0 %reduce-scatter.8.cloned.1.call-start = ((), (), s32[]{:S(2)}) async-start(), calls=%async_computation.11 | async-start | bytes 1179648 | tf_op jit(solution)/shard_map/reduce_scatter | solution.py:88
  695.6 1.3 copy-start.13
  696.9 76.9 %copy-start.1 = (f32[16,128,128]{2,1,0:T(8,128)S(1)}, f32[16,128,128]{2,1,0:T(8,128)}, u32[]{:S(2)}) copy-start(f32[16,128,128]{2,1,0:T(8,128)} %param.17) | copy-start | bytes 3145732
  696.9 76.9 %copy-start.4 = (f32[16,128,128]{2,1,0:T(8,128)S(1)}, f32[16,128,128]{2,1,0:T(8,128)}, u32[]{:S(2)}) copy-start(f32[16,128,128]{2,1,0:T(8,128)} %param.18) | copy-start | bytes 3145732
  852.7 74.9 %copy-start.10 = (f32[16,128,128]{2,0,1:T(8,128)}, f32[16,128,128]{2,0,1:T(8,128)S(1)}, u32[]{:S(2)}) copy-start(f32[16,128,128]{2,0,1:T(8,128)S(1)} %get-tuple-element.281) | copy-start | bytes 3145732
  991.4 57.6 %all-gather.8.cloned.1.call-start = ((), (), s32[]{:S(2)}) async-start(), calls=%async_computation.12 | async-start | bytes 1179648 | tf_op jit(solution)/shard_map/all_gather | solution.py:56
  1053.1 60.4 %all-to-all-start.3 = ((bf16[32,2,128,128]{3,2,1,0:T(8,128)(2,1)}), bf16[32,2,128,128]{3,2,1,0:T(8,128)(2,1)S(1)}, u32[]{:S(2)}, u32[]{:S(2)}) async-start(bf16[32,2,128,128]{3,2,1,0:T(8,128)(2,1)} %bitcast.56), calls=%async_computation.6 | async-start | bytes 4194304 | tf_op jit(solution)/shard_map/all_to_all | solution.py:62
  1113.5 1.4 copy-start.11
  1114.9 77.2 %copy-start.2 = (f32[16,128,128]{2,1,0:T(8,128)S(1)}, f32[16,128,128]{2,1,0:T(8,128)}, u32[]{:S(2)}) copy-start(f32[16,128,128]{2,1,0:T(8,128)} %param.17) | copy-start | bytes 3145732
  1114.9 77.2 %copy-start.5 = (f32[16,128,128]{2,1,0:T(8,128)S(1)}, f32[16,128,128]{2,1,0:T(8,128)}, u32[]{:S(2)}) copy-start(f32[16,128,128]{2,1,0:T(8,128)} %param.18) | copy-start | bytes 3145732
  1114.9 77.2 %copy-start.7 = (f32[16,128,128]{2,0,1:T(8,128)S(1)}, f32[16,128,128]{2,0,1:T(8,128)}, u32[]{:S(2)}) copy-start(f32[16,128,128]{2,0,1:T(8,128)} %get-tuple-element.284) | copy-start | bytes 3145732
  1267.6 80.4 %copy-start.9 = (f32[16,128,128]{2,0,1:T(8,128)S(1)}, f32[16,128,128]{2,0,1:T(8,128)}, u32[]{:S(2)}) copy-start(f32[16,128,128]{2,0,1:T(8,128)} %copy-done.8) | copy-start | bytes 3145732
Sparse Core Ops, SparseCore 0:
  156.8 24.2 reduce-scatter.3
  183.0 29.3 all-gather.3
  573.5 26.4 reduce-scatter.5
  601.7 29.3 all-gather.5
  991.6 26.4 reduce-scatter.7
  1019.7 29.2 all-gather.7
where the time goes:
time: 1360 us
  blocking collectives  723 us (53%)
  waiting for transfers between devices  310 us (23%)
  matrix products  135 us (10%)
  local copies, waits for them, and re-layouts  84.5 us (6%)
  other arithmetic  48.1 us (4%)
  starting transfers between devices  40.1 us (3%)
  between operations  17.1 us (1%)
    psum x10, blocking collectives, add_up(): return lax.psum(values, 'sector')  723 us
    all_to_all x3, waiting for transfers between devices, deliver(): lax.all_to_all(packed, 'sector', split_axis=0, concat_axis=0, tiled=True)  150 us
    dot_general x24, matrix products, one_term(): jnp.einsum('eij,ejk->eik', left_term[edge_left], half, preferred_element_...  115 us
    all_gather x3, waiting for transfers between devices, deliver(): whole = lax.all_gather(rounded, 'mpo', axis=1, tiled=True)  82.3 us
    reduce_scatter x3, waiting for transfers between devices, apply_hamiltonian(): lax.psum_scatter(rounded_terms.astype(jnp.bfloat16), 'mpo', scatter_dimen...  77.3 us
    squeeze x24, local copies, waits for them, and re-layouts, apply_hamiltonian(): lax.scan(one_term, jnp.zeros((edges, size, size), jnp.float32), (left_env...  30.4 us
    all_to_all x3, starting transfers between devices, deliver(): lax.all_to_all(packed, 'sector', split_axis=0, concat_axis=0, tiled=True)  29.8 us
  transfers between devices with their start and end apart: 10, of which 9 were waited for; matrix products, arithmetic and copies ran while one was open for 0% of the time, Pallas kernels for 0%

commit v1 on v0

v1 whole, which is shorter than its diff:
```python
import jax
import jax.numpy as jnp
from jax import lax
from jax.experimental import pallas as pl
from jax.experimental.pallas import tpu as pltpu
from jax.sharding import PartitionSpec as P

APPLIES = 3
CAP = 2
EXTRA = 8
ID_ROW = 4
UNROLL = 4
BF = jnp.bfloat16
F32 = jnp.float32
VMEM = pl.BlockSpec(memory_space=pltpu.VMEM)
SMEM = pl.BlockSpec(memory_space=pltpu.SMEM)
ROW_IN, ROW_LEFT, ROW_RIGHT, ROW_OWNER, ROW_SLOT, ROW_ROWS, ROW_COLS, ROW_POS = range(8)


def call(body, name, in_specs, out_shape, scratch=(), mib=8):
    return pl.pallas_call(
        body,
        name=name,
        in_specs=in_specs,
        out_shape=out_shape,
        out_specs=jax.tree.map(lambda _: VMEM, out_shape),
        scratch_shapes=scratch,
        compiler_params=pltpu.CompilerParams(vmem_limit_bytes=mib << 20),
    )


def out(shape, dtype):
    return jax.ShapeDtypeStruct(shape, dtype)


def total(values):
    return jnp.sum(jnp.sum(values, axis=0, keepdims=True), axis=1, keepdims=True)


def fold(values):
    return jnp.sum(values.reshape(-1, 8, values.shape[-1]), axis=0)


def three_parts(value, row, height):
    high = value.astype(BF).astype(F32)
    middle = (value - high).astype(BF).astype(F32)
    low = value - high - middle
    lane = lax.broadcasted_iota(jnp.int32, (height, 128), 1)
    line = lax.broadcasted_iota(jnp.int32, (height, 128), 0)
    spread = jnp.where(lane == 0, high, jnp.where(lane == 1, middle, jnp.where(lane == 2, low, 0.0)))
    return jnp.where(line == row, spread, 0.0)


def mask_of(meta, block, shape, first_row):
    line = lax.broadcasted_iota(jnp.int32, shape, 0) + first_row
    lane = lax.broadcasted_iota(jnp.int32, shape, 1)
    return (line < meta[ROW_ROWS, block]) & (lane < meta[ROW_COLS, block])


def start_kernel(slots, size, share):
    def body(meta, guess, vector, xin, own, sums):
        acc = jnp.zeros((8, size), F32)
        first_row = pl.multiple_of(meta[ROW_POS, 0] * share, share)
        for b in range(slots):
            value = jnp.where(mask_of(meta, b, (size, size), 0), guess[b], 0.0)
            vector[b] = value
            xin[b] = value.astype(BF)
            acc = acc + fold(value * value)
            mine = guess[b, pl.ds(first_row, share)]
            own[b] = jnp.where(mask_of(meta, b, (share, size), first_row), mine, 0.0)
        sums[...] = three_parts(total(acc), 0, EXTRA)

    return call(
        body,
        "start",
        [SMEM, VMEM],
        (
            out((slots, size, size), F32),
            out((slots, size, size), BF),
            out((slots, share, size), F32),
            out((EXTRA, size), F32),
        ),
    )


def couple_kernel(edges, size, share, group, chips):
    def body(meta, xin, right, left, own, send, tmp):
        x = meta[ROW_POS, 1]
        c = meta[ROW_POS, 2]

        def one(e, u):
            i = meta[ROW_IN, e]
            le = meta[ROW_LEFT, e]
            re = meta[ROW_RIGHT, e]
            value = xin[i]
            acc = None
            for w in range(group):
                half = jnp.dot(value, right[w, re], preferred_element_type=F32).astype(BF)
                term = jnp.dot(left[w, le], half, preferred_element_type=F32)
                acc = term if acc is None else acc + term
            tmp[u] = acc.astype(BF)
            for k in range(chips):
                to = lax.rem(x + k, chips)
                mine = pl.multiple_of((2 * to + c) * share, share)
                other = pl.multiple_of((2 * to + 1 - c) * share, share)
                own[k, e] = tmp[u, pl.ds(mine, share)]
                send[k, e] = tmp[u, pl.ds(other, share)]

        def step(t, carry):
            for u in range(UNROLL):
                one(t * UNROLL + u, u)
            return carry

        lax.fori_loop(0, edges // UNROLL, step, 0)

    shape = out((chips, edges, share, size), BF)
    return call(
        body,
        "couple",
        [SMEM, VMEM, VMEM, VMEM],
        (shape, shape),
        [pltpu.VMEM((UNROLL, size, size), BF)],
    )


def pair_kernel(edges, size, share, chips):
    def body(own, received, *parts):
        for k in range(chips):
            parts[k][...] = (own[k].astype(F32) + received[k].astype(F32)).astype(BF)

    return call(
        body, "pair", [VMEM, VMEM], tuple(out((edges, share, size), BF) for _ in range(chips))
    )


def pack_kernel(edges, size, share, sectors, with_ids):
    height = CAP * share + EXTRA

    def body(meta, sums, first, second, third, fourth, message, seen):
        message[...] = jnp.zeros_like(message)
        line = lax.broadcasted_iota(jnp.int32, (EXTRA, size), 0)
        lane = lax.broadcasted_iota(jnp.int32, (EXTRA, size), 1)
        tail = sums[...]
        if with_ids:
            tail = jnp.where((line == ID_ROW) & (lane < CAP), -1.0, tail)
        for s in range(sectors):
            seen[s] = 0
            message[s, CAP * share :] = tail.astype(BF)
        for e in range(edges):
            owner = meta[ROW_OWNER, e]
            rank = seen[owner]
            seen[owner] = rank + 1
            value = first[e].astype(F32) + second[e].astype(F32)
            value = value + (third[e].astype(F32) + fourth[e].astype(F32))
            message[owner, pl.ds(pl.multiple_of(rank * share, share), share)] = value.astype(BF)
            if with_ids:
                slot = meta[ROW_SLOT, e].astype(F32)
                here = message[owner, CAP * share :].astype(F32)
                here = jnp.where((line == ID_ROW) & (lane == rank), slot, here)
                message[owner, CAP * share :] = here.astype(BF)

    return call(
        body,
        "pack",
        [SMEM] + [VMEM] * 5,
        out((sectors, height, size), BF),
        [pltpu.SMEM((sectors,), jnp.int32)],
    )


def image_kernel(k, slots, size, share, sectors):
    def body(meta, ids, arrived, vector, state, *refs):
        bases = refs[: k - 1]
        images = refs[k - 1 : 2 * k - 2]
        image, basis, message, new_state, acc = refs[2 * k - 2 :]
        sums = jnp.zeros((EXTRA, size), F32)
        acc[...] = jnp.zeros_like(acc)
        for s in range(sectors):
            sums = sums + arrived[s, CAP * share :].astype(F32)
            for c in range(CAP):
                slot = ids[s * CAP + c]
                acc[slot] = acc[slot] + arrived[s, c * share : (c + 1) * share].astype(F32)
        sums = jnp.sum(sums, axis=1, keepdims=True)
        total_of = [sums[j : j + 1] for j in range(k)]
        new_state[...] = state[...]

        def gram(i, j):
            row = 8 + 4 * max(i, j) + min(i, j)
            return state[row : row + 1, 0:1]

        def keep(row, value):
            new_state[row : row + 1] = jnp.broadcast_to(value, (1, size))

        project = total_of[: k - 1]
        length = total_of[k - 1]
        crossed = []
        for i in range(k - 1):
            mixed = jnp.zeros((1, 1), F32)
            for j in range(k - 1):
                mixed = mixed + gram(i, j) * project[j]
            crossed.append(mixed)
            length = length + project[i] * (mixed - 2.0 * project[i])
        length = jnp.maximum(length, 0.0)
        scale = 1.0 / jnp.sqrt(length + 1e-6)
        keep(4, scale)
        for j in range(k - 1):
            keep(5 + j, project[j])
            keep(8 + 4 * (k - 1) + j, scale * (project[j] - crossed[j]))
        keep(8 + 4 * (k - 1) + k - 1, length * scale * scale)
        first_row = meta[ROW_POS, 0] * share
        theta = jnp.zeros((8, size), F32)
        for b in range(slots):
            value = jnp.where(mask_of(meta, b, (share, size), first_row), acc[b], 0.0)
            direction = vector[b]
            for j in range(k - 1):
                value = value - project[j] * images[j][b]
                direction = direction - project[j] * bases[j][b]
            value = value * scale
            direction = direction * scale
            image[b] = value
            basis[b] = direction
            message[b] = value.astype(BF)
            theta = theta + fold(value * direction)
        message[slots] = three_parts(total(theta), 0, share).astype(BF)

    return call(
        body,
        "image",
        [SMEM, SMEM] + [VMEM] * (3 + 2 * (k - 1)),
        (
            out((slots, share, size), F32),
            out((slots, share, size), F32),
            out((slots + 1, share, size), BF),
            out((24, size), F32),
        ),
        [pltpu.VMEM((slots + 1, share, size), F32)],
    )


def spread_kernel(slots, size, sectors):
    def body(gathered, message):
        value = total(gathered[slots].astype(F32))
        message[...] = jnp.broadcast_to(value[None], (sectors, 1, size))

    return call(body, "spread", [VMEM], out((sectors, 1, size), F32))


def correct_kernel(k, slots, size, share, sectors, last):
    def body(meta, thetas, gathered, vector, shift, image, basis, state, *refs):
        bases = refs[: k - 1]
        if last:
            corrected, sums, new_state = refs[k - 1 :]
        else:
            whole_basis, whole, xin, corrected, sums, new_state = refs[k - 1 :]
        theta = jnp.sum(thetas[...].reshape(sectors, size), axis=0, keepdims=True)
        new_state[...] = state[...]
        new_state[k - 1 : k] = theta
        scale = state[4:5]
        project = [state[5 + j : 6 + j] for j in range(k - 1)]
        first_row = pl.multiple_of(meta[ROW_POS, 0] * share, share)

        def residual(mask, value, direction, moved):
            bottom = jnp.maximum(jnp.abs(moved - theta), 1.0)
            return jnp.where(mask, (value - theta * direction) / bottom, 0.0)

        def step(b, carry):
            direction = vector[b]
            for j in range(k - 1):
                direction = direction - project[j] * bases[j][b]
            direction = direction * scale
            value = residual(
                mask_of(meta, b, (size, size), 0),
                gathered[b].astype(F32),
                direction,
                shift[b],
            )
            if not last:
                whole_basis[b] = direction
                whole[b] = value
                xin[b] = value.astype(BF)
            corrected[b] = residual(
                mask_of(meta, b, (share, size), first_row),
                image[b],
                basis[b],
                shift[b, pl.ds(first_row, share)],
            )
            others = [bases[j][b] for j in range(k - 1)] + [direction, value]
            return tuple(a + fold(value * o) for a, o in zip(carry, others))

        carry = lax.fori_loop(
            0, slots, step, tuple(jnp.zeros((8, size), F32) for _ in range(k + 1)), unroll=2
        )
        if last:
            line = lax.broadcasted_iota(jnp.int32, (EXTRA, size), 0)
            tail = jnp.zeros((EXTRA, size), F32)
            for j in range(k + 1):
                tail = jnp.where(line == j, total(carry[j]), tail)
            sums[...] = jnp.broadcast_to(tail[None], (sectors, EXTRA, size))
        else:
            tail = jnp.zeros((EXTRA, size), F32)
            for j in range(k + 1):
                tail = tail + three_parts(total(carry[j]), j, EXTRA)
            sums[...] = tail

    blocks = out((slots, size, size), F32)
    shapes = [out((slots, share, size), F32), out((EXTRA, size), F32), out((24, size), F32)]
    if last:
        shapes[1] = out((sectors, EXTRA, size), F32)
    else:
        shapes = [blocks, blocks, out((slots, size, size), BF)] + shapes
    return call(body, "correct", [SMEM] + [VMEM] * (6 + k), tuple(shapes))


def finish_kernel(slots, size, share, sectors):
    k = APPLIES

    def body(sums, vector, state, *refs):
        bases = refs[:k]
        images = refs[k : 2 * k]
        stacked, final, ritz = refs[2 * k :]
        added = jnp.sum(sums[...], axis=0)
        project = [added[j : j + 1] for j in range(k)]
        length = added[k : k + 1]
        for i in range(k):
            mixed = jnp.zeros((1, size), F32)
            for j in range(k):
                row = 8 + 4 * max(i, j) + min(i, j)
                mixed = mixed + state[row : row + 1] * project[j]
            length = length + project[i] * (mixed - 2.0 * project[i])
        scale = 1.0 / jnp.sqrt(jnp.maximum(length, 0.0) + 1e-6)
        for b in range(slots):
            value = vector[b]
            for j in range(k):
                value = value - project[j] * bases[j][b]
            final[b] = value * scale
            for j in range(k):
                stacked[j, b] = images[j][b]
        ritz[...] = state[0:8]

    return call(
        body,
        "finish",
        [VMEM] * (3 + 2 * k),
        (
            out((k, slots, share, size), F32),
            out((slots, share, size), F32),
            out((8, size), F32),
        ),
    )


def per_device(
    guess,
    diag_shift,
    block_rows,
    block_cols,
    left_env,
    right_env,
    edge_input,
    edge_left,
    edge_right,
    edge_owner,
    edge_slot,
):
    slots, size, _ = guess.shape
    sectors = lax.axis_size("sector")
    terms = lax.axis_size("mpo")
    edges = edge_input.shape[0]
    group = left_env.shape[0]
    share = size // terms
    chips = terms // 2
    place = lax.axis_index("mpo")
    core_swap = [(i, i ^ 1) for i in range(terms)]
    pos = jnp.stack([place, place // 2, place % 2]).astype(jnp.int32)

    def wide(row):
        return jnp.pad(row, (0, edges - row.shape[0]))

    meta = jnp.stack(
        [
            edge_input,
            edge_left,
            edge_right,
            edge_owner[:, 0],
            edge_slot,
            wide(block_rows),
            wide(block_cols),
            wide(pos),
        ]
    )

    def over_sector(values):
        return lax.all_to_all(values, "sector", 0, 0, tiled=True)

    def chip_shift(values, k):
        pairs = [(i, (i + 2 * k) % terms) for i in range(terms)]
        return lax.ppermute(values, "mpo", pairs)

    vector, xin, mine, sums = start_kernel(slots, size, share)(meta, guess)
    state = jnp.zeros((24, size), F32)
    bases, images, whole_bases = [], [], []
    ids = None
    for k in range(1, APPLIES + 1):
        own, send = couple_kernel(edges, size, share, group, chips)(
            meta, xin, right_env, left_env
        )
        received = lax.ppermute(send, "mpo", core_swap)
        parts = pair_kernel(edges, size, share, chips)(own, received)
        shifted = [parts[0]] + [chip_shift(parts[j], j) for j in range(1, chips)]
        message = pack_kernel(edges, size, share, sectors, k == 1)(meta, sums, *shifted)
        arrived = over_sector(message)
        if ids is None:
            ids = arrived[:, CAP * share + ID_ROW, :CAP].astype(jnp.int32).reshape(-1)
            ids = jnp.where(ids < 0, slots, ids)
        image, basis, outgoing, state = image_kernel(k, slots, size, share, sectors)(
            meta, ids, arrived, mine, state, *bases, *images
        )
        gathered = lax.all_gather(outgoing, "mpo", axis=1, tiled=True)
        thetas = over_sector(spread_kernel(slots, size, sectors)(gathered))
        last = k == APPLIES
        result = correct_kernel(k, slots, size, share, sectors, last)(
            meta, thetas, gathered, vector, diag_shift, image, basis, state, *whole_bases
        )
        if last:
            mine, sums, state = result
        else:
            whole_basis, vector, xin, mine, sums, state = result
            whole_bases.append(whole_basis)
        bases.append(basis)
        images.append(image)
    stacked, final, ritz = finish_kernel(slots, size, share, sectors)(
        over_sector(sums), mine, state, *bases, *images
    )
    return stacked, final, ritz[:APPLIES, 0]


def solution(mesh):
    return jax.shard_map(
        per_device,
        mesh=mesh,
        in_specs=(
            P("sector", None, None),
            P("sector", None, None),
            P("sector"),
            P("sector"),
            P("mpo", "sector", None, None),
            P("mpo", "sector", None, None),
            P("sector"),
            P("sector"),
            P("sector"),
            P("sector", None),
            P("sector"),
        ),
        out_specs=(P(None, "sector", "mpo", None), P("sector", "mpo", None), P()),
        check_vma=False,
    )
```

time: 1360 us -> 238 us (0.17)
  blocking collectives: 723 us -> 151 us
  waiting for transfers between devices: 310 us -> 22.8 us
  matrix products: 135 us -> 0 us
  local copies, waits for them, and re-layouts: 84.5 us -> 10.6 us
  other arithmetic: 48.1 us -> 0.14 us
  Pallas kernels: 0 us -> 35 us
  starting transfers between devices: 40.1 us -> 14.7 us
  between operations: 17.1 us -> 0.81 us
    psum x10 -> x0, blocking collectives: 723 us -> none  [add_up(): return lax.psum(values, 'sector')]
    all_to_all x4 -> x0, waiting for transfers between devices: 150 us -> none  [the longest x3 150 us: deliver(): lax.all_to_all(packed, 'sector', split_axis=0, concat_axis=0, tiled=True)]
    dot_general x30 -> x0, matrix products: 135 us -> none  [the longest x24 115 us: one_term(): jnp.einsum('eij,ejk->eik', left_term[edge_left], half, preferred_element_...]
    all_to_all x0 -> x7, blocking collectives: none -> 113 us  [over_sector(): return lax.all_to_all(values, 'sector', 0, 0, tiled=True)]
    all_gather x3 -> x0, waiting for transfers between devices: 82.3 us -> none  [deliver(): whole = lax.all_gather(rounded, 'mpo', axis=1, tiled=True)]
    reduce_scatter x3 -> x0, waiting for transfers between devices: 77.3 us -> none  [apply_hamiltonian(): lax.psum_scatter(rounded_terms.astype(jnp.bfloat16), 'mpo', scatter_dimen...]
    gather x51 -> x0, local copies, waits for them, and re-layouts: 40.9 us -> none  [the longest x24 18 us: one_term(): left_term[edge_left]]
    all_to_all x4 -> x0, starting transfers between devices: 39.7 us -> none  [the longest x3 29.8 us: deliver(): lax.all_to_all(packed, 'sector', split_axis=0, concat_axis=0, tiled=True)]
  transfers between devices with their start and end apart: 10 -> 12, of which waited for: 9 -> 12; matrix products, arithmetic and copies ran while one was open for 0% -> 0% of each run, Pallas kernels for 0% -> 0%
where the time goes in v1:
time: 238 us; the launch traced here: 235 us
  blocking collectives  151 us (63%)
  Pallas kernels  35 us (15%)
  waiting for transfers between devices  22.8 us (10%)
  starting transfers between devices  14.7 us (6%)
  local copies, waits for them, and re-layouts  10.6 us (4%)
    all_to_all x7, blocking collectives, over_sector(): return lax.all_to_all(values, 'sector', 0, 0, tiled=True)  113 us
    all_gather x3, blocking collectives, per_device(): gathered = lax.all_gather(outgoing, 'mpo', axis=1, tiled=True)  38.5 us
    pallas_call x3, Pallas kernels, per_device(): couple_kernel(edges, size, share, group, chips)  22.3 us
    ppermute x9, waiting for transfers between devices, chip_shift(): return lax.ppermute(values, 'mpo', pairs)  17.1 us
    ppermute x9, starting transfers between devices, chip_shift(): return lax.ppermute(values, 'mpo', pairs)  14.4 us
    unnamed x14, local copies, waits for them, and re-layouts  7.79 us
    ppermute x3, waiting for transfers between devices, per_device(): received = lax.ppermute(send, 'mpo', core_swap)  5.69 us
    pallas_call x3, Pallas kernels, per_device(): correct_kernel(k, slots, size, share, sectors, last)  4.76 us
  transfers between devices with their start and end apart: 12, of which 12 were waited for; matrix products, arithmetic and copies ran while one was open for 0% of the time, Pallas kernels for 0%

profile of v1, /device:TPU:4, one launch (start us, length us, event | category | flops | bytes accessed | tf_op | source)
XLA Modules:
  0.0 235.4 jit_solution(15867461080124120010)
XLA Ops:
  4.9 2.2 copy-done
  7.1 2.2 copy-done.2
  9.3 7.4 %couple.3 = (bf16[4,32,16,128]{3,2,1,0:T(8,128)(2,1)S(1)}, bf16[4,32,16,128]{3,2,1,0:T(8,128)(2,1)S(1)}) custom-call(s32[8,32]{1,0:T(8,128)S(1)} %stack.47.meta, bf16[16,128,128]{2,1,0:T(8,128)(2,1)S(1)} %get-tuple-element.56.xin, bf16[8,16,128,128]{3,2,1,0:T(8,128)(2,1)S(1)} %copy-done, bf16[8,16,128,128]{3,2,1,0:T(8,128)(2,1)S(1)} %copy-done.2), custom_call_target="tpu_custom_call" | custom-call | tf_op jit(solution)/shard_map/couple/pallas_call | solution.py:404
  16.8 1.9 collective-permute-done.received
  21.2 2.5 %collective-permute-start.3 = (bf16[32,16,128]{2,1,0:T(8,128)(2,1)S(1)}, bf16[32,16,128]{2,1,0:T(8,128)(2,1)S(1)}, u32[]{:S(2)}, u32[]{:S(2)}) collective-permute-start(bf16[32,16,128]{2,1,0:T(8,128)(2,1)S(1)} %get-tuple-element.62), channel_id=1, source_target_pairs={{0,6},{1,7},{2,0},{3,1},{4,2},{5,3},{6,4},{7,5},{8,14},{9,15},{10,... | collective-permute-start | bytes 393224 | tf_op jit(solution)/shard_map/ppermute | solution.py:397
  24.6 3.2 %collective-permute-done.2.third = bf16[32,16,128]{2,1,0:T(8,128)(2,1)S(1)} collective-permute-done((bf16[32,16,128]{2,1,0:T(8,128)(2,1)S(1)}, bf16[32,16,128]{2,1,0:T(8,128)(2,1)S(1)}, u32[]{:S(2)}, u32[]{:S(2)}) %collective-permute-start.2) | collective-permute-done | bytes 131104 | tf_op jit(solution)/shard_map/ppermute | solution.py:397
  27.7 1.3 collective-permute-done.3.fourth
  30.0 24.7 %all_to_all.35.arrived = bf16[32,40,128]{2,1,0:T(8,128)(2,1)S(1)} all-to-all(bf16[32,40,128]{2,1,0:T(8,128)(2,1)S(1)} %pack.3), channel_id=1, replica_groups=mesh['sector'=32,'mpo'=8] {'sector'}, dimensions={0} | all-to-all | bytes 655360 | tf_op jit(solution)/shard_map/all_to_all | solution.py:393
  55.9 12.1 %all_gather.9.gathered = bf16[17,128,128]{2,1,0:T(8,128)(2,1)S(1)} all-gather(bf16[17,16,128]{2,1,0:T(8,128)(2,1)S(1)} %get-tuple-element.64), channel_id=1, replica_groups=mesh['sector'=32,'mpo'=8] {'mpo'}, dimensions={1}, use_global_device_ids=true | all-gather | bytes 626688 | tf_op jit(solution)/shard_map/all_gather | solution.py:418
  68.1 13.8 %all_to_all.36.thetas = f32[32,1,128]{2,1,0:T(1,128)S(1)} all-to-all(f32[32,1,128]{2,1,0:T(1,128)S(1)} %spread.3), channel_id=1, replica_groups=mesh['sector'=32,'mpo'=8] {'sector'}, dimensions={0} | all-to-all | bytes 32768 | tf_op jit(solution)/shard_map/all_to_all | solution.py:393
  81.9 1.4 correct.3
  83.3 2.2 copy-done.3
  85.5 7.4 %couple.4 = (bf16[4,32,16,128]{3,2,1,0:T(8,128)(2,1)S(1)}, bf16[4,32,16,128]{3,2,1,0:T(8,128)(2,1)S(1)}) custom-call(s32[8,32]{1,0:T(8,128)S(1)} %stack.47.meta, bf16[16,128,128]{2,1,0:T(8,128)(2,1)S(1)} %get-tuple-element.70.xin, bf16[8,16,128,128]{3,2,1,0:T(8,128)(2,1)S(1)} %copy-done.1, bf16[8,16,128,128]{3,2,1,0:T(8,128)(2,1)S(1)} %copy-done.3), custom_call_target="tpu_custom_call" | custom-call | tf_op jit(solution)/shard_map/couple/pallas_call | solution.py:404
  93.0 1.9 collective-permute-done.4.received
  95.1 2.5 %collective-permute-start.5 = (bf16[32,16,128]{2,1,0:T(8,128)(2,1)S(1)}, bf16[32,16,128]{2,1,0:T(8,128)(2,1)S(1)}, u32[]{:S(2)}, u32[]{:S(2)}) collective-permute-start(bf16[32,16,128]{2,1,0:T(8,128)(2,1)S(1)} %get-tuple-element.74), channel_id=1, source_target_pairs={{0,2},{1,3},{2,4},{3,5},{4,6},{5,7},{6,0},{7,1},{8,10},{9,11},{10,... | collective-permute-start | bytes 393224 | tf_op jit(solution)/shard_map/ppermute | solution.py:397
  98.4 1.4 collective-permute-start.7
  99.8 1.6 collective-permute-done.5.second
  101.4 3.2 %collective-permute-done.6.third = bf16[32,16,128]{2,1,0:T(8,128)(2,1)S(1)} collective-permute-done((bf16[32,16,128]{2,1,0:T(8,128)(2,1)S(1)}, bf16[32,16,128]{2,1,0:T(8,128)(2,1)S(1)}, u32[]{:S(2)}, u32[]{:S(2)}) %collective-permute-start.6) | collective-permute-done | bytes 131104 | tf_op jit(solution)/shard_map/ppermute | solution.py:397
  106.2 17.0 %all_to_all.37.arrived = bf16[32,40,128]{2,1,0:T(8,128)(2,1)S(1)} all-to-all(bf16[32,40,128]{2,1,0:T(8,128)(2,1)S(1)} %pack.4), channel_id=1, replica_groups=mesh['sector'=32,'mpo'=8] {'sector'}, dimensions={0} | all-to-all | bytes 655360 | tf_op jit(solution)/shard_map/all_to_all | solution.py:393
  124.1 13.3 %all_gather.10.gathered = bf16[17,128,128]{2,1,0:T(8,128)(2,1)S(1)} all-gather(bf16[17,16,128]{2,1,0:T(8,128)(2,1)S(1)} %get-tuple-element.79), channel_id=1, replica_groups=mesh['sector'=32,'mpo'=8] {'mpo'}, dimensions={1}, use_global_device_ids=true | all-gather | bytes 626688 | tf_op jit(solution)/shard_map/all_gather | solution.py:418
  137.6 13.5 %all_to_all.38.thetas = f32[32,1,128]{2,1,0:T(1,128)S(1)} all-to-all(f32[32,1,128]{2,1,0:T(1,128)S(1)} %spread.4), channel_id=1, replica_groups=mesh['sector'=32,'mpo'=8] {'sector'}, dimensions={0} | all-to-all | bytes 32768 | tf_op jit(solution)/shard_map/all_to_all | solution.py:393
  151.1 1.6 correct.4
  152.7 7.4 %couple.5 = (bf16[4,32,16,128]{3,2,1,0:T(8,128)(2,1)S(1)}, bf16[4,32,16,128]{3,2,1,0:T(8,128)(2,1)S(1)}) custom-call(s32[8,32]{1,0:T(8,128)S(1)} %stack.47.meta, bf16[16,128,128]{2,1,0:T(8,128)(2,1)S(1)} %get-tuple-element.86.xin, bf16[8,16,128,128]{3,2,1,0:T(8,128)(2,1)S(1)} %copy-done.1, bf16[8,16,128,128]{3,2,1,0:T(8,128)(2,1)S(1)} %copy-done.4), custom_call_target="tpu_custom_call" | custom-call | tf_op jit(solution)/shard_map/couple/pallas_call | solution.py:404
  160.2 1.9 collective-permute-done.8.received
  162.2 3.2 %collective-permute-start.9 = (bf16[32,16,128]{2,1,0:T(8,128)(2,1)S(1)}, bf16[32,16,128]{2,1,0:T(8,128)(2,1)S(1)}, u32[]{:S(2)}, u32[]{:S(2)}) collective-permute-start(bf16[32,16,128]{2,1,0:T(8,128)(2,1)S(1)} %get-tuple-element.90), channel_id=1, source_target_pairs={{0,2},{1,3},{2,4},{3,5},{4,6},{5,7},{6,0},{7,1},{8,10},{9,11},{10,... | collective-permute-start | bytes 393224 | tf_op jit(solution)/shard_map/ppermute | solution.py:397
  167.0 2.3 collective-permute-done.9.second
  169.3 3.2 %collective-permute-done.10.third = bf16[32,16,128]{2,1,0:T(8,128)(2,1)S(1)} collective-permute-done((bf16[32,16,128]{2,1,0:T(8,128)(2,1)S(1)}, bf16[32,16,128]{2,1,0:T(8,128)(2,1)S(1)}, u32[]{:S(2)}, u32[]{:S(2)}) %collective-permute-start.10) | collective-permute-done | bytes 131104 | tf_op jit(solution)/shard_map/ppermute | solution.py:397
  174.0 17.1 %all_to_all.39.arrived = bf16[32,40,128]{2,1,0:T(8,128)(2,1)S(1)} all-to-all(bf16[32,40,128]{2,1,0:T(8,128)(2,1)S(1)} %pack.5), channel_id=1, replica_groups=mesh['sector'=32,'mpo'=8] {'sector'}, dimensions={0} | all-to-all | bytes 655360 | tf_op jit(solution)/shard_map/all_to_all | solution.py:393
  192.2 13.1 %all_gather.11.gathered = bf16[17,128,128]{2,1,0:T(8,128)(2,1)S(1)} all-gather(bf16[17,16,128]{2,1,0:T(8,128)(2,1)S(1)} %get-tuple-element.95), channel_id=1, replica_groups=mesh['sector'=32,'mpo'=8] {'mpo'}, dimensions={1}, use_global_device_ids=true | all-gather | bytes 626688 | tf_op jit(solution)/shard_map/all_gather | solution.py:418
  205.4 13.3 %all_to_all.40.thetas = f32[32,1,128]{2,1,0:T(1,128)S(1)} all-to-all(f32[32,1,128]{2,1,0:T(1,128)S(1)} %spread.5), channel_id=1, replica_groups=mesh['sector'=32,'mpo'=8] {'sector'}, dimensions={0} | all-to-all | bytes 32768 | tf_op jit(solution)/shard_map/all_to_all | solution.py:393
  218.7 1.8 correct.5
  220.4 13.5 %all_to_all.41.sums = f32[32,8,128]{2,1,0:T(8,128)S(1)} all-to-all(f32[32,8,128]{2,1,0:T(8,128)S(1)} %get-tuple-element.101), channel_id=1, replica_groups=mesh['sector'=32,'mpo'=8] {'sector'}, dimensions={0} | all-to-all | bytes 262144 | tf_op jit(solution)/shard_map/all_to_all | solution.py:393
  (45 shorter events, 19.4 us)
Async XLA Ops:
  2.8 1.2 copy-start.6
  4.9 2.2 copy-start
  7.1 2.2 copy-start.2
  16.7 65.2 %copy-start.5 = (f32[16,128,128]{2,1,0:T(8,128)S(1)}, f32[16,128,128]{2,1,0:T(8,128)}, u32[]{:S(2)}) copy-start(f32[16,128,128]{2,1,0:T(8,128)} %shift.5) | copy-start | bytes 3145732
  16.7 2.0 collective-permute-start
  18.8 5.7 %collective-permute-start.1 = (bf16[32,16,128]{2,1,0:T(8,128)(2,1)S(1)}, bf16[32,16,128]{2,1,0:T(8,128)(2,1)S(1)}, u32[]{:S(2)}, u32[]{:S(2)}) collective-permute-start(bf16[32,16,128]{2,1,0:T(8,128)(2,1)S(1)} %get-tuple-element.60), channel_id=1, source_target_pairs={{0,2},{1,3},{2,4},{3,5},{4,6},{5,7},{6,0},{7,1},{8,10},{9,11},{10,... | collective-permute-start | bytes 393224 | tf_op jit(solution)/shard_map/ppermute | solution.py:397
  20.2 7.6 %collective-permute-start.2 = (bf16[32,16,128]{2,1,0:T(8,128)(2,1)S(1)}, bf16[32,16,128]{2,1,0:T(8,128)(2,1)S(1)}, u32[]{:S(2)}, u32[]{:S(2)}) collective-permute-start(bf16[32,16,128]{2,1,0:T(8,128)(2,1)S(1)} %get-tuple-element.61), channel_id=1, source_target_pairs={{0,4},{1,5},{2,6},{3,7},{4,0},{5,1},{6,2},{7,3},{8,12},{9,13},{10,... | collective-permute-start | bytes 393224 | tf_op jit(solution)/shard_map/ppermute | solution.py:397
  21.2 7.8 %collective-permute-start.3 = (bf16[32,16,128]{2,1,0:T(8,128)(2,1)S(1)}, bf16[32,16,128]{2,1,0:T(8,128)(2,1)S(1)}, u32[]{:S(2)}, u32[]{:S(2)}) collective-permute-start(bf16[32,16,128]{2,1,0:T(8,128)(2,1)S(1)} %get-tuple-element.62), channel_id=1, source_target_pairs={{0,6},{1,7},{2,0},{3,1},{4,2},{5,3},{6,4},{7,5},{8,14},{9,15},{10,... | collective-permute-start | bytes 393224 | tf_op jit(solution)/shard_map/ppermute | solution.py:397
  54.8 28.5 %copy-start.1 = (bf16[8,16,128,128]{3,2,1,0:T(8,128)(2,1)S(1)}, bf16[8,16,128,128]{3,2,1,0:T(8,128)(2,1)}, u32[]{:S(2)}) copy-start(bf16[8,16,128,128]{3,2,1,0:T(8,128)(2,1)} %right.5) | copy-start | bytes 12582916
  83.3 2.2 copy-start.3
  92.9 2.0 collective-permute-start.4
  94.9 57.7 %copy-start.4 = (bf16[8,16,128,128]{3,2,1,0:T(8,128)(2,1)S(1)}, bf16[8,16,128,128]{3,2,1,0:T(8,128)(2,1)}, u32[]{:S(2)}) copy-start(bf16[8,16,128,128]{3,2,1,0:T(8,128)(2,1)} %left.5) | copy-start | bytes 12582916
  95.1 6.4 %collective-permute-start.5 = (bf16[32,16,128]{2,1,0:T(8,128)(2,1)S(1)}, bf16[32,16,128]{2,1,0:T(8,128)(2,1)S(1)}, u32[]{:S(2)}, u32[]{:S(2)}) collective-permute-start(bf16[32,16,128]{2,1,0:T(8,128)(2,1)S(1)} %get-tuple-element.74), channel_id=1, source_target_pairs={{0,2},{1,3},{2,4},{3,5},{4,6},{5,7},{6,0},{7,1},{8,10},{9,11},{10,... | collective-permute-start | bytes 393224 | tf_op jit(solution)/shard_map/ppermute | solution.py:397
  97.6 7.1 %collective-permute-start.6 = (bf16[32,16,128]{2,1,0:T(8,128)(2,1)S(1)}, bf16[32,16,128]{2,1,0:T(8,128)(2,1)S(1)}, u32[]{:S(2)}, u32[]{:S(2)}) collective-permute-start(bf16[32,16,128]{2,1,0:T(8,128)(2,1)S(1)} %get-tuple-element.75), channel_id=1, source_target_pairs={{0,4},{1,5},{2,6},{3,7},{4,0},{5,1},{6,2},{7,3},{8,12},{9,13},{10,... | collective-permute-start | bytes 393224 | tf_op jit(solution)/shard_map/ppermute | solution.py:397
  98.4 7.0 %collective-permute-start.7 = (bf16[32,16,128]{2,1,0:T(8,128)(2,1)S(1)}, bf16[32,16,128]{2,1,0:T(8,128)(2,1)S(1)}, u32[]{:S(2)}, u32[]{:S(2)}) collective-permute-start(bf16[32,16,128]{2,1,0:T(8,128)(2,1)S(1)} %get-tuple-element.76), channel_id=1, source_target_pairs={{0,6},{1,7},{2,0},{3,1},{4,2},{5,3},{6,4},{7,5},{8,14},{9,15},{10,... | collective-permute-start | bytes 393224 | tf_op jit(solution)/shard_map/ppermute | solution.py:397
  160.1 2.0 collective-permute-start.8
  162.2 7.0 %collective-permute-start.9 = (bf16[32,16,128]{2,1,0:T(8,128)(2,1)S(1)}, bf16[32,16,128]{2,1,0:T(8,128)(2,1)S(1)}, u32[]{:S(2)}, u32[]{:S(2)}) collective-permute-start(bf16[32,16,128]{2,1,0:T(8,128)(2,1)S(1)} %get-tuple-element.90), channel_id=1, source_target_pairs={{0,2},{1,3},{2,4},{3,5},{4,6},{5,7},{6,0},{7,1},{8,10},{9,11},{10,... | collective-permute-start | bytes 393224 | tf_op jit(solution)/shard_map/ppermute | solution.py:397
  165.4 7.1 %collective-permute-start.10 = (bf16[32,16,128]{2,1,0:T(8,128)(2,1)S(1)}, bf16[32,16,128]{2,1,0:T(8,128)(2,1)S(1)}, u32[]{:S(2)}, u32[]{:S(2)}) collective-permute-start(bf16[32,16,128]{2,1,0:T(8,128)(2,1)S(1)} %get-tuple-element.91), channel_id=1, source_target_pairs={{0,4},{1,5},{2,6},{3,7},{4,0},{5,1},{6,2},{7,3},{8,12},{9,13},{10,... | collective-permute-start | bytes 393224 | tf_op jit(solution)/shard_map/ppermute | solution.py:397
  166.2 7.0 %collective-permute-start.11 = (bf16[32,16,128]{2,1,0:T(8,128)(2,1)S(1)}, bf16[32,16,128]{2,1,0:T(8,128)(2,1)S(1)}, u32[]{:S(2)}, u32[]{:S(2)}) collective-permute-start(bf16[32,16,128]{2,1,0:T(8,128)(2,1)S(1)} %get-tuple-element.92), channel_id=1, source_target_pairs={{0,6},{1,7},{2,0},{3,1},{4,2},{5,3},{6,4},{7,5},{8,14},{9,15},{10,... | collective-permute-start | bytes 393224 | tf_op jit(solution)/shard_map/ppermute | solution.py:397

commit v2 on v1

--- a/solution.py
+++ b/solution.py
@@ -14,16 +14,19 @@
 F32 = jnp.float32
 VMEM = pl.BlockSpec(memory_space=pltpu.VMEM)
 SMEM = pl.BlockSpec(memory_space=pltpu.SMEM)
-ROW_IN, ROW_LEFT, ROW_RIGHT, ROW_OWNER, ROW_SLOT, ROW_ROWS, ROW_COLS, ROW_POS = range(8)
-
-
-def call(body, name, in_specs, out_shape, scratch=(), mib=8):
+FAR = pl.BlockSpec(memory_space=pltpu.HBM)
+ROW_IN, ROW_LEFT, ROW_RIGHT, ROW_OWNER, ROW_SLOT, ROW_SIZES, ROW_POS = range(7)
+PIECES = 4
+
+
+def call(body, name, in_specs, out_shape, scratch=(), mib=8, aliases={}, out_specs=None):
     return pl.pallas_call(
         body,
         name=name,
         in_specs=in_specs,
         out_shape=out_shape,
-        out_specs=jax.tree.map(lambda _: VMEM, out_shape),
+        out_specs=out_specs or jax.tree.map(lambda _: VMEM, out_shape),
+        input_output_aliases=aliases,
         scratch_shapes=scratch,
         compiler_params=pltpu.CompilerParams(vmem_limit_bytes=mib << 20),
     )
@@ -51,40 +54,64 @@
     return jnp.where(line == row, spread, 0.0)
 
 
-def mask_of(meta, block, shape, first_row):
+def mask_of(meta, block, slots, shape, first_row):
     line = lax.broadcasted_iota(jnp.int32, shape, 0) + first_row
     lane = lax.broadcasted_iota(jnp.int32, shape, 1)
-    return (line < meta[ROW_ROWS, block]) & (lane < meta[ROW_COLS, block])
-
-
-def start_kernel(slots, size, share):
-    def body(meta, guess, vector, xin, own, sums):
+    return (line < meta[ROW_SIZES, block]) & (lane < meta[ROW_SIZES, slots + block])
+
+
+def start_kernel(slots, size, share, group):
+    def body(meta, far_guess, right, left, *refs):
+        vector, xin, own, sums, state, right_near, left_near, guess, sems, guess_sem = refs
+        state[...] = jnp.zeros_like(state)
+        first = pltpu.make_async_copy(far_guess, guess, guess_sem)
+        first.start()
+        copies = []
+        for i, (far, near) in enumerate(((right, right_near), (left, left_near))):
+            for p in range(PIECES):
+                part = pl.ds(p * (group // PIECES), group // PIECES)
+                copies.append(pltpu.make_async_copy(far.at[part], near.at[part], sems.at[i, p]))
+        for copy in copies:
+            copy.start()
         acc = jnp.zeros((8, size), F32)
         first_row = pl.multiple_of(meta[ROW_POS, 0] * share, share)
+        first.wait()
         for b in range(slots):
-            value = jnp.where(mask_of(meta, b, (size, size), 0), guess[b], 0.0)
+            value = jnp.where(mask_of(meta, b, slots, (size, size), 0), guess[b], 0.0)
             vector[b] = value
             xin[b] = value.astype(BF)
             acc = acc + fold(value * value)
             mine = guess[b, pl.ds(first_row, share)]
-            own[b] = jnp.where(mask_of(meta, b, (share, size), first_row), mine, 0.0)
+            own[b] = jnp.where(mask_of(meta, b, slots, (share, size), first_row), mine, 0.0)
         sums[...] = three_parts(total(acc), 0, EXTRA)
-
+        for copy in copies:
+            copy.wait()
+
+    near = pltpu.VMEM((group, slots, size, size), BF)
     return call(
         body,
         "start",
-        [SMEM, VMEM],
+        [SMEM, FAR, FAR, FAR],
         (
             out((slots, size, size), F32),
             out((slots, size, size), BF),
             out((slots, share, size), F32),
             out((EXTRA, size), F32),
+            out((24, size), F32),
+            near,
+            near,
         ),
-    )
-
-
-def couple_kernel(edges, size, share, group, chips):
-    def body(meta, xin, right, left, own, send, tmp):
+        [
+            pltpu.VMEM((slots, size, size), F32),
+            pltpu.SemaphoreType.DMA((2, PIECES)),
+            pltpu.SemaphoreType.DMA,
+        ],
+    )
+
+
+def couple_kernel(edges, slots, size, share, group, chips):
+    def body(meta, xin, right, left, own, send, *refs):
+        tmp = refs[-1]
         x = meta[ROW_POS, 1]
         c = meta[ROW_POS, 2]
 
@@ -114,12 +141,14 @@
         lax.fori_loop(0, edges // UNROLL, step, 0)
 
     shape = out((chips, edges, share, size), BF)
+    near = pltpu.VMEM((group, slots, size, size), BF)
     return call(
         body,
         "couple",
         [SMEM, VMEM, VMEM, VMEM],
-        (shape, shape),
+        (shape, shape, near, near),
         [pltpu.VMEM((UNROLL, size, size), BF)],
+        aliases={2: 2, 3: 3},
     )
 
 
@@ -133,7 +162,7 @@
     )
 
 
-def pack_kernel(edges, size, share, sectors, with_ids):
+def pack_kernel(edges, size, share, sectors):
     height = CAP * share + EXTRA
 
     def body(meta, sums, first, second, third, fourth, message, seen):
@@ -141,8 +170,7 @@
         line = lax.broadcasted_iota(jnp.int32, (EXTRA, size), 0)
         lane = lax.broadcasted_iota(jnp.int32, (EXTRA, size), 1)
         tail = sums[...]
-        if with_ids:
-            tail = jnp.where((line == ID_ROW) & (lane < CAP), -1.0, tail)
+        tail = jnp.where((line == ID_ROW) & (lane < CAP), -1.0, tail)
         for s in range(sectors):
             seen[s] = 0
             message[s, CAP * share :] = tail.astype(BF)
@@ -153,11 +181,10 @@
             value = first[e].astype(F32) + second[e].astype(F32)
             value = value + (third[e].astype(F32) + fourth[e].astype(F32))
             message[owner, pl.ds(pl.multiple_of(rank * share, share), share)] = value.astype(BF)
-            if with_ids:
-                slot = meta[ROW_SLOT, e].astype(F32)
-                here = message[owner, CAP * share :].astype(F32)
-                here = jnp.where((line == ID_ROW) & (lane == rank), slot, here)
-                message[owner, CAP * share :] = here.astype(BF)
+            slot = meta[ROW_SLOT, e].astype(F32)
+            here = message[owner, CAP * share :].astype(F32)
+            here = jnp.where((line == ID_ROW) & (lane == rank), slot, here)
+            message[owner, CAP * share :] = here.astype(BF)
 
     return call(
         body,
@@ -169,16 +196,22 @@
 
 
 def image_kernel(k, slots, size, share, sectors):
-    def body(meta, ids, arrived, vector, state, *refs):
+    def body(meta, arrived, vector, state, *refs):
         bases = refs[: k - 1]
         images = refs[k - 1 : 2 * k - 2]
-        image, basis, message, new_state, acc = refs[2 * k - 2 :]
+        image, basis, message, new_state, acc, slot_lanes, ids = refs[2 * k - 2 :]
+        line = lax.broadcasted_iota(jnp.int32, (EXTRA, size), 0)
+        for s in range(sectors):
+            tail = arrived[s, CAP * share :].astype(F32)
+            slot = jnp.sum(jnp.where(line == ID_ROW, tail, 0.0), axis=0, keepdims=True)
+            slot_lanes[s : s + 1] = jnp.where(slot < 0.0, float(slots), slot).astype(jnp.int32)
+        pltpu.sync_copy(slot_lanes, ids)
         sums = jnp.zeros((EXTRA, size), F32)
         acc[...] = jnp.zeros_like(acc)
         for s in range(sectors):
             sums = sums + arrived[s, CAP * share :].astype(F32)
             for c in range(CAP):
-                slot = ids[s * CAP + c]
+                slot = ids[s, c]
                 acc[slot] = acc[slot] + arrived[s, c * share : (c + 1) * share].astype(F32)
         sums = jnp.sum(sums, axis=1, keepdims=True)
         total_of = [sums[j : j + 1] for j in range(k)]
@@ -208,9 +241,8 @@
             keep(8 + 4 * (k - 1) + j, scale * (project[j] - crossed[j]))
         keep(8 + 4 * (k - 1) + k - 1, length * scale * scale)
         first_row = meta[ROW_POS, 0] * share
-        theta = jnp.zeros((8, size), F32)
         for b in range(slots):
-            value = jnp.where(mask_of(meta, b, (share, size), first_row), acc[b], 0.0)
+            value = jnp.where(mask_of(meta, b, slots, (share, size), first_row), acc[b], 0.0)
             direction = vector[b]
             for j in range(k - 1):
                 value = value - project[j] * images[j][b]
@@ -220,43 +252,81 @@
             image[b] = value
             basis[b] = direction
             message[b] = value.astype(BF)
-            theta = theta + fold(value * direction)
-        message[slots] = three_parts(total(theta), 0, share).astype(BF)
 
     return call(
         body,
         "image",
-        [SMEM, SMEM] + [VMEM] * (3 + 2 * (k - 1)),
+        [SMEM] + [VMEM] * (3 + 2 * (k - 1)),
         (
             out((slots, share, size), F32),
             out((slots, share, size), F32),
-            out((slots + 1, share, size), BF),
+            out((slots, share, size), BF),
             out((24, size), F32),
         ),
-        [pltpu.VMEM((slots + 1, share, size), F32)],
-    )
-
-
-def spread_kernel(slots, size, sectors):
-    def body(gathered, message):
-        value = total(gathered[slots].astype(F32))
-        message[...] = jnp.broadcast_to(value[None], (sectors, 1, size))
-
-    return call(body, "spread", [VMEM], out((sectors, 1, size), F32))
+        [
+            pltpu.VMEM((slots + 1, share, size), F32),
+            pltpu.VMEM((sectors, size), jnp.int32),
+            pltpu.SMEM((sectors, size), jnp.int32),
+        ],
+    )
+
+
+def gather_kernel(slots, size, share, chips):
+    def body(*refs):
+        for k in range(chips):
+            refs[chips][k] = refs[k][...]
+
+    return call(body, "gather", [VMEM] * chips, out((chips, slots, share, size), BF))
+
+
+def weigh_kernel(k, slots, size, share, sectors, chips):
+    def body(meta, mine, other, vector, state, *refs):
+        bases = refs[: k - 1]
+        image, basis, message = refs[k - 1 :]
+        x = meta[ROW_POS, 1]
+        c = meta[ROW_POS, 2]
+        for j in range(chips):
+            origin = 2 * lax.rem(x + chips - j, chips)
+            near = pl.multiple_of((origin + c) * share, share)
+            far = pl.multiple_of((origin + 1 - c) * share, share)
+            image[:, pl.ds(near, share)] = mine[j]
+            image[:, pl.ds(far, share)] = other[j]
+        scale = state[4:5]
+        project = [state[5 + j : 6 + j] for j in range(k - 1)]
+
+        def step(b, acc):
+            direction = vector[b]
+            for j in range(k - 1):
+                direction = direction - project[j] * bases[j][b]
+            direction = direction * scale
+            basis[b] = direction
+            return acc + fold(direction * image[b].astype(F32))
+
+        acc = lax.fori_loop(0, slots, step, jnp.zeros((8, size), F32), unroll=2)
+        message[...] = jnp.broadcast_to(total(acc)[None], (sectors, 1, size))
+
+    return call(
+        body,
+        "weigh",
+        [SMEM] + [VMEM] * (3 + k),
+        (
+            out((slots, size, size), BF),
+            out((slots, size, size), F32),
+            out((sectors, 1, size), F32),
+        ),
+    )
 
 
 def correct_kernel(k, slots, size, share, sectors, last):
-    def body(meta, thetas, gathered, vector, shift, image, basis, state, *refs):
+    def body(meta, thetas, whole_image, whole_basis, shift, image, basis, state, *refs):
         bases = refs[: k - 1]
         if last:
             corrected, sums, new_state = refs[k - 1 :]
         else:
-            whole_basis, whole, xin, corrected, sums, new_state = refs[k - 1 :]
+            whole, xin, corrected, sums, new_state = refs[k - 1 :]
         theta = jnp.sum(thetas[...].reshape(sectors, size), axis=0, keepdims=True)
         new_state[...] = state[...]
         new_state[k - 1 : k] = theta
-        scale = state[4:5]
-        project = [state[5 + j : 6 + j] for j in range(k - 1)]
         first_row = pl.multiple_of(meta[ROW_POS, 0] * share, share)
 
         def residual(mask, value, direction, moved):
@@ -264,22 +334,18 @@
             return jnp.where(mask, (value - theta * direction) / bottom, 0.0)
 
         def step(b, carry):
-            direction = vector[b]
-            for j in range(k - 1):
-                direction = direction - project[j] * bases[j][b]
-            direction = direction * scale
+            direction = whole_basis[b]
             value = residual(
-                mask_of(meta, b, (size, size), 0),
-                gathered[b].astype(F32),
+                mask_of(meta, b, slots, (size, size), 0),
+                whole_image[b].astype(F32),
                 direction,
                 shift[b],
             )
             if not last:
-                whole_basis[b] = direction
                 whole[b] = value
                 xin[b] = value.astype(BF)
             corrected[b] = residual(
-                mask_of(meta, b, (share, size), first_row),
+                mask_of(meta, b, slots, (share, size), first_row),
                 image[b],
                 basis[b],
                 shift[b, pl.ds(first_row, share)],
@@ -307,7 +373,7 @@
     if last:
         shapes[1] = out((sectors, EXTRA, size), F32)
     else:
-        shapes = [blocks, blocks, out((slots, size, size), BF)] + shapes
+        shapes = [blocks, out((slots, size, size), BF)] + shapes
     return call(body, "correct", [SMEM] + [VMEM] * (6 + k), tuple(shapes))
 
 
@@ -335,7 +401,8 @@
             final[b] = value * scale
             for j in range(k):
                 stacked[j, b] = images[j][b]
-        ritz[...] = state[0:8]
+        for j in range(k):
+            ritz[j] = jnp.max(state[j : j + 1])
 
     return call(
         body,
@@ -344,8 +411,9 @@
         (
             out((k, slots, share, size), F32),
             out((slots, share, size), F32),
-            out((8, size), F32),
+            out((k,), F32),
         ),
+        out_specs=(VMEM, VMEM, SMEM),
     )
 
 
@@ -371,11 +439,7 @@
     chips = terms // 2
     place = lax.axis_index("mpo")
     core_swap = [(i, i ^ 1) for i in range(terms)]
-    pos = jnp.stack([place, place // 2, place % 2]).astype(jnp.int32)
-
-    def wide(row):
-        return jnp.pad(row, (0, edges - row.shape[0]))
-
+    entry = jnp.arange(edges, dtype=jnp.int32)
     meta = jnp.stack(
         [
             edge_input,
@@ -383,9 +447,8 @@
             edge_right,
             edge_owner[:, 0],
             edge_slot,
-            wide(block_rows),
-            wide(block_cols),
-            wide(pos),
+            jnp.concatenate([block_rows, block_cols]),
+            jnp.where(entry == 0, place, jnp.where(entry == 1, place // 2, place % 2)),
         ]
     )
 
@@ -396,42 +459,48 @@
         pairs = [(i, (i + 2 * k) % terms) for i in range(terms)]
         return lax.ppermute(values, "mpo", pairs)
 
-    vector, xin, mine, sums = start_kernel(slots, size, share)(meta, guess)
-    state = jnp.zeros((24, size), F32)
+    def far(values):
+        return pltpu.with_memory_space_constraint(values, pltpu.HBM)
+
+    vector, xin, mine, sums, state, right_near, left_near = start_kernel(slots, size, share, group)(
+        meta, far(guess), far(right_env), far(left_env)
+    )
     bases, images, whole_bases = [], [], []
-    ids = None
     for k in range(1, APPLIES + 1):
-        own, send = couple_kernel(edges, size, share, group, chips)(
-            meta, xin, right_env, left_env
+        own, send, right_near, left_near = couple_kernel(edges, slots, size, share, group, chips)(
+            meta, xin, right_near, left_near
         )
         received = lax.ppermute(send, "mpo", core_swap)
         parts = pair_kernel(edges, size, share, chips)(own, received)
         shifted = [parts[0]] + [chip_shift(parts[j], j) for j in range(1, chips)]
-        message = pack_kernel(edges, size, share, sectors, k == 1)(meta, sums, *shifted)
+        message = pack_kernel(edges, size, share, sectors)(meta, sums, *shifted)
         arrived = over_sector(message)
-        if ids is None:
-            ids = arrived[:, CAP * share + ID_ROW, :CAP].astype(jnp.int32).reshape(-1)
-            ids = jnp.where(ids < 0, slots, ids)
         image, basis, outgoing, state = image_kernel(k, slots, size, share, sectors)(
-            meta, ids, arrived, mine, state, *bases, *images
+            meta, arrived, mine, state, *bases, *images
         )
-        gathered = lax.all_gather(outgoing, "mpo", axis=1, tiled=True)
-        thetas = over_sector(spread_kernel(slots, size, sectors)(gathered))
+        rows = [outgoing, chip_shift(outgoing, 1), None, chip_shift(outgoing, chips - 1)]
+        rows[2] = chip_shift(rows[1], 1)
+        near_rows = gather_kernel(slots, size, share, chips)(*rows)
+        far_rows = lax.ppermute(near_rows, "mpo", core_swap)
+        whole_image, whole_basis, parts = weigh_kernel(k, slots, size, share, sectors, chips)(
+            meta, near_rows, far_rows, vector, state, *whole_bases
+        )
+        thetas = over_sector(parts)
         last = k == APPLIES
         result = correct_kernel(k, slots, size, share, sectors, last)(
-            meta, thetas, gathered, vector, diag_shift, image, basis, state, *whole_bases
+            meta, thetas, whole_image, whole_basis, diag_shift, image, basis, state, *whole_bases
         )
         if last:
             mine, sums, state = result
         else:
-            whole_basis, vector, xin, mine, sums, state = result
+            vector, xin, mine, sums, state = result
             whole_bases.append(whole_basis)
         bases.append(basis)
         images.append(image)
     stacked, final, ritz = finish_kernel(slots, size, share, sectors)(
         over_sector(sums), mine, state, *bases, *images
     )
-    return stacked, final, ritz[:APPLIES, 0]
+    return stacked, final, ritz
 
 
 def solution(mesh):

time: 238 us -> 233 us (0.979)
  blocking collectives: 151 us -> 113 us
  starting transfers between devices: 14.7 us -> 33.1 us
  waiting for transfers between devices: 22.8 us -> 38 us
  local copies, waits for them, and re-layouts: 10.6 us -> 0.74 us
  Pallas kernels: 35 us -> 43.5 us
    all_gather x3 -> x0, blocking collectives: 38.5 us -> none  [per_device(): gathered = lax.all_gather(outgoing, 'mpo', axis=1, tiled=True)]
    ppermute x9 -> x18, starting transfers between devices: 14.4 us -> 32.5 us  [chip_shift(): return lax.ppermute(values, 'mpo', pairs)]
    ppermute x9 -> x18, waiting for transfers between devices: 17.1 us -> 27.8 us  [chip_shift(): return lax.ppermute(values, 'mpo', pairs)]
    unnamed x14 -> x2, local copies, waits for them, and re-layouts: 7.79 us -> 0.01 us
    pallas_call x10 -> x13, Pallas kernels: 25.9 us -> 32.6 us  [the longest x3 22.3 us: per_device(): couple_kernel(edges, slots, size, share, group, chips)]
    ppermute x0 -> x3, waiting for transfers between devices: none -> 4.57 us  [per_device(): far_rows = lax.ppermute(near_rows, 'mpo', core_swap)]
  transfers between devices with their start and end apart: 12 -> 24, of which waited for: 12 -> 19; matrix products, arithmetic and copies ran while one was open for 0% -> 0% of each run, Pallas kernels for 0% -> 0%
where the time goes in v2:
time: 233 us; the launch traced here: 230 us
  blocking collectives  113 us (48%)
  Pallas kernels  43.5 us (19%)
  waiting for transfers between devices  38 us (16%)
  starting transfers between devices  33.1 us (14%)
    all_to_all x7, blocking collectives, over_sector(): return lax.all_to_all(values, 'sector', 0, 0, tiled=True)  113 us
    ppermute x18, starting transfers between devices, chip_shift(): return lax.ppermute(values, 'mpo', pairs)  32.5 us
    ppermute x18, waiting for transfers between devices, chip_shift(): return lax.ppermute(values, 'mpo', pairs)  27.8 us
    pallas_call x3, Pallas kernels, per_device(): couple_kernel(edges, slots, size, share, group, chips)  22.3 us
    ppermute x3, waiting for transfers between devices, per_device(): received = lax.ppermute(send, 'mpo', core_swap)  5.69 us
    pallas_call x3, Pallas kernels, per_device(): image_kernel(k, slots, size, share, sectors)  5.33 us
  transfers between devices with their start and end apart: 24, of which 19 were waited for; matrix products, arithmetic and copies ran while one was open for 0% of the time, Pallas kernels for 0%

profile of v2, /device:TPU:4, one launch (start us, length us, event | category | flops | bytes accessed | tf_op | source)
XLA Modules:
  0.0 230.0 jit_solution(14173478033242169941)
XLA Ops:
  2.1 4.4 %start.1 = (f32[16,128,128]{2,1,0:T(8,128)S(1)}, bf16[16,128,128]{2,1,0:T(8,128)(2,1)S(1)}, f32[16,16,128]{2,1,0:T(8,128)S(1)}, f32[8,128]{1,0:T(8,128)S(1)}, f3...) custom-call(s32[7,32]{1,0:T(8,128)S(1)} %stack.24.meta, ...), custom_call_target="tpu_custom_call" | custom-call | tf_op jit(solution)/shard_map/start/pallas_call | solution.py:465
  6.6 7.4 %couple.3 = (bf16[4,32,16,128]{3,2,1,0:T(8,128)(2,1)S(1)}, bf16[4,32,16,128]{3,2,1,0:T(8,128)(2,1)S(1)}, bf16[8,16,128,128]{3,2,1,0:T(8,128)(2,1)S(1)}, bf16[8,16,128,128]{3,2,1,0:T(8,128)(2,1)S(1)}) custom-call(s32[7,32]{1,0:T(8,128)S(1)} %stack.24.meta, ...), custom_call_target="tpu_custom_call", output_to_operand_aliasing={{2}: (2, {}), {3}: (3, {})} | custom-call | tf_op jit(solution)/shard_map/couple/pallas_call | solution.py:470
  14.1 1.9 collective-permute-done.received
  18.5 2.5 %collective-permute-start.3 = (bf16[32,16,128]{2,1,0:T(8,128)(2,1)S(1)}, bf16[32,16,128]{2,1,0:T(8,128)(2,1)S(1)}, u32[]{:S(2)}, u32[]{:S(2)}) collective-permute-start(bf16[32,16,128]{2,1,0:T(8,128)(2,1)S(1)} %get-tuple-element.75), channel_id=1, source_target_pairs={{0,6},{1,7},{2,0},{3,1},{4,2},{5,3},{6,4},{7,5},{8,14},{9,15},{10,... | collective-permute-start | bytes 393224 | tf_op jit(solution)/shard_map/ppermute | solution.py:460
  21.9 3.2 %collective-permute-done.2.third = bf16[32,16,128]{2,1,0:T(8,128)(2,1)S(1)} collective-permute-done((bf16[32,16,128]{2,1,0:T(8,128)(2,1)S(1)}, bf16[32,16,128]{2,1,0:T(8,128)(2,1)S(1)}, u32[]{:S(2)}, u32[]{:S(2)}) %collective-permute-start.2) | collective-permute-done | bytes 131104 | tf_op jit(solution)/shard_map/ppermute | solution.py:460
  27.3 24.7 %all_to_all.35.arrived = bf16[32,40,128]{2,1,0:T(8,128)(2,1)S(1)} all-to-all(bf16[32,40,128]{2,1,0:T(8,128)(2,1)S(1)} %pack.3), channel_id=1, replica_groups=mesh['sector'=32,'mpo'=8] {'sector'}, dimensions={0} | all-to-all | bytes 655360 | tf_op jit(solution)/shard_map/all_to_all | solution.py:456
  55.8 2.2 collective-permute-done.4.refs_1_
  58.0 1.8 collective-permute-start.5
  59.9 2.5 %collective-permute-done.5.refs_2_ = bf16[16,16,128]{2,1,0:T(8,128)(2,1)S(1)} collective-permute-done((bf16[16,16,128]{2,1,0:T(8,128)(2,1)S(1)}, bf16[16,16,128]{2,1,0:T(8,128)(2,1)S(1)}, u32[]{:S(2)}, u32[]{:S(2)}) %collective-permute-start.5) | collective-permute-done | bytes 65568 | tf_op jit(solution)/shard_map/ppermute | solution.py:460
  64.9 14.2 %all_to_all.36.thetas = f32[32,1,128]{2,1,0:T(1,128)S(1)} all-to-all(f32[32,1,128]{2,1,0:T(1,128)S(1)} %get-tuple-element.81), channel_id=1, replica_groups=mesh['sector'=32,'mpo'=8] {'sector'}, dimensions={0} | all-to-all | bytes 32768 | tf_op jit(solution)/shard_map/all_to_all | solution.py:456
  80.5 7.4 %couple.4 = (bf16[4,32,16,128]{3,2,1,0:T(8,128)(2,1)S(1)}, bf16[4,32,16,128]{3,2,1,0:T(8,128)(2,1)S(1)}, bf16[8,16,128,128]{3,2,1,0:T(8,128)(2,1)S(1)}, bf16[8,16,128,128]{3,2,1,0:T(8,128)(2,1)S(1)}) custom-call(s32[7,32]{1,0:T(8,128)S(1)} %stack.24.meta, ...), custom_call_target="tpu_custom_call", output_to_operand_aliasing={{2}: (2, {}), {3}: (3, {})} | custom-call | tf_op jit(solution)/shard_map/couple/pallas_call | solution.py:470
  88.0 1.9 collective-permute-done.8.received
  93.2 2.5 %collective-permute-start.11 = (bf16[32,16,128]{2,1,0:T(8,128)(2,1)S(1)}, bf16[32,16,128]{2,1,0:T(8,128)(2,1)S(1)}, u32[]{:S(2)}, u32[]{:S(2)}) collective-permute-start(bf16[32,16,128]{2,1,0:T(8,128)(2,1)S(1)} %get-tuple-element.95), channel_id=1, source_target_pairs={{0,6},{1,7},{2,0},{3,1},{4,2},{5,3},{6,4},{7,5},{8,14},{9,15},{10,... | collective-permute-start | bytes 393224 | tf_op jit(solution)/shard_map/ppermute | solution.py:460
  95.7 4.0 %collective-permute-done.10.third = bf16[32,16,128]{2,1,0:T(8,128)(2,1)S(1)} collective-permute-done((bf16[32,16,128]{2,1,0:T(8,128)(2,1)S(1)}, bf16[32,16,128]{2,1,0:T(8,128)(2,1)S(1)}, u32[]{:S(2)}, u32[]{:S(2)}) %collective-permute-start.10) | collective-permute-done | bytes 131104 | tf_op jit(solution)/shard_map/ppermute | solution.py:460
  101.5 17.1 %all_to_all.37.arrived = bf16[32,40,128]{2,1,0:T(8,128)(2,1)S(1)} all-to-all(bf16[32,40,128]{2,1,0:T(8,128)(2,1)S(1)} %pack.4), channel_id=1, replica_groups=mesh['sector'=32,'mpo'=8] {'sector'}, dimensions={0} | all-to-all | bytes 655360 | tf_op jit(solution)/shard_map/all_to_all | solution.py:456
  120.4 3.3 %collective-permute-start.12 = (bf16[16,16,128]{2,1,0:T(8,128)(2,1)S(1)}, bf16[16,16,128]{2,1,0:T(8,128)(2,1)S(1)}, u32[]{:S(2)}, u32[]{:S(2)}) collective-permute-start(bf16[16,16,128]{2,1,0:T(8,128)(2,1)S(1)} %get-tuple-element.98.refs_0_), channel_id=1, source_target_pairs={{0,2},{1,3},{2,4},{3,5},{4,6},{5,7},{6,0},{7,1},{8,10},{9,11},{10,... | collective-permute-start | bytes 196616 | tf_op jit(solution)/shard_map/ppermute | solution.py:460
  123.7 2.1 collective-permute-done.12.refs_1_
  125.8 2.5 %collective-permute-start.13 = (bf16[16,16,128]{2,1,0:T(8,128)(2,1)S(1)}, bf16[16,16,128]{2,1,0:T(8,128)(2,1)S(1)}, u32[]{:S(2)}, u32[]{:S(2)}) collective-permute-start(bf16[16,16,128]{2,1,0:T(8,128)(2,1)S(1)} %collective-permute-done.12.refs_1_), channel_id=1, source_target_pairs={{0,2},{1,3},{2,4},{3,5},{4,6},{5,7},{6,0},{7,1},{8,10},{9,11},{10,... | collective-permute-start | bytes 196616 | tf_op jit(solution)/shard_map/ppermute | solution.py:460
  128.3 1.9 collective-permute-done.13.refs_2_
  132.9 13.2 %all_to_all.38.thetas = f32[32,1,128]{2,1,0:T(1,128)S(1)} all-to-all(f32[32,1,128]{2,1,0:T(1,128)S(1)} %get-tuple-element.101), channel_id=1, replica_groups=mesh['sector'=32,'mpo'=8] {'sector'}, dimensions={0} | all-to-all | bytes 32768 | tf_op jit(solution)/shard_map/all_to_all | solution.py:456
  147.5 7.4 %couple.5 = (bf16[4,32,16,128]{3,2,1,0:T(8,128)(2,1)S(1)}, bf16[4,32,16,128]{3,2,1,0:T(8,128)(2,1)S(1)}, bf16[8,16,128,128]{3,2,1,0:T(8,128)(2,1)S(1)}, bf16[8,16,128,128]{3,2,1,0:T(8,128)(2,1)S(1)}) custom-call(s32[7,32]{1,0:T(8,128)S(1)} %stack.24.meta, ...), custom_call_target="tpu_custom_call", output_to_operand_aliasing={{2}: (2, {}), {3}: (3, {})} | custom-call | tf_op jit(solution)/shard_map/couple/pallas_call | solution.py:470
  155.0 1.9 collective-permute-done.16.received
  157.0 2.5 %collective-permute-start.17 = (bf16[32,16,128]{2,1,0:T(8,128)(2,1)S(1)}, bf16[32,16,128]{2,1,0:T(8,128)(2,1)S(1)}, u32[]{:S(2)}, u32[]{:S(2)}) collective-permute-start(bf16[32,16,128]{2,1,0:T(8,128)(2,1)S(1)} %get-tuple-element.113), channel_id=1, source_target_pairs={{0,2},{1,3},{2,4},{3,5},{4,6},{5,7},{6,0},{7,1},{8,10},{9,11},{10,... | collective-permute-start | bytes 393224 | tf_op jit(solution)/shard_map/ppermute | solution.py:460
  161.0 2.5 %collective-permute-start.19 = (bf16[32,16,128]{2,1,0:T(8,128)(2,1)S(1)}, bf16[32,16,128]{2,1,0:T(8,128)(2,1)S(1)}, u32[]{:S(2)}, u32[]{:S(2)}) collective-permute-start(bf16[32,16,128]{2,1,0:T(8,128)(2,1)S(1)} %get-tuple-element.115), channel_id=1, source_target_pairs={{0,6},{1,7},{2,0},{3,1},{4,2},{5,3},{6,4},{7,5},{8,14},{9,15},{10,... | collective-permute-start | bytes 393224 | tf_op jit(solution)/shard_map/ppermute | solution.py:460
  163.5 4.0 %collective-permute-done.18.third = bf16[32,16,128]{2,1,0:T(8,128)(2,1)S(1)} collective-permute-done((bf16[32,16,128]{2,1,0:T(8,128)(2,1)S(1)}, bf16[32,16,128]{2,1,0:T(8,128)(2,1)S(1)}, u32[]{:S(2)}, u32[]{:S(2)}) %collective-permute-start.18) | collective-permute-done | bytes 131104 | tf_op jit(solution)/shard_map/ppermute | solution.py:460
  169.3 17.1 %all_to_all.39.arrived = bf16[32,40,128]{2,1,0:T(8,128)(2,1)S(1)} all-to-all(bf16[32,40,128]{2,1,0:T(8,128)(2,1)S(1)} %pack.5), channel_id=1, replica_groups=mesh['sector'=32,'mpo'=8] {'sector'}, dimensions={0} | all-to-all | bytes 655360 | tf_op jit(solution)/shard_map/all_to_all | solution.py:456
  188.2 3.3 %collective-permute-start.20 = (bf16[16,16,128]{2,1,0:T(8,128)(2,1)S(1)}, bf16[16,16,128]{2,1,0:T(8,128)(2,1)S(1)}, u32[]{:S(2)}, u32[]{:S(2)}) collective-permute-start(bf16[16,16,128]{2,1,0:T(8,128)(2,1)S(1)} %get-tuple-element.118.refs_0_), channel_id=1, source_target_pairs={{0,2},{1,3},{2,4},{3,5},{4,6},{5,7},{6,0},{7,1},{8,10},{9,11},{10,... | collective-permute-start | bytes 196616 | tf_op jit(solution)/shard_map/ppermute | solution.py:460
  191.5 2.1 collective-permute-done.20.refs_1_
  193.6 2.5 %collective-permute-start.21 = (bf16[16,16,128]{2,1,0:T(8,128)(2,1)S(1)}, bf16[16,16,128]{2,1,0:T(8,128)(2,1)S(1)}, u32[]{:S(2)}, u32[]{:S(2)}) collective-permute-start(bf16[16,16,128]{2,1,0:T(8,128)(2,1)S(1)} %collective-permute-done.20.refs_1_), channel_id=1, source_target_pairs={{0,2},{1,3},{2,4},{3,5},{4,6},{5,7},{6,0},{7,1},{8,10},{9,11},{10,... | collective-permute-start | bytes 196616 | tf_op jit(solution)/shard_map/ppermute | solution.py:460
  196.1 1.9 collective-permute-done.21.refs_2_
  200.8 13.2 %all_to_all.40.thetas = f32[32,1,128]{2,1,0:T(1,128)S(1)} all-to-all(f32[32,1,128]{2,1,0:T(1,128)S(1)} %get-tuple-element.121), channel_id=1, replica_groups=mesh['sector'=32,'mpo'=8] {'sector'}, dimensions={0} | all-to-all | bytes 32768 | tf_op jit(solution)/shard_map/all_to_all | solution.py:456
  215.5 13.5 %all_to_all.41.sums = f32[32,8,128]{2,1,0:T(8,128)S(1)} all-to-all(f32[32,8,128]{2,1,0:T(8,128)S(1)} %get-tuple-element.126), channel_id=1, replica_groups=mesh['sector'=32,'mpo'=8] {'sector'}, dimensions={0} | all-to-all | bytes 262144 | tf_op jit(solution)/shard_map/all_to_all | solution.py:456
  (51 shorter events, 36.4 us)
Async XLA Ops:
  14.0 65.1 %copy-start = (f32[16,128,128]{2,1,0:T(8,128)S(1)}, f32[16,128,128]{2,1,0:T(8,128)}, u32[]{:S(2)}) copy-start(f32[16,128,128]{2,1,0:T(8,128)} %shift.5) | copy-start | bytes 3145732
  14.0 2.0 collective-permute-start
  16.1 5.7 %collective-permute-start.1 = (bf16[32,16,128]{2,1,0:T(8,128)(2,1)S(1)}, bf16[32,16,128]{2,1,0:T(8,128)(2,1)S(1)}, u32[]{:S(2)}, u32[]{:S(2)}) collective-permute-start(bf16[32,16,128]{2,1,0:T(8,128)(2,1)S(1)} %get-tuple-element.73), channel_id=1, source_target_pairs={{0,2},{1,3},{2,4},{3,5},{4,6},{5,7},{6,0},{7,1},{8,10},{9,11},{10,... | collective-permute-start | bytes 393224 | tf_op jit(solution)/shard_map/ppermute | solution.py:460
  17.5 7.6 %collective-permute-start.2 = (bf16[32,16,128]{2,1,0:T(8,128)(2,1)S(1)}, bf16[32,16,128]{2,1,0:T(8,128)(2,1)S(1)}, u32[]{:S(2)}, u32[]{:S(2)}) collective-permute-start(bf16[32,16,128]{2,1,0:T(8,128)(2,1)S(1)} %get-tuple-element.74), channel_id=1, source_target_pairs={{0,4},{1,5},{2,6},{3,7},{4,0},{5,1},{6,2},{7,3},{8,12},{9,13},{10,... | collective-permute-start | bytes 393224 | tf_op jit(solution)/shard_map/ppermute | solution.py:460
  18.5 7.8 %collective-permute-start.3 = (bf16[32,16,128]{2,1,0:T(8,128)(2,1)S(1)}, bf16[32,16,128]{2,1,0:T(8,128)(2,1)S(1)}, u32[]{:S(2)}, u32[]{:S(2)}) collective-permute-start(bf16[32,16,128]{2,1,0:T(8,128)(2,1)S(1)} %get-tuple-element.75), channel_id=1, source_target_pairs={{0,6},{1,7},{2,0},{3,1},{4,2},{5,3},{6,4},{7,5},{8,14},{9,15},{10,... | collective-permute-start | bytes 393224 | tf_op jit(solution)/shard_map/ppermute | solution.py:460
  53.7 4.3 %collective-permute-start.4 = (bf16[16,16,128]{2,1,0:T(8,128)(2,1)S(1)}, bf16[16,16,128]{2,1,0:T(8,128)(2,1)S(1)}, u32[]{:S(2)}, u32[]{:S(2)}) collective-permute-start(bf16[16,16,128]{2,1,0:T(8,128)(2,1)S(1)} %get-tuple-element.78.refs_0_), channel_id=1, source_target_pairs={{0,2},{1,3},{2,4},{3,5},{4,6},{5,7},{6,0},{7,1},{8,10},{9,11},{10,... | collective-permute-start | bytes 196616 | tf_op jit(solution)/shard_map/ppermute | solution.py:460
  55.0 4.9 %collective-permute-start.6 = (bf16[16,16,128]{2,1,0:T(8,128)(2,1)S(1)}, bf16[16,16,128]{2,1,0:T(8,128)(2,1)S(1)}, u32[]{:S(2)}, u32[]{:S(2)}) collective-permute-start(bf16[16,16,128]{2,1,0:T(8,128)(2,1)S(1)} %get-tuple-element.78.refs_0_), channel_id=1, source_target_pairs={{0,6},{1,7},{2,0},{3,1},{4,2},{5,3},{6,4},{7,5},{8,14},{9,15},{10,... | collective-permute-start | bytes 196616 | tf_op jit(solution)/shard_map/ppermute | solution.py:460
  58.0 4.3 %collective-permute-start.5 = (bf16[16,16,128]{2,1,0:T(8,128)(2,1)S(1)}, bf16[16,16,128]{2,1,0:T(8,128)(2,1)S(1)}, u32[]{:S(2)}, u32[]{:S(2)}) collective-permute-start(bf16[16,16,128]{2,1,0:T(8,128)(2,1)S(1)} %collective-permute-done.4.refs_1_), channel_id=1, source_target_pairs={{0,2},{1,3},{2,4},{3,5},{4,6},{5,7},{6,0},{7,1},{8,10},{9,11},{10,... | collective-permute-start | bytes 196616 | tf_op jit(solution)/shard_map/ppermute | solution.py:460
  62.3 1.6 collective-permute-start.7
  87.9 2.0 collective-permute-start.8
  90.0 5.7 %collective-permute-start.9 = (bf16[32,16,128]{2,1,0:T(8,128)(2,1)S(1)}, bf16[32,16,128]{2,1,0:T(8,128)(2,1)S(1)}, u32[]{:S(2)}, u32[]{:S(2)}) collective-permute-start(bf16[32,16,128]{2,1,0:T(8,128)(2,1)S(1)} %get-tuple-element.93), channel_id=1, source_target_pairs={{0,2},{1,3},{2,4},{3,5},{4,6},{5,7},{6,0},{7,1},{8,10},{9,11},{10,... | collective-permute-start | bytes 393224 | tf_op jit(solution)/shard_map/ppermute | solution.py:460
  91.5 8.2 %collective-permute-start.10 = (bf16[32,16,128]{2,1,0:T(8,128)(2,1)S(1)}, bf16[32,16,128]{2,1,0:T(8,128)(2,1)S(1)}, u32[]{:S(2)}, u32[]{:S(2)}) collective-permute-start(bf16[32,16,128]{2,1,0:T(8,128)(2,1)S(1)} %get-tuple-element.94), channel_id=1, source_target_pairs={{0,4},{1,5},{2,6},{3,7},{4,0},{5,1},{6,2},{7,3},{8,12},{9,13},{10,... | collective-permute-start | bytes 393224 | tf_op jit(solution)/shard_map/ppermute | solution.py:460
  93.2 7.4 %collective-permute-start.11 = (bf16[32,16,128]{2,1,0:T(8,128)(2,1)S(1)}, bf16[32,16,128]{2,1,0:T(8,128)(2,1)S(1)}, u32[]{:S(2)}, u32[]{:S(2)}) collective-permute-start(bf16[32,16,128]{2,1,0:T(8,128)(2,1)S(1)} %get-tuple-element.95), channel_id=1, source_target_pairs={{0,6},{1,7},{2,0},{3,1},{4,2},{5,3},{6,4},{7,5},{8,14},{9,15},{10,... | collective-permute-start | bytes 393224 | tf_op jit(solution)/shard_map/ppermute | solution.py:460
  120.4 5.5 %collective-permute-start.12 = (bf16[16,16,128]{2,1,0:T(8,128)(2,1)S(1)}, bf16[16,16,128]{2,1,0:T(8,128)(2,1)S(1)}, u32[]{:S(2)}, u32[]{:S(2)}) collective-permute-start(bf16[16,16,128]{2,1,0:T(8,128)(2,1)S(1)} %get-tuple-element.98.refs_0_), channel_id=1, source_target_pairs={{0,2},{1,3},{2,4},{3,5},{4,6},{5,7},{6,0},{7,1},{8,10},{9,11},{10,... | collective-permute-start | bytes 196616 | tf_op jit(solution)/shard_map/ppermute | solution.py:460
  123.7 4.6 %collective-permute-start.14 = (bf16[16,16,128]{2,1,0:T(8,128)(2,1)S(1)}, bf16[16,16,128]{2,1,0:T(8,128)(2,1)S(1)}, u32[]{:S(2)}, u32[]{:S(2)}) collective-permute-start(bf16[16,16,128]{2,1,0:T(8,128)(2,1)S(1)} %get-tuple-element.98.refs_0_), channel_id=1, source_target_pairs={{0,6},{1,7},{2,0},{3,1},{4,2},{5,3},{6,4},{7,5},{8,14},{9,15},{10,... | collective-permute-start | bytes 196616 | tf_op jit(solution)/shard_map/ppermute | solution.py:460
  125.8 4.4 %collective-permute-start.13 = (bf16[16,16,128]{2,1,0:T(8,128)(2,1)S(1)}, bf16[16,16,128]{2,1,0:T(8,128)(2,1)S(1)}, u32[]{:S(2)}, u32[]{:S(2)}) collective-permute-start(bf16[16,16,128]{2,1,0:T(8,128)(2,1)S(1)} %collective-permute-done.12.refs_1_), channel_id=1, source_target_pairs={{0,2},{1,3},{2,4},{3,5},{4,6},{5,7},{6,0},{7,1},{8,10},{9,11},{10,... | collective-permute-start | bytes 196616 | tf_op jit(solution)/shard_map/ppermute | solution.py:460
  130.2 1.6 collective-permute-start.15
  154.9 2.0 collective-permute-start.16
  157.0 6.5 %collective-permute-start.17 = (bf16[32,16,128]{2,1,0:T(8,128)(2,1)S(1)}, bf16[32,16,128]{2,1,0:T(8,128)(2,1)S(1)}, u32[]{:S(2)}, u32[]{:S(2)}) collective-permute-start(bf16[32,16,128]{2,1,0:T(8,128)(2,1)S(1)} %get-tuple-element.113), channel_id=1, source_target_pairs={{0,2},{1,3},{2,4},{3,5},{4,6},{5,7},{6,0},{7,1},{8,10},{9,11},{10,... | collective-permute-start | bytes 393224 | tf_op jit(solution)/shard_map/ppermute | solution.py:460
  159.5 8.0 %collective-permute-start.18 = (bf16[32,16,128]{2,1,0:T(8,128)(2,1)S(1)}, bf16[32,16,128]{2,1,0:T(8,128)(2,1)S(1)}, u32[]{:S(2)}, u32[]{:S(2)}) collective-permute-start(bf16[32,16,128]{2,1,0:T(8,128)(2,1)S(1)} %get-tuple-element.114), channel_id=1, source_target_pairs={{0,4},{1,5},{2,6},{3,7},{4,0},{5,1},{6,2},{7,3},{8,12},{9,13},{10,... | collective-permute-start | bytes 393224 | tf_op jit(solution)/shard_map/ppermute | solution.py:460
  161.0 7.4 %collective-permute-start.19 = (bf16[32,16,128]{2,1,0:T(8,128)(2,1)S(1)}, bf16[32,16,128]{2,1,0:T(8,128)(2,1)S(1)}, u32[]{:S(2)}, u32[]{:S(2)}) collective-permute-start(bf16[32,16,128]{2,1,0:T(8,128)(2,1)S(1)} %get-tuple-element.115), channel_id=1, source_target_pairs={{0,6},{1,7},{2,0},{3,1},{4,2},{5,3},{6,4},{7,5},{8,14},{9,15},{10,... | collective-permute-start | bytes 393224 | tf_op jit(solution)/shard_map/ppermute | solution.py:460
  188.2 5.4 %collective-permute-start.20 = (bf16[16,16,128]{2,1,0:T(8,128)(2,1)S(1)}, bf16[16,16,128]{2,1,0:T(8,128)(2,1)S(1)}, u32[]{:S(2)}, u32[]{:S(2)}) collective-permute-start(bf16[16,16,128]{2,1,0:T(8,128)(2,1)S(1)} %get-tuple-element.118.refs_0_), channel_id=1, source_target_pairs={{0,2},{1,3},{2,4},{3,5},{4,6},{5,7},{6,0},{7,1},{8,10},{9,11},{10,... | collective-permute-start | bytes 196616 | tf_op jit(solution)/shard_map/ppermute | solution.py:460
  191.5 4.6 %collective-permute-start.22 = (bf16[16,16,128]{2,1,0:T(8,128)(2,1)S(1)}, bf16[16,16,128]{2,1,0:T(8,128)(2,1)S(1)}, u32[]{:S(2)}, u32[]{:S(2)}) collective-permute-start(bf16[16,16,128]{2,1,0:T(8,128)(2,1)S(1)} %get-tuple-element.118.refs_0_), channel_id=1, source_target_pairs={{0,6},{1,7},{2,0},{3,1},{4,2},{5,3},{6,4},{7,5},{8,14},{9,15},{10,... | collective-permute-start | bytes 196616 | tf_op jit(solution)/shard_map/ppermute | solution.py:460
  193.6 4.4 %collective-permute-start.21 = (bf16[16,16,128]{2,1,0:T(8,128)(2,1)S(1)}, bf16[16,16,128]{2,1,0:T(8,128)(2,1)S(1)}, u32[]{:S(2)}, u32[]{:S(2)}) collective-permute-start(bf16[16,16,128]{2,1,0:T(8,128)(2,1)S(1)} %collective-permute-done.20.refs_1_), channel_id=1, source_target_pairs={{0,2},{1,3},{2,4},{3,5},{4,6},{5,7},{6,0},{7,1},{8,10},{9,11},{10,... | collective-permute-start | bytes 196616 | tf_op jit(solution)/shard_map/ppermute | solution.py:460
  198.0 1.6 collective-permute-start.23

commit v3 on v2

--- a/solution.py
+++ b/solution.py
@@ -9,14 +9,33 @@
 CAP = 2
 EXTRA = 8
 ID_ROW = 4
-UNROLL = 4
+UNROLL = 16
 BF = jnp.bfloat16
 F32 = jnp.float32
 VMEM = pl.BlockSpec(memory_space=pltpu.VMEM)
 SMEM = pl.BlockSpec(memory_space=pltpu.SMEM)
 FAR = pl.BlockSpec(memory_space=pltpu.HBM)
-ROW_IN, ROW_LEFT, ROW_RIGHT, ROW_OWNER, ROW_SLOT, ROW_SIZES, ROW_POS = range(7)
 PIECES = 4
+
+
+class Meta:
+    def __init__(self, ref, edges, slots):
+        self.ref, self.edges, self.slots = ref, edges, slots
+
+    def edge(self, column, e):
+        return self.ref[column * self.edges + e]
+
+    def rows(self, b):
+        return self.ref[5 * self.edges + b]
+
+    def cols(self, b):
+        return self.ref[5 * self.edges + self.slots + b]
+
+    def place(self):
+        return self.ref[5 * self.edges + 2 * self.slots]
+
+
+IN, LEFT, RIGHT, OWNER, SLOT = range(5)
 
 
 def call(body, name, in_specs, out_shape, scratch=(), mib=8, aliases={}, out_specs=None):
@@ -54,14 +73,15 @@
     return jnp.where(line == row, spread, 0.0)
 
 
-def mask_of(meta, block, slots, shape, first_row):
+def mask_of(meta, block, shape, first_row):
     line = lax.broadcasted_iota(jnp.int32, shape, 0) + first_row
     lane = lax.broadcasted_iota(jnp.int32, shape, 1)
-    return (line < meta[ROW_SIZES, block]) & (lane < meta[ROW_SIZES, slots + block])
-
-
-def start_kernel(slots, size, share, group):
+    return (line < meta.rows(block)) & (lane < meta.cols(block))
+
+
+def start_kernel(edges, slots, size, share, group):
     def body(meta, far_guess, right, left, *refs):
+        meta = Meta(meta, edges, slots)
         vector, xin, own, sums, state, right_near, left_near, guess, sems, guess_sem = refs
         state[...] = jnp.zeros_like(state)
         first = pltpu.make_async_copy(far_guess, guess, guess_sem)
@@ -74,15 +94,15 @@
         for copy in copies:
             copy.start()
         acc = jnp.zeros((8, size), F32)
-        first_row = pl.multiple_of(meta[ROW_POS, 0] * share, share)
+        first_row = pl.multiple_of(meta.place() * share, share)
         first.wait()
         for b in range(slots):
-            value = jnp.where(mask_of(meta, b, slots, (size, size), 0), guess[b], 0.0)
+            value = jnp.where(mask_of(meta, b, (size, size), 0), guess[b], 0.0)
             vector[b] = value
             xin[b] = value.astype(BF)
             acc = acc + fold(value * value)
             mine = guess[b, pl.ds(first_row, share)]
-            own[b] = jnp.where(mask_of(meta, b, slots, (share, size), first_row), mine, 0.0)
+            own[b] = jnp.where(mask_of(meta, b, (share, size), first_row), mine, 0.0)
         sums[...] = three_parts(total(acc), 0, EXTRA)
         for copy in copies:
             copy.wait()
@@ -111,14 +131,15 @@
 
 def couple_kernel(edges, slots, size, share, group, chips):
     def body(meta, xin, right, left, own, send, *refs):
+        meta = Meta(meta, edges, slots)
         tmp = refs[-1]
-        x = meta[ROW_POS, 1]
-        c = meta[ROW_POS, 2]
+        x = meta.place() // 2
+        c = lax.rem(meta.place(), 2)
 
         def one(e, u):
-            i = meta[ROW_IN, e]
-            le = meta[ROW_LEFT, e]
-            re = meta[ROW_RIGHT, e]
+            i = meta.edge(IN, e)
+            le = meta.edge(LEFT, e)
+            re = meta.edge(RIGHT, e)
             value = xin[i]
             acc = None
             for w in range(group):
@@ -162,29 +183,32 @@
     )
 
 
-def pack_kernel(edges, size, share, sectors):
+def pack_kernel(edges, slots, size, share, sectors, with_ids):
     height = CAP * share + EXTRA
 
     def body(meta, sums, first, second, third, fourth, message, seen):
+        meta = Meta(meta, edges, slots)
         message[...] = jnp.zeros_like(message)
         line = lax.broadcasted_iota(jnp.int32, (EXTRA, size), 0)
         lane = lax.broadcasted_iota(jnp.int32, (EXTRA, size), 1)
         tail = sums[...]
-        tail = jnp.where((line == ID_ROW) & (lane < CAP), -1.0, tail)
+        if with_ids:
+            tail = jnp.where((line == ID_ROW) & (lane < CAP), -1.0, tail)
         for s in range(sectors):
             seen[s] = 0
             message[s, CAP * share :] = tail.astype(BF)
         for e in range(edges):
-            owner = meta[ROW_OWNER, e]
+            owner = meta.edge(OWNER, e)
             rank = seen[owner]
             seen[owner] = rank + 1
             value = first[e].astype(F32) + second[e].astype(F32)
             value = value + (third[e].astype(F32) + fourth[e].astype(F32))
             message[owner, pl.ds(pl.multiple_of(rank * share, share), share)] = value.astype(BF)
-            slot = meta[ROW_SLOT, e].astype(F32)
-            here = message[owner, CAP * share :].astype(F32)
-            here = jnp.where((line == ID_ROW) & (lane == rank), slot, here)
-            message[owner, CAP * share :] = here.astype(BF)
+            if with_ids:
+                slot = meta.edge(SLOT, e).astype(F32)
+                here = message[owner, CAP * share :].astype(F32)
+                here = jnp.where((line == ID_ROW) & (lane == rank), slot, here)
+                message[owner, CAP * share :] = here.astype(BF)
 
     return call(
         body,
@@ -195,23 +219,31 @@
     )
 
 
-def image_kernel(k, slots, size, share, sectors):
+def image_kernel(k, edges, slots, size, share, sectors):
     def body(meta, arrived, vector, state, *refs):
+        meta = Meta(meta, edges, slots)
         bases = refs[: k - 1]
         images = refs[k - 1 : 2 * k - 2]
-        image, basis, message, new_state, acc, slot_lanes, ids = refs[2 * k - 2 :]
-        line = lax.broadcasted_iota(jnp.int32, (EXTRA, size), 0)
-        for s in range(sectors):
-            tail = arrived[s, CAP * share :].astype(F32)
-            slot = jnp.sum(jnp.where(line == ID_ROW, tail, 0.0), axis=0, keepdims=True)
-            slot_lanes[s : s + 1] = jnp.where(slot < 0.0, float(slots), slot).astype(jnp.int32)
-        pltpu.sync_copy(slot_lanes, ids)
+        if k == 1:
+            image, basis, message, new_state, ids, acc, slot_lanes, wide_ids = refs
+            line = lax.broadcasted_iota(jnp.int32, (EXTRA, size), 0)
+            for s in range(sectors):
+                tail = arrived[s, CAP * share :].astype(F32)
+                slot = jnp.sum(jnp.where(line == ID_ROW, tail, 0.0), axis=0, keepdims=True)
+                slot = jnp.where(slot < 0.0, float(slots), slot)
+                slot_lanes[s : s + 1] = slot.astype(jnp.int32)
+            pltpu.sync_copy(slot_lanes, wide_ids)
+            for s in range(sectors):
+                for c in range(CAP):
+                    ids[s * CAP + c] = wide_ids[s, c]
+        else:
+            ids, image, basis, message, new_state, acc = refs[2 * k - 2 :]
         sums = jnp.zeros((EXTRA, size), F32)
         acc[...] = jnp.zeros_like(acc)
         for s in range(sectors):
             sums = sums + arrived[s, CAP * share :].astype(F32)
             for c in range(CAP):
-                slot = ids[s, c]
+                slot = ids[s * CAP + c]
                 acc[slot] = acc[slot] + arrived[s, c * share : (c + 1) * share].astype(F32)
         sums = jnp.sum(sums, axis=1, keepdims=True)
         total_of = [sums[j : j + 1] for j in range(k)]
@@ -240,9 +272,9 @@
             keep(5 + j, project[j])
             keep(8 + 4 * (k - 1) + j, scale * (project[j] - crossed[j]))
         keep(8 + 4 * (k - 1) + k - 1, length * scale * scale)
-        first_row = meta[ROW_POS, 0] * share
+        first_row = meta.place() * share
         for b in range(slots):
-            value = jnp.where(mask_of(meta, b, slots, (share, size), first_row), acc[b], 0.0)
+            value = jnp.where(mask_of(meta, b, (share, size), first_row), acc[b], 0.0)
             direction = vector[b]
             for j in range(k - 1):
                 value = value - project[j] * images[j][b]
@@ -253,21 +285,22 @@
             basis[b] = direction
             message[b] = value.astype(BF)
 
+    rows = (slots, share, size)
+    shapes = [out(rows, F32), out(rows, F32), out(rows, BF), out((24, size), F32)]
+    specs = [VMEM] * 4
+    scratch = [pltpu.VMEM((slots + 1, share, size), F32)]
+    if k == 1:
+        shapes.append(out((sectors * CAP,), jnp.int32))
+        specs.append(SMEM)
+        scratch.append(pltpu.VMEM((sectors, size), jnp.int32))
+        scratch.append(pltpu.SMEM((sectors, size), jnp.int32))
     return call(
         body,
         "image",
-        [SMEM] + [VMEM] * (3 + 2 * (k - 1)),
-        (
-            out((slots, share, size), F32),
-            out((slots, share, size), F32),
-            out((slots, share, size), BF),
-            out((24, size), F32),
-        ),
-        [
-            pltpu.VMEM((slots + 1, share, size), F32),
-            pltpu.VMEM((sectors, size), jnp.int32),
-            pltpu.SMEM((sectors, size), jnp.int32),
-        ],
+        [SMEM] + [VMEM] * (3 + 2 * (k - 1)) + ([SMEM] if k > 1 else []),
+        tuple(shapes),
+        scratch,
+        out_specs=tuple(specs),
     )
 
 
@@ -279,12 +312,13 @@
     return call(body, "gather", [VMEM] * chips, out((chips, slots, share, size), BF))
 
 
-def weigh_kernel(k, slots, size, share, sectors, chips):
+def weigh_kernel(k, edges, slots, size, share, sectors, chips):
     def body(meta, mine, other, vector, state, *refs):
+        meta = Meta(meta, edges, slots)
         bases = refs[: k - 1]
         image, basis, message = refs[k - 1 :]
-        x = meta[ROW_POS, 1]
-        c = meta[ROW_POS, 2]
+        x = meta.place() // 2
+        c = lax.rem(meta.place(), 2)
         for j in range(chips):
             origin = 2 * lax.rem(x + chips - j, chips)
             near = pl.multiple_of((origin + c) * share, share)
@@ -317,8 +351,9 @@
     )
 
 
-def correct_kernel(k, slots, size, share, sectors, last):
+def correct_kernel(k, edges, slots, size, share, sectors, last):
     def body(meta, thetas, whole_image, whole_basis, shift, image, basis, state, *refs):
+        meta = Meta(meta, edges, slots)
         bases = refs[: k - 1]
         if last:
             corrected, sums, new_state = refs[k - 1 :]
@@ -327,7 +362,7 @@
         theta = jnp.sum(thetas[...].reshape(sectors, size), axis=0, keepdims=True)
         new_state[...] = state[...]
         new_state[k - 1 : k] = theta
-        first_row = pl.multiple_of(meta[ROW_POS, 0] * share, share)
+        first_row = pl.multiple_of(meta.place() * share, share)
 
         def residual(mask, value, direction, moved):
             bottom = jnp.maximum(jnp.abs(moved - theta), 1.0)
@@ -336,7 +371,7 @@
         def step(b, carry):
             direction = whole_basis[b]
             value = residual(
-                mask_of(meta, b, slots, (size, size), 0),
+                mask_of(meta, b, (size, size), 0),
                 whole_image[b].astype(F32),
                 direction,
                 shift[b],
@@ -345,7 +380,7 @@
                 whole[b] = value
                 xin[b] = value.astype(BF)
             corrected[b] = residual(
-                mask_of(meta, b, slots, (share, size), first_row),
+                mask_of(meta, b, (share, size), first_row),
                 image[b],
                 basis[b],
                 shift[b, pl.ds(first_row, share)],
@@ -439,16 +474,16 @@
     chips = terms // 2
     place = lax.axis_index("mpo")
     core_swap = [(i, i ^ 1) for i in range(terms)]
-    entry = jnp.arange(edges, dtype=jnp.int32)
-    meta = jnp.stack(
+    meta = jnp.concatenate(
         [
             edge_input,
             edge_left,
             edge_right,
             edge_owner[:, 0],
             edge_slot,
-            jnp.concatenate([block_rows, block_cols]),
-            jnp.where(entry == 0, place, jnp.where(entry == 1, place // 2, place % 2)),
+            block_rows,
+            block_cols,
+            place[None].astype(jnp.int32),
         ]
     )
 
@@ -462,10 +497,10 @@
     def far(values):
         return pltpu.with_memory_space_constraint(values, pltpu.HBM)
 
-    vector, xin, mine, sums, state, right_near, left_near = start_kernel(slots, size, share, group)(
+    vector, xin, mine, sums, state, right_near, left_near = start_kernel(edges, slots, size, share, group)(
         meta, far(guess), far(right_env), far(left_env)
     )
-    bases, images, whole_bases = [], [], []
+    bases, images, whole_bases, ids = [], [], [], []
     for k in range(1, APPLIES + 1):
         own, send, right_near, left_near = couple_kernel(edges, slots, size, share, group, chips)(
             meta, xin, right_near, left_near
@@ -473,21 +508,25 @@
         received = lax.ppermute(send, "mpo", core_swap)
         parts = pair_kernel(edges, size, share, chips)(own, received)
         shifted = [parts[0]] + [chip_shift(parts[j], j) for j in range(1, chips)]
-        message = pack_kernel(edges, size, share, sectors)(meta, sums, *shifted)
+        message = pack_kernel(edges, slots, size, share, sectors, k == 1)(meta, sums, *shifted)
         arrived = over_sector(message)
-        image, basis, outgoing, state = image_kernel(k, slots, size, share, sectors)(
-            meta, arrived, mine, state, *bases, *images
+        result = image_kernel(k, edges, slots, size, share, sectors)(
+            meta, arrived, mine, state, *bases, *images, *ids
         )
-        rows = [outgoing, chip_shift(outgoing, 1), None, chip_shift(outgoing, chips - 1)]
-        rows[2] = chip_shift(rows[1], 1)
+        image, basis, outgoing, state = result[:4]
+        if k == 1:
+            ids = result[4:]
+        rows = [outgoing] + [chip_shift(outgoing, j) for j in range(1, chips)]
         near_rows = gather_kernel(slots, size, share, chips)(*rows)
         far_rows = lax.ppermute(near_rows, "mpo", core_swap)
-        whole_image, whole_basis, parts = weigh_kernel(k, slots, size, share, sectors, chips)(
+        whole_image, whole_basis, parts = weigh_kernel(
+            k, edges, slots, size, share, sectors, chips
+        )(
             meta, near_rows, far_rows, vector, state, *whole_bases
         )
         thetas = over_sector(parts)
         last = k == APPLIES
-        result = correct_kernel(k, slots, size, share, sectors, last)(
+        result = correct_kernel(k, edges, slots, size, share, sectors, last)(
             meta, thetas, whole_image, whole_basis, diag_shift, image, basis, state, *whole_bases
         )
         if last:

time: 233 us -> 220 us (0.944); the launches traced: 230 us -> 219 us
  Pallas kernels: 43.5 us -> 35.8 us
  starting transfers between devices: 33.1 us -> 30.1 us
    pallas_call x3, Pallas kernels: 22.3 us -> 16.7 us  [per_device(): couple_kernel(edges, slots, size, share, group, chips)]
    ppermute x18, starting transfers between devices: 32.5 us -> 29.3 us  [chip_shift(): return lax.ppermute(values, 'mpo', pairs)]
  transfers between devices with their start and end apart: 24 -> 24, of which waited for: 19 -> 24; matrix products, arithmetic and copies ran while one was open for 0% -> 0% of each run, Pallas kernels for 0% -> 0%
where the time goes in v3:
time: 220 us; the launch traced here: 219 us
  blocking collectives  113 us (51%)
  waiting for transfers between devices  39 us (18%)
  Pallas kernels  35.8 us (16%)
  starting transfers between devices  30.1 us (14%)
    all_to_all x7, blocking collectives, over_sector(): return lax.all_to_all(values, 'sector', 0, 0, tiled=True)  113 us
    ppermute x18, starting transfers between devices, chip_shift(): return lax.ppermute(values, 'mpo', pairs)  29.3 us
    ppermute x18, waiting for transfers between devices, chip_shift(): return lax.ppermute(values, 'mpo', pairs)  28.7 us
    pallas_call x3, Pallas kernels, per_device(): couple_kernel(edges, slots, size, share, group, chips)  16.7 us
    ppermute x3, waiting for transfers between devices, per_device(): received = lax.ppermute(send, 'mpo', core_swap)  5.69 us
    ppermute x3, waiting for transfers between devices, per_device(): far_rows = lax.ppermute(near_rows, 'mpo', core_swap)  4.57 us
  transfers between devices with their start and end apart: 24, of which 24 were waited for; matrix products, arithmetic and copies ran while one was open for 0% of the time, Pallas kernels for 0%

profile of v3, /device:TPU:4, one launch (start us, length us, event | category | flops | bytes accessed | tf_op | source)
XLA Modules:
  0.0 219.4 jit_solution(12184996937119697735)
XLA Ops:
  1.5 4.4 %start.1 = (f32[16,128,128]{2,1,0:T(8,128)S(1)}, bf16[16,128,128]{2,1,0:T(8,128)(2,1)S(1)}, f32[16,16,128]{2,1,0:T(8,128)S(1)}, f32[8,128]{1,0:T(8,128)S(1)}, f3...) custom-call(s32[193]{0:T(256)S(1)} %concatenate.3.meta, ...), custom_call_target="tpu_custom_call" | custom-call | tf_op jit(solution)/shard_map/start/pallas_call | solution.py:500
  5.8 5.6 %couple.3 = (bf16[4,32,16,128]{3,2,1,0:T(8,128)(2,1)S(1)}, bf16[4,32,16,128]{3,2,1,0:T(8,128)(2,1)S(1)}, bf16[8,16,128,128]{3,2,1,0:T(8,128)(2,1)S(1)}, bf16[8,16,128,128]{3,2,1,0:T(8,128)(2,1)S(1)}) custom-call(s32[193]{0:T(256)S(1)} %concatenate.3.meta, ...), custom_call_target="tpu_custom_call", output_to_operand_aliasing={{2}: (2, {}), {3}: (3, {})} | custom-call | tf_op jit(solution)/shard_map/couple/pallas_call | solution.py:505
  11.5 1.9 collective-permute-done.received
  15.9 2.5 %collective-permute-start.3 = (bf16[32,16,128]{2,1,0:T(8,128)(2,1)S(1)}, bf16[32,16,128]{2,1,0:T(8,128)(2,1)S(1)}, u32[]{:S(2)}, u32[]{:S(2)}) collective-permute-start(bf16[32,16,128]{2,1,0:T(8,128)(2,1)S(1)} %get-tuple-element.76), channel_id=1, source_target_pairs={{0,6},{1,7},{2,0},{3,1},{4,2},{5,3},{6,4},{7,5},{8,14},{9,15},{10,... | collective-permute-start | bytes 393224 | tf_op jit(solution)/shard_map/ppermute | solution.py:495
  19.3 3.2 %collective-permute-done.2.third = bf16[32,16,128]{2,1,0:T(8,128)(2,1)S(1)} collective-permute-done((bf16[32,16,128]{2,1,0:T(8,128)(2,1)S(1)}, bf16[32,16,128]{2,1,0:T(8,128)(2,1)S(1)}, u32[]{:S(2)}, u32[]{:S(2)}) %collective-permute-start.2) | collective-permute-done | bytes 131104 | tf_op jit(solution)/shard_map/ppermute | solution.py:495
  24.6 24.7 %all_to_all.35.arrived = bf16[32,40,128]{2,1,0:T(8,128)(2,1)S(1)} all-to-all(bf16[32,40,128]{2,1,0:T(8,128)(2,1)S(1)} %pack.3), channel_id=1, replica_groups=mesh['sector'=32,'mpo'=8] {'sector'}, dimensions={0} | all-to-all | bytes 655360 | tf_op jit(solution)/shard_map/all_to_all | solution.py:491
  49.3 2.2 %image.3 = (f32[16,16,128]{2,1,0:T(8,128)S(1)}, f32[16,16,128]{2,1,0:T(8,128)S(1)}, bf16[16,16,128]{2,1,0:T(8,128)(2,1)S(1)}, f32[24,128]{1,0:T(8,128)S(1)}, s32[64]{0:T(128)S(1)}) custom-call(s32[193]{0:T(256)S(1)} %concatenate.3.meta, bf16[32,40,128]{2,1,0:T(8,128)(2,1)S(1)} %all_to_all.35.arrived, f32[16,16,128]{2,1,0:T(8,128)S(1)} %get-tuple-element.77.vector, ...), custom_call_target="tpu_custom_call" | custom-call | tf_op jit(solution)/shard_map/image/pallas_call | solution.py:513
  52.4 2.5 %collective-permute-start.5 = (bf16[16,16,128]{2,1,0:T(8,128)(2,1)S(1)}, bf16[16,16,128]{2,1,0:T(8,128)(2,1)S(1)}, u32[]{:S(2)}, u32[]{:S(2)}) collective-permute-start(bf16[16,16,128]{2,1,0:T(8,128)(2,1)S(1)} %get-tuple-element.79.refs_0_), channel_id=1, source_target_pairs={{0,4},{1,5},{2,6},{3,7},{4,0},{5,1},{6,2},{7,3},{8,12},{9,13},{10,... | collective-permute-start | bytes 196616 | tf_op jit(solution)/shard_map/ppermute | solution.py:495
  55.9 2.3 %collective-permute-done.5.refs_2_ = bf16[16,16,128]{2,1,0:T(8,128)(2,1)S(1)} collective-permute-done((bf16[16,16,128]{2,1,0:T(8,128)(2,1)S(1)}, bf16[16,16,128]{2,1,0:T(8,128)(2,1)S(1)}, u32[]{:S(2)}, u32[]{:S(2)}) %collective-permute-start.5) | collective-permute-done | bytes 65568 | tf_op jit(solution)/shard_map/ppermute | solution.py:495
  61.7 13.8 %all_to_all.36.thetas = f32[32,1,128]{2,1,0:T(1,128)S(1)} all-to-all(f32[32,1,128]{2,1,0:T(1,128)S(1)} %get-tuple-element.82), channel_id=1, replica_groups=mesh['sector'=32,'mpo'=8] {'sector'}, dimensions={0} | all-to-all | bytes 32768 | tf_op jit(solution)/shard_map/all_to_all | solution.py:491
  76.9 5.6 %couple.4 = (bf16[4,32,16,128]{3,2,1,0:T(8,128)(2,1)S(1)}, bf16[4,32,16,128]{3,2,1,0:T(8,128)(2,1)S(1)}, bf16[8,16,128,128]{3,2,1,0:T(8,128)(2,1)S(1)}, bf16[8,16,128,128]{3,2,1,0:T(8,128)(2,1)S(1)}) custom-call(s32[193]{0:T(256)S(1)} %concatenate.3.meta, ...), custom_call_target="tpu_custom_call", output_to_operand_aliasing={{2}: (2, {}), {3}: (3, {})} | custom-call | tf_op jit(solution)/shard_map/couple/pallas_call | solution.py:505
  82.6 1.9 collective-permute-done.8.received
  87.0 2.5 %collective-permute-start.11 = (bf16[32,16,128]{2,1,0:T(8,128)(2,1)S(1)}, bf16[32,16,128]{2,1,0:T(8,128)(2,1)S(1)}, u32[]{:S(2)}, u32[]{:S(2)}) collective-permute-start(bf16[32,16,128]{2,1,0:T(8,128)(2,1)S(1)} %get-tuple-element.96), channel_id=1, source_target_pairs={{0,6},{1,7},{2,0},{3,1},{4,2},{5,3},{6,4},{7,5},{8,14},{9,15},{10,... | collective-permute-start | bytes 393224 | tf_op jit(solution)/shard_map/ppermute | solution.py:495
  90.3 3.2 %collective-permute-done.10.third = bf16[32,16,128]{2,1,0:T(8,128)(2,1)S(1)} collective-permute-done((bf16[32,16,128]{2,1,0:T(8,128)(2,1)S(1)}, bf16[32,16,128]{2,1,0:T(8,128)(2,1)S(1)}, u32[]{:S(2)}, u32[]{:S(2)}) %collective-permute-start.10) | collective-permute-done | bytes 131104 | tf_op jit(solution)/shard_map/ppermute | solution.py:495
  95.5 16.8 %all_to_all.37.arrived = bf16[32,40,128]{2,1,0:T(8,128)(2,1)S(1)} all-to-all(bf16[32,40,128]{2,1,0:T(8,128)(2,1)S(1)} %pack.4), channel_id=1, replica_groups=mesh['sector'=32,'mpo'=8] {'sector'}, dimensions={0} | all-to-all | bytes 655360 | tf_op jit(solution)/shard_map/all_to_all | solution.py:491
  113.3 2.1 collective-permute-start.14
  115.4 3.6 %collective-permute-start.13 = (bf16[16,16,128]{2,1,0:T(8,128)(2,1)S(1)}, bf16[16,16,128]{2,1,0:T(8,128)(2,1)S(1)}, u32[]{:S(2)}, u32[]{:S(2)}) collective-permute-start(bf16[16,16,128]{2,1,0:T(8,128)(2,1)S(1)} %get-tuple-element.100.refs_0_), channel_id=1, source_target_pairs={{0,4},{1,5},{2,6},{3,7},{4,0},{5,1},{6,2},{7,3},{8,12},{9,13},{10,... | collective-permute-start | bytes 196616 | tf_op jit(solution)/shard_map/ppermute | solution.py:495
  119.2 2.1 collective-permute-done.13.refs_2_
  121.3 2.0 collective-permute-done.12.refs_1_
  125.9 13.5 %all_to_all.38.thetas = f32[32,1,128]{2,1,0:T(1,128)S(1)} all-to-all(f32[32,1,128]{2,1,0:T(1,128)S(1)} %get-tuple-element.103), channel_id=1, replica_groups=mesh['sector'=32,'mpo'=8] {'sector'}, dimensions={0} | all-to-all | bytes 32768 | tf_op jit(solution)/shard_map/all_to_all | solution.py:491
  140.8 5.6 %couple.5 = (bf16[4,32,16,128]{3,2,1,0:T(8,128)(2,1)S(1)}, bf16[4,32,16,128]{3,2,1,0:T(8,128)(2,1)S(1)}, bf16[8,16,128,128]{3,2,1,0:T(8,128)(2,1)S(1)}, bf16[8,16,128,128]{3,2,1,0:T(8,128)(2,1)S(1)}) custom-call(s32[193]{0:T(256)S(1)} %concatenate.3.meta, ...), custom_call_target="tpu_custom_call", output_to_operand_aliasing={{2}: (2, {}), {3}: (3, {})} | custom-call | tf_op jit(solution)/shard_map/couple/pallas_call | solution.py:505
  146.7 1.9 collective-permute-done.16.received
  150.8 2.5 %collective-permute-start.19 = (bf16[32,16,128]{2,1,0:T(8,128)(2,1)S(1)}, bf16[32,16,128]{2,1,0:T(8,128)(2,1)S(1)}, u32[]{:S(2)}, u32[]{:S(2)}) collective-permute-start(bf16[32,16,128]{2,1,0:T(8,128)(2,1)S(1)} %get-tuple-element.117), channel_id=1, source_target_pairs={{0,6},{1,7},{2,0},{3,1},{4,2},{5,3},{6,4},{7,5},{8,14},{9,15},{10,... | collective-permute-start | bytes 393224 | tf_op jit(solution)/shard_map/ppermute | solution.py:495
  154.7 2.6 %collective-permute-done.18.third = bf16[32,16,128]{2,1,0:T(8,128)(2,1)S(1)} collective-permute-done((bf16[32,16,128]{2,1,0:T(8,128)(2,1)S(1)}, bf16[32,16,128]{2,1,0:T(8,128)(2,1)S(1)}, u32[]{:S(2)}, u32[]{:S(2)}) %collective-permute-start.18) | collective-permute-done | bytes 131104 | tf_op jit(solution)/shard_map/ppermute | solution.py:495
  157.3 1.6 collective-permute-done.19.fourth
  159.7 16.8 %all_to_all.39.arrived = bf16[32,40,128]{2,1,0:T(8,128)(2,1)S(1)} all-to-all(bf16[32,40,128]{2,1,0:T(8,128)(2,1)S(1)} %pack.5), channel_id=1, replica_groups=mesh['sector'=32,'mpo'=8] {'sector'}, dimensions={0} | all-to-all | bytes 655360 | tf_op jit(solution)/shard_map/all_to_all | solution.py:491
  177.4 2.2 %collective-permute-start.22 = (bf16[16,16,128]{2,1,0:T(8,128)(2,1)S(1)}, bf16[16,16,128]{2,1,0:T(8,128)(2,1)S(1)}, u32[]{:S(2)}, u32[]{:S(2)}) collective-permute-start(bf16[16,16,128]{2,1,0:T(8,128)(2,1)S(1)} %get-tuple-element.120.refs_0_), channel_id=1, source_target_pairs={{0,6},{1,7},{2,0},{3,1},{4,2},{5,3},{6,4},{7,5},{8,14},{9,15},{10,... | collective-permute-start | bytes 196616 | tf_op jit(solution)/shard_map/ppermute | solution.py:495
  179.6 3.2 %collective-permute-start.21 = (bf16[16,16,128]{2,1,0:T(8,128)(2,1)S(1)}, bf16[16,16,128]{2,1,0:T(8,128)(2,1)S(1)}, u32[]{:S(2)}, u32[]{:S(2)}) collective-permute-start(bf16[16,16,128]{2,1,0:T(8,128)(2,1)S(1)} %get-tuple-element.120.refs_0_), channel_id=1, source_target_pairs={{0,4},{1,5},{2,6},{3,7},{4,0},{5,1},{6,2},{7,3},{8,12},{9,13},{10,... | collective-permute-start | bytes 196616 | tf_op jit(solution)/shard_map/ppermute | solution.py:495
  183.0 2.4 %collective-permute-done.21.refs_2_ = bf16[16,16,128]{2,1,0:T(8,128)(2,1)S(1)} collective-permute-done((bf16[16,16,128]{2,1,0:T(8,128)(2,1)S(1)}, bf16[16,16,128]{2,1,0:T(8,128)(2,1)S(1)}, u32[]{:S(2)}, u32[]{:S(2)}) %collective-permute-start.21) | collective-permute-done | bytes 65568 | tf_op jit(solution)/shard_map/ppermute | solution.py:495
  185.4 1.7 collective-permute-done.20.refs_1_
  189.8 13.5 %all_to_all.40.thetas = f32[32,1,128]{2,1,0:T(1,128)S(1)} all-to-all(f32[32,1,128]{2,1,0:T(1,128)S(1)} %get-tuple-element.123), channel_id=1, replica_groups=mesh['sector'=32,'mpo'=8] {'sector'}, dimensions={0} | all-to-all | bytes 32768 | tf_op jit(solution)/shard_map/all_to_all | solution.py:491
  204.9 13.5 %all_to_all.41.sums = f32[32,8,128]{2,1,0:T(8,128)S(1)} all-to-all(f32[32,8,128]{2,1,0:T(8,128)S(1)} %get-tuple-element.128), channel_id=1, replica_groups=mesh['sector'=32,'mpo'=8] {'sector'}, dimensions={0} | all-to-all | bytes 262144 | tf_op jit(solution)/shard_map/all_to_all | solution.py:491
  (49 shorter events, 34.3 us)
Async XLA Ops:
  11.4 64.2 %copy-start = (f32[16,128,128]{2,1,0:T(8,128)S(1)}, f32[16,128,128]{2,1,0:T(8,128)}, u32[]{:S(2)}) copy-start(f32[16,128,128]{2,1,0:T(8,128)} %shift.5) | copy-start | bytes 3145732
  11.4 2.0 collective-permute-start
  13.5 5.7 %collective-permute-start.1 = (bf16[32,16,128]{2,1,0:T(8,128)(2,1)S(1)}, bf16[32,16,128]{2,1,0:T(8,128)(2,1)S(1)}, u32[]{:S(2)}, u32[]{:S(2)}) collective-permute-start(bf16[32,16,128]{2,1,0:T(8,128)(2,1)S(1)} %get-tuple-element.74), channel_id=1, source_target_pairs={{0,2},{1,3},{2,4},{3,5},{4,6},{5,7},{6,0},{7,1},{8,10},{9,11},{10,... | collective-permute-start | bytes 393224 | tf_op jit(solution)/shard_map/ppermute | solution.py:495
  14.8 7.6 %collective-permute-start.2 = (bf16[32,16,128]{2,1,0:T(8,128)(2,1)S(1)}, bf16[32,16,128]{2,1,0:T(8,128)(2,1)S(1)}, u32[]{:S(2)}, u32[]{:S(2)}) collective-permute-start(bf16[32,16,128]{2,1,0:T(8,128)(2,1)S(1)} %get-tuple-element.75), channel_id=1, source_target_pairs={{0,4},{1,5},{2,6},{3,7},{4,0},{5,1},{6,2},{7,3},{8,12},{9,13},{10,... | collective-permute-start | bytes 393224 | tf_op jit(solution)/shard_map/ppermute | solution.py:495
  15.9 7.8 %collective-permute-start.3 = (bf16[32,16,128]{2,1,0:T(8,128)(2,1)S(1)}, bf16[32,16,128]{2,1,0:T(8,128)(2,1)S(1)}, u32[]{:S(2)}, u32[]{:S(2)}) collective-permute-start(bf16[32,16,128]{2,1,0:T(8,128)(2,1)S(1)} %get-tuple-element.76), channel_id=1, source_target_pairs={{0,6},{1,7},{2,0},{3,1},{4,2},{5,3},{6,4},{7,5},{8,14},{9,15},{10,... | collective-permute-start | bytes 393224 | tf_op jit(solution)/shard_map/ppermute | solution.py:495
  51.5 4.3 %collective-permute-start.6 = (bf16[16,16,128]{2,1,0:T(8,128)(2,1)S(1)}, bf16[16,16,128]{2,1,0:T(8,128)(2,1)S(1)}, u32[]{:S(2)}, u32[]{:S(2)}) collective-permute-start(bf16[16,16,128]{2,1,0:T(8,128)(2,1)S(1)} %get-tuple-element.79.refs_0_), channel_id=1, source_target_pairs={{0,6},{1,7},{2,0},{3,1},{4,2},{5,3},{6,4},{7,5},{8,14},{9,15},{10,... | collective-permute-start | bytes 196616 | tf_op jit(solution)/shard_map/ppermute | solution.py:495
  52.4 5.8 %collective-permute-start.5 = (bf16[16,16,128]{2,1,0:T(8,128)(2,1)S(1)}, bf16[16,16,128]{2,1,0:T(8,128)(2,1)S(1)}, u32[]{:S(2)}, u32[]{:S(2)}) collective-permute-start(bf16[16,16,128]{2,1,0:T(8,128)(2,1)S(1)} %get-tuple-element.79.refs_0_), channel_id=1, source_target_pairs={{0,4},{1,5},{2,6},{3,7},{4,0},{5,1},{6,2},{7,3},{8,12},{9,13},{10,... | collective-permute-start | bytes 196616 | tf_op jit(solution)/shard_map/ppermute | solution.py:495
  54.9 4.3 %collective-permute-start.4 = (bf16[16,16,128]{2,1,0:T(8,128)(2,1)S(1)}, bf16[16,16,128]{2,1,0:T(8,128)(2,1)S(1)}, u32[]{:S(2)}, u32[]{:S(2)}) collective-permute-start(bf16[16,16,128]{2,1,0:T(8,128)(2,1)S(1)} %get-tuple-element.79.refs_0_), channel_id=1, source_target_pairs={{0,2},{1,3},{2,4},{3,5},{4,6},{5,7},{6,0},{7,1},{8,10},{9,11},{10,... | collective-permute-start | bytes 196616 | tf_op jit(solution)/shard_map/ppermute | solution.py:495
  59.2 1.6 collective-permute-start.7
  82.5 2.0 collective-permute-start.8
  84.6 5.7 %collective-permute-start.9 = (bf16[32,16,128]{2,1,0:T(8,128)(2,1)S(1)}, bf16[32,16,128]{2,1,0:T(8,128)(2,1)S(1)}, u32[]{:S(2)}, u32[]{:S(2)}) collective-permute-start(bf16[32,16,128]{2,1,0:T(8,128)(2,1)S(1)} %get-tuple-element.94), channel_id=1, source_target_pairs={{0,2},{1,3},{2,4},{3,5},{4,6},{5,7},{6,0},{7,1},{8,10},{9,11},{10,... | collective-permute-start | bytes 393224 | tf_op jit(solution)/shard_map/ppermute | solution.py:495
  85.4 8.1 %collective-permute-start.10 = (bf16[32,16,128]{2,1,0:T(8,128)(2,1)S(1)}, bf16[32,16,128]{2,1,0:T(8,128)(2,1)S(1)}, u32[]{:S(2)}, u32[]{:S(2)}) collective-permute-start(bf16[32,16,128]{2,1,0:T(8,128)(2,1)S(1)} %get-tuple-element.95), channel_id=1, source_target_pairs={{0,4},{1,5},{2,6},{3,7},{4,0},{5,1},{6,2},{7,3},{8,12},{9,13},{10,... | collective-permute-start | bytes 393224 | tf_op jit(solution)/shard_map/ppermute | solution.py:495
  87.0 7.8 %collective-permute-start.11 = (bf16[32,16,128]{2,1,0:T(8,128)(2,1)S(1)}, bf16[32,16,128]{2,1,0:T(8,128)(2,1)S(1)}, u32[]{:S(2)}, u32[]{:S(2)}) collective-permute-start(bf16[32,16,128]{2,1,0:T(8,128)(2,1)S(1)} %get-tuple-element.96), channel_id=1, source_target_pairs={{0,6},{1,7},{2,0},{3,1},{4,2},{5,3},{6,4},{7,5},{8,14},{9,15},{10,... | collective-permute-start | bytes 393224 | tf_op jit(solution)/shard_map/ppermute | solution.py:495
  113.3 5.9 %collective-permute-start.14 = (bf16[16,16,128]{2,1,0:T(8,128)(2,1)S(1)}, bf16[16,16,128]{2,1,0:T(8,128)(2,1)S(1)}, u32[]{:S(2)}, u32[]{:S(2)}) collective-permute-start(bf16[16,16,128]{2,1,0:T(8,128)(2,1)S(1)} %get-tuple-element.100.refs_0_), channel_id=1, source_target_pairs={{0,6},{1,7},{2,0},{3,1},{4,2},{5,3},{6,4},{7,5},{8,14},{9,15},{10,... | collective-permute-start | bytes 196616 | tf_op jit(solution)/shard_map/ppermute | solution.py:495
  115.4 5.9 %collective-permute-start.13 = (bf16[16,16,128]{2,1,0:T(8,128)(2,1)S(1)}, bf16[16,16,128]{2,1,0:T(8,128)(2,1)S(1)}, u32[]{:S(2)}, u32[]{:S(2)}) collective-permute-start(bf16[16,16,128]{2,1,0:T(8,128)(2,1)S(1)} %get-tuple-element.100.refs_0_), channel_id=1, source_target_pairs={{0,4},{1,5},{2,6},{3,7},{4,0},{5,1},{6,2},{7,3},{8,12},{9,13},{10,... | collective-permute-start | bytes 196616 | tf_op jit(solution)/shard_map/ppermute | solution.py:495
  119.0 4.3 %collective-permute-start.12 = (bf16[16,16,128]{2,1,0:T(8,128)(2,1)S(1)}, bf16[16,16,128]{2,1,0:T(8,128)(2,1)S(1)}, u32[]{:S(2)}, u32[]{:S(2)}) collective-permute-start(bf16[16,16,128]{2,1,0:T(8,128)(2,1)S(1)} %get-tuple-element.100.refs_0_), channel_id=1, source_target_pairs={{0,2},{1,3},{2,4},{3,5},{4,6},{5,7},{6,0},{7,1},{8,10},{9,11},{10,... | collective-permute-start | bytes 196616 | tf_op jit(solution)/shard_map/ppermute | solution.py:495
  123.3 1.6 collective-permute-start.15
  146.4 2.2 %collective-permute-start.16 = (bf16[4,32,16,128]{3,2,1,0:T(8,128)(2,1)S(1)}, bf16[4,32,16,128]{3,2,1,0:T(8,128)(2,1)S(1)}, u32[]{:S(2)}, u32[]{:S(2)}) collective-permute-start(bf16[4,32,16,128]{3,2,1,0:T(8,128)(2,1)S(1)} %get-tuple-element.113), channel_id=1, source_target_pairs={{0,1},{1,0},{2,3},{3,2},{4,5},{5,4},{6,7},{7,6},{8,9},{9,8},{10,11... | collective-permute-start | bytes 1572872 | tf_op jit(solution)/shard_map/ppermute | solution.py:508
  148.7 6.0 %collective-permute-start.17 = (bf16[32,16,128]{2,1,0:T(8,128)(2,1)S(1)}, bf16[32,16,128]{2,1,0:T(8,128)(2,1)S(1)}, u32[]{:S(2)}, u32[]{:S(2)}) collective-permute-start(bf16[32,16,128]{2,1,0:T(8,128)(2,1)S(1)} %get-tuple-element.115), channel_id=1, source_target_pairs={{0,2},{1,3},{2,4},{3,5},{4,6},{5,7},{6,0},{7,1},{8,10},{9,11},{10,... | collective-permute-start | bytes 393224 | tf_op jit(solution)/shard_map/ppermute | solution.py:495
  149.5 7.8 %collective-permute-start.18 = (bf16[32,16,128]{2,1,0:T(8,128)(2,1)S(1)}, bf16[32,16,128]{2,1,0:T(8,128)(2,1)S(1)}, u32[]{:S(2)}, u32[]{:S(2)}) collective-permute-start(bf16[32,16,128]{2,1,0:T(8,128)(2,1)S(1)} %get-tuple-element.116), channel_id=1, source_target_pairs={{0,4},{1,5},{2,6},{3,7},{4,0},{5,1},{6,2},{7,3},{8,12},{9,13},{10,... | collective-permute-start | bytes 393224 | tf_op jit(solution)/shard_map/ppermute | solution.py:495
  150.8 8.1 %collective-permute-start.19 = (bf16[32,16,128]{2,1,0:T(8,128)(2,1)S(1)}, bf16[32,16,128]{2,1,0:T(8,128)(2,1)S(1)}, u32[]{:S(2)}, u32[]{:S(2)}) collective-permute-start(bf16[32,16,128]{2,1,0:T(8,128)(2,1)S(1)} %get-tuple-element.117), channel_id=1, source_target_pairs={{0,6},{1,7},{2,0},{3,1},{4,2},{5,3},{6,4},{7,5},{8,14},{9,15},{10,... | collective-permute-start | bytes 393224 | tf_op jit(solution)/shard_map/ppermute | solution.py:495
  177.4 5.6 %collective-permute-start.22 = (bf16[16,16,128]{2,1,0:T(8,128)(2,1)S(1)}, bf16[16,16,128]{2,1,0:T(8,128)(2,1)S(1)}, u32[]{:S(2)}, u32[]{:S(2)}) collective-permute-start(bf16[16,16,128]{2,1,0:T(8,128)(2,1)S(1)} %get-tuple-element.120.refs_0_), channel_id=1, source_target_pairs={{0,6},{1,7},{2,0},{3,1},{4,2},{5,3},{6,4},{7,5},{8,14},{9,15},{10,... | collective-permute-start | bytes 196616 | tf_op jit(solution)/shard_map/ppermute | solution.py:495
  179.6 5.8 %collective-permute-start.21 = (bf16[16,16,128]{2,1,0:T(8,128)(2,1)S(1)}, bf16[16,16,128]{2,1,0:T(8,128)(2,1)S(1)}, u32[]{:S(2)}, u32[]{:S(2)}) collective-permute-start(bf16[16,16,128]{2,1,0:T(8,128)(2,1)S(1)} %get-tuple-element.120.refs_0_), channel_id=1, source_target_pairs={{0,4},{1,5},{2,6},{3,7},{4,0},{5,1},{6,2},{7,3},{8,12},{9,13},{10,... | collective-permute-start | bytes 196616 | tf_op jit(solution)/shard_map/ppermute | solution.py:495
  182.8 4.3 %collective-permute-start.20 = (bf16[16,16,128]{2,1,0:T(8,128)(2,1)S(1)}, bf16[16,16,128]{2,1,0:T(8,128)(2,1)S(1)}, u32[]{:S(2)}, u32[]{:S(2)}) collective-permute-start(bf16[16,16,128]{2,1,0:T(8,128)(2,1)S(1)} %get-tuple-element.120.refs_0_), channel_id=1, source_target_pairs={{0,2},{1,3},{2,4},{3,5},{4,6},{5,7},{6,0},{7,1},{8,10},{9,11},{10,... | collective-permute-start | bytes 196616 | tf_op jit(solution)/shard_map/ppermute | solution.py:495
  187.1 1.6 collective-permute-start.23

commit v4 on v3

--- a/solution.py
+++ b/solution.py
@@ -219,7 +219,9 @@
     )
 
 
-def image_kernel(k, edges, slots, size, share, sectors):
+def image_kernel(k, edges, slots, size, share, sectors, devices):
+    last = k == APPLIES
+
     def body(meta, arrived, vector, state, *refs):
         meta = Meta(meta, edges, slots)
         bases = refs[: k - 1]
@@ -273,6 +275,7 @@
             keep(8 + 4 * (k - 1) + j, scale * (project[j] - crossed[j]))
         keep(8 + 4 * (k - 1) + k - 1, length * scale * scale)
         first_row = meta.place() * share
+        theta = jnp.zeros((8, size), F32)
         for b in range(slots):
             value = jnp.where(mask_of(meta, b, (share, size), first_row), acc[b], 0.0)
             direction = vector[b]
@@ -283,10 +286,16 @@
             direction = direction * scale
             image[b] = value
             basis[b] = direction
-            message[b] = value.astype(BF)
+            if last:
+                theta = theta + fold(value * direction)
+            else:
+                message[b] = value.astype(BF)
+        if last:
+            message[...] = jnp.broadcast_to(total(theta)[None], (devices, 1, size))
 
     rows = (slots, share, size)
-    shapes = [out(rows, F32), out(rows, F32), out(rows, BF), out((24, size), F32)]
+    sent = out((devices, 1, size), F32) if last else out(rows, BF)
+    shapes = [out(rows, F32), out(rows, F32), sent, out((24, size), F32)]
     specs = [VMEM] * 4
     scratch = [pltpu.VMEM((slots + 1, share, size), F32)]
     if k == 1:
@@ -351,22 +360,20 @@
     )
 
 
-def correct_kernel(k, edges, slots, size, share, sectors, last):
+def residual(mask, value, direction, moved, theta):
+    bottom = jnp.maximum(jnp.abs(moved - theta), 1.0)
+    return jnp.where(mask, (value - theta * direction) / bottom, 0.0)
+
+
+def correct_kernel(k, edges, slots, size, share):
     def body(meta, thetas, whole_image, whole_basis, shift, image, basis, state, *refs):
         meta = Meta(meta, edges, slots)
         bases = refs[: k - 1]
-        if last:
-            corrected, sums, new_state = refs[k - 1 :]
-        else:
-            whole, xin, corrected, sums, new_state = refs[k - 1 :]
-        theta = jnp.sum(thetas[...].reshape(sectors, size), axis=0, keepdims=True)
+        whole, xin, corrected, sums, new_state = refs[k - 1 :]
+        theta = jnp.sum(thetas[...], axis=0)
         new_state[...] = state[...]
         new_state[k - 1 : k] = theta
         first_row = pl.multiple_of(meta.place() * share, share)
-
-        def residual(mask, value, direction, moved):
-            bottom = jnp.maximum(jnp.abs(moved - theta), 1.0)
-            return jnp.where(mask, (value - theta * direction) / bottom, 0.0)
 
         def step(b, carry):
             direction = whole_basis[b]
@@ -375,15 +382,16 @@
                 whole_image[b].astype(F32),
                 direction,
                 shift[b],
+                theta,
             )
-            if not last:
-                whole[b] = value
-                xin[b] = value.astype(BF)
+            whole[b] = value
+            xin[b] = value.astype(BF)
             corrected[b] = residual(
                 mask_of(meta, b, (share, size), first_row),
                 image[b],
                 basis[b],
                 shift[b, pl.ds(first_row, share)],
+                theta,
             )
             others = [bases[j][b] for j in range(k - 1)] + [direction, value]
             return tuple(a + fold(value * o) for a, o in zip(carry, others))
@@ -391,28 +399,67 @@
         carry = lax.fori_loop(
             0, slots, step, tuple(jnp.zeros((8, size), F32) for _ in range(k + 1)), unroll=2
         )
-        if last:
-            line = lax.broadcasted_iota(jnp.int32, (EXTRA, size), 0)
-            tail = jnp.zeros((EXTRA, size), F32)
-            for j in range(k + 1):
-                tail = jnp.where(line == j, total(carry[j]), tail)
-            sums[...] = jnp.broadcast_to(tail[None], (sectors, EXTRA, size))
-        else:
-            tail = jnp.zeros((EXTRA, size), F32)
-            for j in range(k + 1):
-                tail = tail + three_parts(total(carry[j]), j, EXTRA)
-            sums[...] = tail
-
-    blocks = out((slots, size, size), F32)
-    shapes = [out((slots, share, size), F32), out((EXTRA, size), F32), out((24, size), F32)]
-    if last:
-        shapes[1] = out((sectors, EXTRA, size), F32)
-    else:
-        shapes = [blocks, out((slots, size, size), BF)] + shapes
-    return call(body, "correct", [SMEM] + [VMEM] * (6 + k), tuple(shapes))
-
-
-def finish_kernel(slots, size, share, sectors):
+        tail = jnp.zeros((EXTRA, size), F32)
+        for j in range(k + 1):
+            tail = tail + three_parts(total(carry[j]), j, EXTRA)
+        sums[...] = tail
+
+    return call(
+        body,
+        "correct",
+        [SMEM] + [VMEM] * (6 + k),
+        (
+            out((slots, size, size), F32),
+            out((slots, size, size), BF),
+            out((slots, share, size), F32),
+            out((EXTRA, size), F32),
+            out((24, size), F32),
+        ),
+    )
+
+
+def correct_rows_kernel(edges, slots, size, share, devices):
+    k = APPLIES
+
+    def body(meta, thetas, shift, image, state, *refs):
+        meta = Meta(meta, edges, slots)
+        bases = refs[:k]
+        corrected, message, new_state = refs[k:]
+        theta = jnp.sum(thetas[...], axis=0)
+        new_state[...] = state[...]
+        new_state[k - 1 : k] = theta
+        first_row = pl.multiple_of(meta.place() * share, share)
+        carry = [jnp.zeros((8, size), F32) for _ in range(k + 1)]
+        for b in range(slots):
+            value = residual(
+                mask_of(meta, b, (share, size), first_row),
+                image[b],
+                bases[k - 1][b],
+                shift[b, pl.ds(first_row, share)],
+                theta,
+            )
+            corrected[b] = value
+            others = [bases[j][b] for j in range(k)] + [value]
+            carry = [a + fold(value * o) for a, o in zip(carry, others)]
+        lane = lax.broadcasted_iota(jnp.int32, (1, size), 1)
+        row = jnp.zeros((1, size), F32)
+        for j in range(k + 1):
+            row = jnp.where(lane == j, total(carry[j]), row)
+        message[...] = jnp.broadcast_to(row[None], (devices, 1, size))
+
+    return call(
+        body,
+        "correct_rows",
+        [SMEM] + [VMEM] * (4 + k),
+        (
+            out((slots, share, size), F32),
+            out((devices, 1, size), F32),
+            out((24, size), F32),
+        ),
+    )
+
+
+def finish_kernel(slots, size, share):
     k = APPLIES
 
     def body(sums, vector, state, *refs):
@@ -420,13 +467,15 @@
         images = refs[k : 2 * k]
         stacked, final, ritz = refs[2 * k :]
         added = jnp.sum(sums[...], axis=0)
-        project = [added[j : j + 1] for j in range(k)]
-        length = added[k : k + 1]
+        lane = lax.broadcasted_iota(jnp.int32, (1, size), 1)
+        totals = [total(jnp.where(lane == j, added, 0.0)) for j in range(k + 1)]
+        project = totals[:k]
+        length = totals[k]
         for i in range(k):
-            mixed = jnp.zeros((1, size), F32)
+            mixed = jnp.zeros((1, 1), F32)
             for j in range(k):
                 row = 8 + 4 * max(i, j) + min(i, j)
-                mixed = mixed + state[row : row + 1] * project[j]
+                mixed = mixed + state[row : row + 1, 0:1] * project[j]
             length = length + project[i] * (mixed - 2.0 * project[i])
         scale = 1.0 / jnp.sqrt(jnp.maximum(length, 0.0) + 1e-6)
         for b in range(slots):
@@ -472,6 +521,7 @@
     group = left_env.shape[0]
     share = size // terms
     chips = terms // 2
+    devices = sectors * terms
     place = lax.axis_index("mpo")
     core_swap = [(i, i ^ 1) for i in range(terms)]
     meta = jnp.concatenate(
@@ -490,6 +540,9 @@
     def over_sector(values):
         return lax.all_to_all(values, "sector", 0, 0, tiled=True)
 
+    def over_all(values):
+        return lax.all_to_all(values, ("sector", "mpo"), 0, 0, tiled=True)
+
     def chip_shift(values, k):
         pairs = [(i, (i + 2 * k) % terms) for i in range(terms)]
         return lax.ppermute(values, "mpo", pairs)
@@ -510,36 +563,38 @@
         shifted = [parts[0]] + [chip_shift(parts[j], j) for j in range(1, chips)]
         message = pack_kernel(edges, slots, size, share, sectors, k == 1)(meta, sums, *shifted)
         arrived = over_sector(message)
-        result = image_kernel(k, edges, slots, size, share, sectors)(
+        result = image_kernel(k, edges, slots, size, share, sectors, devices)(
             meta, arrived, mine, state, *bases, *images, *ids
         )
         image, basis, outgoing, state = result[:4]
+        bases.append(basis)
+        images.append(image)
         if k == 1:
             ids = result[4:]
+        if k == APPLIES:
+            break
         rows = [outgoing] + [chip_shift(outgoing, j) for j in range(1, chips)]
         near_rows = gather_kernel(slots, size, share, chips)(*rows)
         far_rows = lax.ppermute(near_rows, "mpo", core_swap)
         whole_image, whole_basis, parts = weigh_kernel(
             k, edges, slots, size, share, sectors, chips
-        )(
-            meta, near_rows, far_rows, vector, state, *whole_bases
+        )(meta, near_rows, far_rows, vector, state, *whole_bases)
+        vector, xin, mine, sums, state = correct_kernel(k, edges, slots, size, share)(
+            meta,
+            over_sector(parts),
+            whole_image,
+            whole_basis,
+            diag_shift,
+            image,
+            basis,
+            state,
+            *whole_bases,
         )
-        thetas = over_sector(parts)
-        last = k == APPLIES
-        result = correct_kernel(k, edges, slots, size, share, sectors, last)(
-            meta, thetas, whole_image, whole_basis, diag_shift, image, basis, state, *whole_bases
-        )
-        if last:
-            mine, sums, state = result
-        else:
-            vector, xin, mine, sums, state = result
-            whole_bases.append(whole_basis)
-        bases.append(basis)
-        images.append(image)
-    stacked, final, ritz = finish_kernel(slots, size, share, sectors)(
-        over_sector(sums), mine, state, *bases, *images
-    )
-    return stacked, final, ritz
+        whole_bases.append(whole_basis)
+    mine, parts, state = correct_rows_kernel(edges, slots, size, share, devices)(
+        meta, over_all(outgoing), diag_shift, image, state, *bases
+    )
+    return finish_kernel(slots, size, share)(over_all(parts), mine, state, *bases, *images)
 
 
 def solution(mesh):

time: 220 us -> 222 us (level); the launches traced: 219 us -> 219 us
  blocking collectives: 113 us -> 124 us
  waiting for transfers between devices: 39 us -> 33.2 us
  starting transfers between devices: 30.1 us -> 24.5 us
    all_to_all x0 -> x2, blocking collectives: none -> 38 us  [over_all(): return lax.all_to_all(values, ('sector', 'mpo'), 0, 0, tiled=True)]
    all_to_all x7 -> x5, blocking collectives: 113 us -> 85.7 us  [over_sector(): return lax.all_to_all(values, 'sector', 0, 0, tiled=True)]
    ppermute x18 -> x15, starting transfers between devices: 29.3 us -> 23.8 us  [chip_shift(): return lax.ppermute(values, 'mpo', pairs)]
    ppermute x18 -> x15, waiting for transfers between devices: 28.7 us -> 24.4 us  [chip_shift(): return lax.ppermute(values, 'mpo', pairs)]
    ppermute x3 -> x2, waiting for transfers between devices: 4.57 us -> 3.04 us  [per_device(): far_rows = lax.ppermute(near_rows, 'mpo', core_swap)]
  transfers between devices with their start and end apart: 24 -> 20, of which waited for: 24 -> 20; matrix products, arithmetic and copies ran while one was open for 0% -> 0% of each run, Pallas kernels for 0% -> 0%
where the time goes in v4:
time: 222 us; the launch traced here: 219 us
  blocking collectives  124 us (56%)
  Pallas kernels  35.6 us (16%)
  waiting for transfers between devices  33.2 us (15%)
  starting transfers between devices  24.5 us (11%)
    all_to_all x5, blocking collectives, over_sector(): return lax.all_to_all(values, 'sector', 0, 0, tiled=True)  85.7 us
    all_to_all x2, blocking collectives, over_all(): return lax.all_to_all(values, ('sector', 'mpo'), 0, 0, tiled=True)  38 us
    ppermute x15, waiting for transfers between devices, chip_shift(): return lax.ppermute(values, 'mpo', pairs)  24.4 us
    ppermute x15, starting transfers between devices, chip_shift(): return lax.ppermute(values, 'mpo', pairs)  23.8 us
    pallas_call x3, Pallas kernels, per_device(): couple_kernel(edges, slots, size, share, group, chips)  16.7 us
    ppermute x3, waiting for transfers between devices, per_device(): received = lax.ppermute(send, 'mpo', core_swap)  5.69 us
  transfers between devices with their start and end apart: 20, of which 20 were waited for; matrix products, arithmetic and copies ran while one was open for 0% of the time, Pallas kernels for 0%

profile of v4, /device:TPU:4, one launch (start us, length us, event | category | flops | bytes accessed | tf_op | source)
XLA Modules:
  0.0 218.9 jit_solution(10807819426649529534)
XLA Ops:
  1.5 4.4 %start.1 = (f32[16,128,128]{2,1,0:T(8,128)S(1)}, bf16[16,128,128]{2,1,0:T(8,128)(2,1)S(1)}, f32[16,16,128]{2,1,0:T(8,128)S(1)}, f32[8,128]{1,0:T(8,128)S(1)}, f3...) custom-call(s32[193]{0:T(256)S(1)} %concatenate.3.meta, ...), custom_call_target="tpu_custom_call" | custom-call | tf_op jit(solution)/shard_map/start/pallas_call | solution.py:553
  5.8 5.6 %couple.3 = (bf16[4,32,16,128]{3,2,1,0:T(8,128)(2,1)S(1)}, bf16[4,32,16,128]{3,2,1,0:T(8,128)(2,1)S(1)}, bf16[8,16,128,128]{3,2,1,0:T(8,128)(2,1)S(1)}, bf16[8,16,128,128]{3,2,1,0:T(8,128)(2,1)S(1)}) custom-call(s32[193]{0:T(256)S(1)} %concatenate.3.meta, ...), custom_call_target="tpu_custom_call", output_to_operand_aliasing={{2}: (2, {}), {3}: (3, {})} | custom-call | tf_op jit(solution)/shard_map/couple/pallas_call | solution.py:558
  11.5 1.9 collective-permute-done.received
  15.9 2.5 %collective-permute-start.3 = (bf16[32,16,128]{2,1,0:T(8,128)(2,1)S(1)}, bf16[32,16,128]{2,1,0:T(8,128)(2,1)S(1)}, u32[]{:S(2)}, u32[]{:S(2)}) collective-permute-start(bf16[32,16,128]{2,1,0:T(8,128)(2,1)S(1)} %get-tuple-element.72), channel_id=1, source_target_pairs={{0,6},{1,7},{2,0},{3,1},{4,2},{5,3},{6,4},{7,5},{8,14},{9,15},{10,... | collective-permute-start | bytes 393224 | tf_op jit(solution)/shard_map/ppermute | solution.py:548
  19.3 3.2 %collective-permute-done.2.third = bf16[32,16,128]{2,1,0:T(8,128)(2,1)S(1)} collective-permute-done((bf16[32,16,128]{2,1,0:T(8,128)(2,1)S(1)}, bf16[32,16,128]{2,1,0:T(8,128)(2,1)S(1)}, u32[]{:S(2)}, u32[]{:S(2)}) %collective-permute-start.2) | collective-permute-done | bytes 131104 | tf_op jit(solution)/shard_map/ppermute | solution.py:548
  24.6 24.7 %all_to_all.35.arrived = bf16[32,40,128]{2,1,0:T(8,128)(2,1)S(1)} all-to-all(bf16[32,40,128]{2,1,0:T(8,128)(2,1)S(1)} %pack.3), channel_id=1, replica_groups=mesh['sector'=32,'mpo'=8] {'sector'}, dimensions={0} | all-to-all | bytes 655360 | tf_op jit(solution)/shard_map/all_to_all | solution.py:541
  49.3 2.2 %image.3 = (f32[16,16,128]{2,1,0:T(8,128)S(1)}, f32[16,16,128]{2,1,0:T(8,128)S(1)}, bf16[16,16,128]{2,1,0:T(8,128)(2,1)S(1)}, f32[24,128]{1,0:T(8,128)S(1)}, s32[64]{0:T(128)S(1)}) custom-call(s32[193]{0:T(256)S(1)} %concatenate.3.meta, bf16[32,40,128]{2,1,0:T(8,128)(2,1)S(1)} %all_to_all.35.arrived, f32[16,16,128]{2,1,0:T(8,128)S(1)} %get-tuple-element.73.vector, ...), custom_call_target="tpu_custom_call" | custom-call | tf_op jit(solution)/shard_map/image/pallas_call | solution.py:566
  52.4 2.5 %collective-permute-start.5 = (bf16[16,16,128]{2,1,0:T(8,128)(2,1)S(1)}, bf16[16,16,128]{2,1,0:T(8,128)(2,1)S(1)}, u32[]{:S(2)}, u32[]{:S(2)}) collective-permute-start(bf16[16,16,128]{2,1,0:T(8,128)(2,1)S(1)} %get-tuple-element.75.refs_0_), channel_id=1, source_target_pairs={{0,4},{1,5},{2,6},{3,7},{4,0},{5,1},{6,2},{7,3},{8,12},{9,13},{10,... | collective-permute-start | bytes 196616 | tf_op jit(solution)/shard_map/ppermute | solution.py:548
  55.9 2.3 %collective-permute-done.5.refs_2_ = bf16[16,16,128]{2,1,0:T(8,128)(2,1)S(1)} collective-permute-done((bf16[16,16,128]{2,1,0:T(8,128)(2,1)S(1)}, bf16[16,16,128]{2,1,0:T(8,128)(2,1)S(1)}, u32[]{:S(2)}, u32[]{:S(2)}) %collective-permute-start.5) | collective-permute-done | bytes 65568 | tf_op jit(solution)/shard_map/ppermute | solution.py:548
  59.3 1.5 collective-permute-done.7.other
  61.7 13.8 %all_to_all.36.thetas = f32[32,1,128]{2,1,0:T(1,128)S(1)} all-to-all(f32[32,1,128]{2,1,0:T(1,128)S(1)} %get-tuple-element.78), channel_id=1, replica_groups=mesh['sector'=32,'mpo'=8] {'sector'}, dimensions={0} | all-to-all | bytes 32768 | tf_op jit(solution)/shard_map/all_to_all | solution.py:541
  76.9 5.6 %couple.4 = (bf16[4,32,16,128]{3,2,1,0:T(8,128)(2,1)S(1)}, bf16[4,32,16,128]{3,2,1,0:T(8,128)(2,1)S(1)}, bf16[8,16,128,128]{3,2,1,0:T(8,128)(2,1)S(1)}, bf16[8,16,128,128]{3,2,1,0:T(8,128)(2,1)S(1)}) custom-call(s32[193]{0:T(256)S(1)} %concatenate.3.meta, ...), custom_call_target="tpu_custom_call", output_to_operand_aliasing={{2}: (2, {}), {3}: (3, {})} | custom-call | tf_op jit(solution)/shard_map/couple/pallas_call | solution.py:558
  82.6 1.9 collective-permute-done.8.received
  85.4 1.6 collective-permute-start.10
  87.0 2.5 %collective-permute-start.11 = (bf16[32,16,128]{2,1,0:T(8,128)(2,1)S(1)}, bf16[32,16,128]{2,1,0:T(8,128)(2,1)S(1)}, u32[]{:S(2)}, u32[]{:S(2)}) collective-permute-start(bf16[32,16,128]{2,1,0:T(8,128)(2,1)S(1)} %get-tuple-element.92), channel_id=1, source_target_pairs={{0,6},{1,7},{2,0},{3,1},{4,2},{5,3},{6,4},{7,5},{8,14},{9,15},{10,... | collective-permute-start | bytes 393224 | tf_op jit(solution)/shard_map/ppermute | solution.py:548
  90.3 3.2 %collective-permute-done.10.third = bf16[32,16,128]{2,1,0:T(8,128)(2,1)S(1)} collective-permute-done((bf16[32,16,128]{2,1,0:T(8,128)(2,1)S(1)}, bf16[32,16,128]{2,1,0:T(8,128)(2,1)S(1)}, u32[]{:S(2)}, u32[]{:S(2)}) %collective-permute-start.10) | collective-permute-done | bytes 131104 | tf_op jit(solution)/shard_map/ppermute | solution.py:548
  95.5 16.8 %all_to_all.37.arrived = bf16[32,40,128]{2,1,0:T(8,128)(2,1)S(1)} all-to-all(bf16[32,40,128]{2,1,0:T(8,128)(2,1)S(1)} %pack.4), channel_id=1, replica_groups=mesh['sector'=32,'mpo'=8] {'sector'}, dimensions={0} | all-to-all | bytes 655360 | tf_op jit(solution)/shard_map/all_to_all | solution.py:541
  113.3 2.1 collective-permute-start.14
  115.4 3.6 %collective-permute-start.13 = (bf16[16,16,128]{2,1,0:T(8,128)(2,1)S(1)}, bf16[16,16,128]{2,1,0:T(8,128)(2,1)S(1)}, u32[]{:S(2)}, u32[]{:S(2)}) collective-permute-start(bf16[16,16,128]{2,1,0:T(8,128)(2,1)S(1)} %get-tuple-element.96.refs_0_), channel_id=1, source_target_pairs={{0,4},{1,5},{2,6},{3,7},{4,0},{5,1},{6,2},{7,3},{8,12},{9,13},{10,... | collective-permute-start | bytes 196616 | tf_op jit(solution)/shard_map/ppermute | solution.py:548
  119.2 2.1 collective-permute-done.13.refs_2_
  121.3 2.0 collective-permute-done.12.refs_1_
  123.4 1.5 collective-permute-done.15.other
  125.9 13.5 %all_to_all.38.thetas = f32[32,1,128]{2,1,0:T(1,128)S(1)} all-to-all(f32[32,1,128]{2,1,0:T(1,128)S(1)} %get-tuple-element.99), channel_id=1, replica_groups=mesh['sector'=32,'mpo'=8] {'sector'}, dimensions={0} | all-to-all | bytes 32768 | tf_op jit(solution)/shard_map/all_to_all | solution.py:541
  139.4 2.3 %correct.3 = (f32[16,128,128]{2,1,0:T(8,128)}, bf16[16,128,128]{2,1,0:T(8,128)(2,1)S(1)}, f32[16,16,128]{2,1,0:T(8,128)S(1)}, f32[8,128]{1,0:T(8,128)S(1)}, f32[24,128]{1,0:T(8,128)S(1)}) custom-call(s32[193]{0:T(256)S(1)} %concatenate.3.meta, f32[32,1,128]{2,1,0:T(1,128)S(1)} %all_to_all.38.thetas, ...), custom_call_target="tpu_custom_call" | custom-call | tf_op jit(solution)/shard_map/correct/pallas_call | solution.py:582
  141.7 5.6 %couple.5 = (bf16[4,32,16,128]{3,2,1,0:T(8,128)(2,1)S(1)}, bf16[4,32,16,128]{3,2,1,0:T(8,128)(2,1)S(1)}, bf16[8,16,128,128]{3,2,1,0:T(8,128)(2,1)S(1)}, bf16[8,16,128,128]{3,2,1,0:T(8,128)(2,1)S(1)}) custom-call(s32[193]{0:T(256)S(1)} %concatenate.3.meta, ...), custom_call_target="tpu_custom_call", output_to_operand_aliasing={{2}: (2, {}), {3}: (3, {})} | custom-call | tf_op jit(solution)/shard_map/couple/pallas_call | solution.py:558
  147.6 1.9 collective-permute-done.16.received
  151.7 2.5 %collective-permute-start.19 = (bf16[32,16,128]{2,1,0:T(8,128)(2,1)S(1)}, bf16[32,16,128]{2,1,0:T(8,128)(2,1)S(1)}, u32[]{:S(2)}, u32[]{:S(2)}) collective-permute-start(bf16[32,16,128]{2,1,0:T(8,128)(2,1)S(1)} %get-tuple-element.113), channel_id=1, source_target_pairs={{0,6},{1,7},{2,0},{3,1},{4,2},{5,3},{6,4},{7,5},{8,14},{9,15},{10,... | collective-permute-start | bytes 393224 | tf_op jit(solution)/shard_map/ppermute | solution.py:548
  155.7 2.6 %collective-permute-done.18.third = bf16[32,16,128]{2,1,0:T(8,128)(2,1)S(1)} collective-permute-done((bf16[32,16,128]{2,1,0:T(8,128)(2,1)S(1)}, bf16[32,16,128]{2,1,0:T(8,128)(2,1)S(1)}, u32[]{:S(2)}, u32[]{:S(2)}) %collective-permute-start.18) | collective-permute-done | bytes 131104 | tf_op jit(solution)/shard_map/ppermute | solution.py:548
  158.2 1.6 collective-permute-done.19.fourth
  160.6 16.8 %all_to_all.39.arrived = bf16[32,40,128]{2,1,0:T(8,128)(2,1)S(1)} all-to-all(bf16[32,40,128]{2,1,0:T(8,128)(2,1)S(1)} %pack.5), channel_id=1, replica_groups=mesh['sector'=32,'mpo'=8] {'sector'}, dimensions={0} | all-to-all | bytes 655360 | tf_op jit(solution)/shard_map/all_to_all | solution.py:541
  178.5 19.7 %all_to_all.40.thetas = f32[256,1,128]{2,1,0:T(1,128)S(1)} all-to-all(f32[256,1,128]{2,1,0:T(1,128)S(1)} %get-tuple-element.116), channel_id=1, replica_groups=mesh['sector'=32,'mpo'=8] {'sector','mpo'}, dimensions={0} | all-to-all | bytes 262144 | tf_op jit(solution)/shard_map/all_to_all | solution.py:544
  199.2 18.4 %all_to_all.41.sums = f32[256,1,128]{2,1,0:T(1,128)S(1)} all-to-all(f32[256,1,128]{2,1,0:T(1,128)S(1)} %get-tuple-element.120), channel_id=1, replica_groups=mesh['sector'=32,'mpo'=8] {'sector','mpo'}, dimensions={0} | all-to-all | bytes 262144 | tf_op jit(solution)/shard_map/all_to_all | solution.py:544
  (39 shorter events, 25.4 us)
Async XLA Ops:
  11.4 64.2 %copy-start = (f32[16,128,128]{2,1,0:T(8,128)S(1)}, f32[16,128,128]{2,1,0:T(8,128)}, u32[]{:S(2)}) copy-start(f32[16,128,128]{2,1,0:T(8,128)} %shift.5) | copy-start | bytes 3145732
  11.4 2.0 collective-permute-start
  13.5 5.7 %collective-permute-start.1 = (bf16[32,16,128]{2,1,0:T(8,128)(2,1)S(1)}, bf16[32,16,128]{2,1,0:T(8,128)(2,1)S(1)}, u32[]{:S(2)}, u32[]{:S(2)}) collective-permute-start(bf16[32,16,128]{2,1,0:T(8,128)(2,1)S(1)} %get-tuple-element.70), channel_id=1, source_target_pairs={{0,2},{1,3},{2,4},{3,5},{4,6},{5,7},{6,0},{7,1},{8,10},{9,11},{10,... | collective-permute-start | bytes 393224 | tf_op jit(solution)/shard_map/ppermute | solution.py:548
  14.8 7.6 %collective-permute-start.2 = (bf16[32,16,128]{2,1,0:T(8,128)(2,1)S(1)}, bf16[32,16,128]{2,1,0:T(8,128)(2,1)S(1)}, u32[]{:S(2)}, u32[]{:S(2)}) collective-permute-start(bf16[32,16,128]{2,1,0:T(8,128)(2,1)S(1)} %get-tuple-element.71), channel_id=1, source_target_pairs={{0,4},{1,5},{2,6},{3,7},{4,0},{5,1},{6,2},{7,3},{8,12},{9,13},{10,... | collective-permute-start | bytes 393224 | tf_op jit(solution)/shard_map/ppermute | solution.py:548
  15.9 7.8 %collective-permute-start.3 = (bf16[32,16,128]{2,1,0:T(8,128)(2,1)S(1)}, bf16[32,16,128]{2,1,0:T(8,128)(2,1)S(1)}, u32[]{:S(2)}, u32[]{:S(2)}) collective-permute-start(bf16[32,16,128]{2,1,0:T(8,128)(2,1)S(1)} %get-tuple-element.72), channel_id=1, source_target_pairs={{0,6},{1,7},{2,0},{3,1},{4,2},{5,3},{6,4},{7,5},{8,14},{9,15},{10,... | collective-permute-start | bytes 393224 | tf_op jit(solution)/shard_map/ppermute | solution.py:548
  51.5 4.3 %collective-permute-start.6 = (bf16[16,16,128]{2,1,0:T(8,128)(2,1)S(1)}, bf16[16,16,128]{2,1,0:T(8,128)(2,1)S(1)}, u32[]{:S(2)}, u32[]{:S(2)}) collective-permute-start(bf16[16,16,128]{2,1,0:T(8,128)(2,1)S(1)} %get-tuple-element.75.refs_0_), channel_id=1, source_target_pairs={{0,6},{1,7},{2,0},{3,1},{4,2},{5,3},{6,4},{7,5},{8,14},{9,15},{10,... | collective-permute-start | bytes 196616 | tf_op jit(solution)/shard_map/ppermute | solution.py:548
  52.4 5.8 %collective-permute-start.5 = (bf16[16,16,128]{2,1,0:T(8,128)(2,1)S(1)}, bf16[16,16,128]{2,1,0:T(8,128)(2,1)S(1)}, u32[]{:S(2)}, u32[]{:S(2)}) collective-permute-start(bf16[16,16,128]{2,1,0:T(8,128)(2,1)S(1)} %get-tuple-element.75.refs_0_), channel_id=1, source_target_pairs={{0,4},{1,5},{2,6},{3,7},{4,0},{5,1},{6,2},{7,3},{8,12},{9,13},{10,... | collective-permute-start | bytes 196616 | tf_op jit(solution)/shard_map/ppermute | solution.py:548
  54.9 4.3 %collective-permute-start.4 = (bf16[16,16,128]{2,1,0:T(8,128)(2,1)S(1)}, bf16[16,16,128]{2,1,0:T(8,128)(2,1)S(1)}, u32[]{:S(2)}, u32[]{:S(2)}) collective-permute-start(bf16[16,16,128]{2,1,0:T(8,128)(2,1)S(1)} %get-tuple-element.75.refs_0_), channel_id=1, source_target_pairs={{0,2},{1,3},{2,4},{3,5},{4,6},{5,7},{6,0},{7,1},{8,10},{9,11},{10,... | collective-permute-start | bytes 196616 | tf_op jit(solution)/shard_map/ppermute | solution.py:548
  59.2 1.6 collective-permute-start.7
  82.5 2.0 collective-permute-start.8
  84.6 5.7 %collective-permute-start.9 = (bf16[32,16,128]{2,1,0:T(8,128)(2,1)S(1)}, bf16[32,16,128]{2,1,0:T(8,128)(2,1)S(1)}, u32[]{:S(2)}, u32[]{:S(2)}) collective-permute-start(bf16[32,16,128]{2,1,0:T(8,128)(2,1)S(1)} %get-tuple-element.90), channel_id=1, source_target_pairs={{0,2},{1,3},{2,4},{3,5},{4,6},{5,7},{6,0},{7,1},{8,10},{9,11},{10,... | collective-permute-start | bytes 393224 | tf_op jit(solution)/shard_map/ppermute | solution.py:548
  85.4 8.1 %collective-permute-start.10 = (bf16[32,16,128]{2,1,0:T(8,128)(2,1)S(1)}, bf16[32,16,128]{2,1,0:T(8,128)(2,1)S(1)}, u32[]{:S(2)}, u32[]{:S(2)}) collective-permute-start(bf16[32,16,128]{2,1,0:T(8,128)(2,1)S(1)} %get-tuple-element.91), channel_id=1, source_target_pairs={{0,4},{1,5},{2,6},{3,7},{4,0},{5,1},{6,2},{7,3},{8,12},{9,13},{10,... | collective-permute-start | bytes 393224 | tf_op jit(solution)/shard_map/ppermute | solution.py:548
  87.0 7.8 %collective-permute-start.11 = (bf16[32,16,128]{2,1,0:T(8,128)(2,1)S(1)}, bf16[32,16,128]{2,1,0:T(8,128)(2,1)S(1)}, u32[]{:S(2)}, u32[]{:S(2)}) collective-permute-start(bf16[32,16,128]{2,1,0:T(8,128)(2,1)S(1)} %get-tuple-element.92), channel_id=1, source_target_pairs={{0,6},{1,7},{2,0},{3,1},{4,2},{5,3},{6,4},{7,5},{8,14},{9,15},{10,... | collective-permute-start | bytes 393224 | tf_op jit(solution)/shard_map/ppermute | solution.py:548
  113.3 5.9 %collective-permute-start.14 = (bf16[16,16,128]{2,1,0:T(8,128)(2,1)S(1)}, bf16[16,16,128]{2,1,0:T(8,128)(2,1)S(1)}, u32[]{:S(2)}, u32[]{:S(2)}) collective-permute-start(bf16[16,16,128]{2,1,0:T(8,128)(2,1)S(1)} %get-tuple-element.96.refs_0_), channel_id=1, source_target_pairs={{0,6},{1,7},{2,0},{3,1},{4,2},{5,3},{6,4},{7,5},{8,14},{9,15},{10,... | collective-permute-start | bytes 196616 | tf_op jit(solution)/shard_map/ppermute | solution.py:548
  115.4 5.9 %collective-permute-start.13 = (bf16[16,16,128]{2,1,0:T(8,128)(2,1)S(1)}, bf16[16,16,128]{2,1,0:T(8,128)(2,1)S(1)}, u32[]{:S(2)}, u32[]{:S(2)}) collective-permute-start(bf16[16,16,128]{2,1,0:T(8,128)(2,1)S(1)} %get-tuple-element.96.refs_0_), channel_id=1, source_target_pairs={{0,4},{1,5},{2,6},{3,7},{4,0},{5,1},{6,2},{7,3},{8,12},{9,13},{10,... | collective-permute-start | bytes 196616 | tf_op jit(solution)/shard_map/ppermute | solution.py:548
  119.0 4.3 %collective-permute-start.12 = (bf16[16,16,128]{2,1,0:T(8,128)(2,1)S(1)}, bf16[16,16,128]{2,1,0:T(8,128)(2,1)S(1)}, u32[]{:S(2)}, u32[]{:S(2)}) collective-permute-start(bf16[16,16,128]{2,1,0:T(8,128)(2,1)S(1)} %get-tuple-element.96.refs_0_), channel_id=1, source_target_pairs={{0,2},{1,3},{2,4},{3,5},{4,6},{5,7},{6,0},{7,1},{8,10},{9,11},{10,... | collective-permute-start | bytes 196616 | tf_op jit(solution)/shard_map/ppermute | solution.py:548
  123.3 1.6 collective-permute-start.15
  147.3 2.2 %collective-permute-start.16 = (bf16[4,32,16,128]{3,2,1,0:T(8,128)(2,1)S(1)}, bf16[4,32,16,128]{3,2,1,0:T(8,128)(2,1)S(1)}, u32[]{:S(2)}, u32[]{:S(2)}) collective-permute-start(bf16[4,32,16,128]{3,2,1,0:T(8,128)(2,1)S(1)} %get-tuple-element.109), channel_id=1, source_target_pairs={{0,1},{1,0},{2,3},{3,2},{4,5},{5,4},{6,7},{7,6},{8,9},{9,8},{10,11... | collective-permute-start | bytes 1572872 | tf_op jit(solution)/shard_map/ppermute | solution.py:561
  149.7 6.0 %collective-permute-start.17 = (bf16[32,16,128]{2,1,0:T(8,128)(2,1)S(1)}, bf16[32,16,128]{2,1,0:T(8,128)(2,1)S(1)}, u32[]{:S(2)}, u32[]{:S(2)}) collective-permute-start(bf16[32,16,128]{2,1,0:T(8,128)(2,1)S(1)} %get-tuple-element.111), channel_id=1, source_target_pairs={{0,2},{1,3},{2,4},{3,5},{4,6},{5,7},{6,0},{7,1},{8,10},{9,11},{10,... | collective-permute-start | bytes 393224 | tf_op jit(solution)/shard_map/ppermute | solution.py:548
  150.5 7.8 %collective-permute-start.18 = (bf16[32,16,128]{2,1,0:T(8,128)(2,1)S(1)}, bf16[32,16,128]{2,1,0:T(8,128)(2,1)S(1)}, u32[]{:S(2)}, u32[]{:S(2)}) collective-permute-start(bf16[32,16,128]{2,1,0:T(8,128)(2,1)S(1)} %get-tuple-element.112), channel_id=1, source_target_pairs={{0,4},{1,5},{2,6},{3,7},{4,0},{5,1},{6,2},{7,3},{8,12},{9,13},{10,... | collective-permute-start | bytes 393224 | tf_op jit(solution)/shard_map/ppermute | solution.py:548
  151.7 8.1 %collective-permute-start.19 = (bf16[32,16,128]{2,1,0:T(8,128)(2,1)S(1)}, bf16[32,16,128]{2,1,0:T(8,128)(2,1)S(1)}, u32[]{:S(2)}, u32[]{:S(2)}) collective-permute-start(bf16[32,16,128]{2,1,0:T(8,128)(2,1)S(1)} %get-tuple-element.113), channel_id=1, source_target_pairs={{0,6},{1,7},{2,0},{3,1},{4,2},{5,3},{6,4},{7,5},{8,14},{9,15},{10,... | collective-permute-start | bytes 393224 | tf_op jit(solution)/shard_map/ppermute | solution.py:548

commit v5 on v3

--- a/solution.py
+++ b/solution.py
@@ -79,38 +79,97 @@
     return (line < meta.rows(block)) & (lane < meta.cols(block))
 
 
-def start_kernel(edges, slots, size, share, group):
+def couple_rows(meta, chips, share, own, send, tmp, e, u, value):
+    x = meta.place() // 2
+    c = lax.rem(meta.place(), 2)
+    tmp[u] = value.astype(BF)
+    for k in range(chips):
+        to = lax.rem(x + k, chips)
+        mine = pl.multiple_of((2 * to + c) * share, share)
+        other = pl.multiple_of((2 * to + 1 - c) * share, share)
+        own[k, e] = tmp[u, pl.ds(mine, share)]
+        send[k, e] = tmp[u, pl.ds(other, share)]
+
+
+def add_terms(meta, xin, right, left, e, terms, acc):
+    value = xin[meta.edge(IN, e)]
+    le = meta.edge(LEFT, e)
+    re = meta.edge(RIGHT, e)
+    for w in terms:
+        half = jnp.dot(value, right[w, re], preferred_element_type=F32).astype(BF)
+        term = jnp.dot(left[w, le], half, preferred_element_type=F32)
+        acc = term if acc is None else acc + term
+    return acc
+
+
+def unrolled(edges, one):
+    def step(t, carry):
+        for u in range(UNROLL):
+            one(t * UNROLL + u, u)
+        return carry
+
+    lax.fori_loop(0, edges // UNROLL, step, 0)
+
+
+def begin_kernel(edges, slots, size, share, group, chips):
+    terms = group // PIECES
+
     def body(meta, far_guess, right, left, *refs):
         meta = Meta(meta, edges, slots)
-        vector, xin, own, sums, state, right_near, left_near, guess, sems, guess_sem = refs
-        state[...] = jnp.zeros_like(state)
+        vector, xin, mine, sums, state, right_near, left_near, own, send = refs[:9]
+        guess, acc, tmp, sems, guess_sem = refs[9:]
         first = pltpu.make_async_copy(far_guess, guess, guess_sem)
         first.start()
         copies = []
-        for i, (far, near) in enumerate(((right, right_near), (left, left_near))):
-            for p in range(PIECES):
-                part = pl.ds(p * (group // PIECES), group // PIECES)
-                copies.append(pltpu.make_async_copy(far.at[part], near.at[part], sems.at[i, p]))
-        for copy in copies:
-            copy.start()
-        acc = jnp.zeros((8, size), F32)
+        for p in range(PIECES):
+            part = pl.ds(p * terms, terms)
+            copies.append(
+                [
+                    pltpu.make_async_copy(far.at[part], near.at[part], sems.at[i, p])
+                    for i, (far, near) in enumerate(((right, right_near), (left, left_near)))
+                ]
+            )
+            for copy in copies[p]:
+                copy.start()
+        state[...] = jnp.zeros_like(state)
         first_row = pl.multiple_of(meta.place() * share, share)
         first.wait()
-        for b in range(slots):
+
+        def block(b, squares):
             value = jnp.where(mask_of(meta, b, (size, size), 0), guess[b], 0.0)
             vector[b] = value
             xin[b] = value.astype(BF)
-            acc = acc + fold(value * value)
-            mine = guess[b, pl.ds(first_row, share)]
-            own[b] = jnp.where(mask_of(meta, b, (share, size), first_row), mine, 0.0)
-        sums[...] = three_parts(total(acc), 0, EXTRA)
-        for copy in copies:
-            copy.wait()
+            rows = guess[b, pl.ds(first_row, share)]
+            mine[b] = jnp.where(mask_of(meta, b, (share, size), first_row), rows, 0.0)
+            return squares + fold(value * value)
+
+        squares = lax.fori_loop(0, slots, block, jnp.zeros((8, size), F32), unroll=4)
+        sums[...] = three_parts(total(squares), 0, EXTRA)
+        half = PIECES // 2
+        for p in range(half):
+            for copy in copies[p]:
+                copy.wait()
+
+        def early(e, u):
+            acc[e] = add_terms(meta, xin, right_near, left_near, e, range(group // 2), None)
+
+        unrolled(edges, early)
+        for p in range(half, PIECES):
+            for copy in copies[p]:
+                copy.wait()
+
+        def late(e, u):
+            rest = range(group // 2, group)
+            value = add_terms(meta, xin, right_near, left_near, e, rest, acc[e])
+            couple_rows(meta, chips, share, own, send, tmp, e, u, value)
+
+        unrolled(edges, late)
 
     near = pltpu.VMEM((group, slots, size, size), BF)
+    shape = out((chips, edges, share, size), BF)
     return call(
         body,
-        "start",
+        "begin",
         [SMEM, FAR, FAR, FAR],
         (
             out((slots, size, size), F32),
@@ -120,9 +179,13 @@
             out((24, size), F32),
             near,
             near,
+            shape,
+            shape,
         ),
         [
             pltpu.VMEM((slots, size, size), F32),
+            pltpu.VMEM((edges, size, size), F32),
+            pltpu.VMEM((UNROLL, size, size), BF),
             pltpu.SemaphoreType.DMA((2, PIECES)),
             pltpu.SemaphoreType.DMA,
         ],
@@ -133,33 +196,12 @@
     def body(meta, xin, right, left, own, send, *refs):
         meta = Meta(meta, edges, slots)
         tmp = refs[-1]
-        x = meta.place() // 2
-        c = lax.rem(meta.place(), 2)
 
         def one(e, u):
-            i = meta.edge(IN, e)
-            le = meta.edge(LEFT, e)
-            re = meta.edge(RIGHT, e)
-            value = xin[i]
-            acc = None
-            for w in range(group):
-                half = jnp.dot(value, right[w, re], preferred_element_type=F32).astype(BF)
-                term = jnp.dot(left[w, le], half, preferred_element_type=F32)
-                acc = term if acc is None else acc + term
-            tmp[u] = acc.astype(BF)
-            for k in range(chips):
-                to = lax.rem(x + k, chips)
-                mine = pl.multiple_of((2 * to + c) * share, share)
-                other = pl.multiple_of((2 * to + 1 - c) * share, share)
-                own[k, e] = tmp[u, pl.ds(mine, share)]
-                send[k, e] = tmp[u, pl.ds(other, share)]
-
-        def step(t, carry):
-            for u in range(UNROLL):
-                one(t * UNROLL + u, u)
-            return carry
-
-        lax.fori_loop(0, edges // UNROLL, step, 0)
+            value = add_terms(meta, xin, right, left, e, range(group), None)
+            couple_rows(meta, chips, share, own, send, tmp, e, u, value)
+
+        unrolled(edges, one)
 
     shape = out((chips, edges, share, size), BF)
     near = pltpu.VMEM((group, slots, size, size), BF)
@@ -320,7 +362,7 @@
         x = meta.place() // 2
         c = lax.rem(meta.place(), 2)
         for j in range(chips):
-            origin = 2 * lax.rem(x + chips - j, chips)
+            origin = 2 * lax.bitwise_xor(x, j)
             near = pl.multiple_of((origin + c) * share, share)
             far = pl.multiple_of((origin + 1 - c) * share, share)
             image[:, pl.ds(near, share)] = mine[j]
@@ -356,7 +398,14 @@
         meta = Meta(meta, edges, slots)
         bases = refs[: k - 1]
         if last:
-            corrected, sums, new_state = refs[k - 1 :]
+            corrected, sums, new_state, stacked, sems = refs[2 * k - 2 :]
+            sources = list(refs[k - 1 : 2 * k - 2]) + [image]
+            copies = [
+                pltpu.make_async_copy(source, stacked.at[j], sems.at[j])
+                for j, source in enumerate(sources)
+            ]
+            for copy in copies:
+                copy.start()
         else:
             whole, xin, corrected, sums, new_state = refs[k - 1 :]
         theta = jnp.sum(thetas[...].reshape(sectors, size), axis=0, keepdims=True)
@@ -397,6 +446,8 @@
             for j in range(k + 1):
                 tail = jnp.where(line == j, total(carry[j]), tail)
             sums[...] = jnp.broadcast_to(tail[None], (sectors, EXTRA, size))
+            for copy in copies:
+                copy.wait()
         else:
             tail = jnp.zeros((EXTRA, size), F32)
             for j in range(k + 1):
@@ -407,8 +458,16 @@
     shapes = [out((slots, share, size), F32), out((EXTRA, size), F32), out((24, size), F32)]
     if last:
         shapes[1] = out((sectors, EXTRA, size), F32)
-    else:
-        shapes = [blocks, out((slots, size, size), BF)] + shapes
+        shapes.append(out((k, slots, share, size), F32))
+        return call(
+            body,
+            "correct",
+            [SMEM] + [VMEM] * (5 + 2 * k),
+            tuple(shapes),
+            [pltpu.SemaphoreType.DMA((k,))],
+            out_specs=(VMEM, VMEM, VMEM, FAR),
+        )
+    shapes = [blocks, out((slots, size, size), BF)] + shapes
     return call(body, "correct", [SMEM] + [VMEM] * (6 + k), tuple(shapes))
 
 
@@ -417,8 +476,7 @@
 
     def body(sums, vector, state, *refs):
         bases = refs[:k]
-        images = refs[k : 2 * k]
-        stacked, final, ritz = refs[2 * k :]
+        final, ritz = refs[k:]
         added = jnp.sum(sums[...], axis=0)
         project = [added[j : j + 1] for j in range(k)]
         length = added[k : k + 1]
@@ -434,21 +492,15 @@
             for j in range(k):
                 value = value - project[j] * bases[j][b]
             final[b] = value * scale
-            for j in range(k):
-                stacked[j, b] = images[j][b]
         for j in range(k):
             ritz[j] = jnp.max(state[j : j + 1])
 
     return call(
         body,
         "finish",
-        [VMEM] * (3 + 2 * k),
-        (
-            out((k, slots, share, size), F32),
-            out((slots, share, size), F32),
-            out((k,), F32),
-        ),
-        out_specs=(VMEM, VMEM, SMEM),
+        [VMEM] * (3 + k),
+        (out((slots, share, size), F32), out((k,), F32)),
+        out_specs=(VMEM, SMEM),
     )
 
 
@@ -490,6 +542,10 @@
     def over_sector(values):
         return lax.all_to_all(values, "sector", 0, 0, tiled=True)
 
+    def chip_pair(values, k):
+        pairs = [(i, 2 * ((i // 2) ^ k) + i % 2) for i in range(terms)]
+        return lax.ppermute(values, "mpo", pairs)
+
     def chip_shift(values, k):
         pairs = [(i, (i + 2 * k) % terms) for i in range(terms)]
         return lax.ppermute(values, "mpo", pairs)
@@ -497,14 +553,15 @@
     def far(values):
         return pltpu.with_memory_space_constraint(values, pltpu.HBM)
 
-    vector, xin, mine, sums, state, right_near, left_near = start_kernel(edges, slots, size, share, group)(
-        meta, far(guess), far(right_env), far(left_env)
-    )
+    vector, xin, mine, sums, state, right_near, left_near, own, send = begin_kernel(
+        edges, slots, size, share, group, chips
+    )(meta, far(guess), far(right_env), far(left_env))
     bases, images, whole_bases, ids = [], [], [], []
     for k in range(1, APPLIES + 1):
-        own, send, right_near, left_near = couple_kernel(edges, slots, size, share, group, chips)(
-            meta, xin, right_near, left_near
-        )
+        if k > 1:
+            own, send, right_near, left_near = couple_kernel(
+                edges, slots, size, share, group, chips
+            )(meta, xin, right_near, left_near)
         received = lax.ppermute(send, "mpo", core_swap)
         parts = pair_kernel(edges, size, share, chips)(own, received)
         shifted = [parts[0]] + [chip_shift(parts[j], j) for j in range(1, chips)]
@@ -516,7 +573,7 @@
         image, basis, outgoing, state = result[:4]
         if k == 1:
             ids = result[4:]
-        rows = [outgoing] + [chip_shift(outgoing, j) for j in range(1, chips)]
+        rows = [outgoing] + [chip_pair(outgoing, j) for j in range(1, chips)]
         near_rows = gather_kernel(slots, size, share, chips)(*rows)
         far_rows = lax.ppermute(near_rows, "mpo", core_swap)
         whole_image, whole_basis, parts = weigh_kernel(
@@ -526,18 +583,19 @@
         )
         thetas = over_sector(parts)
         last = k == APPLIES
+        others = [*whole_bases, *images] if last else whole_bases
         result = correct_kernel(k, edges, slots, size, share, sectors, last)(
-            meta, thetas, whole_image, whole_basis, diag_shift, image, basis, state, *whole_bases
+            meta, thetas, whole_image, whole_basis, diag_shift, image, basis, state, *others
         )
         if last:
-            mine, sums, state = result
+            mine, sums, state, stacked = result
         else:
             vector, xin, mine, sums, state = result
             whole_bases.append(whole_basis)
         bases.append(basis)
         images.append(image)
-    stacked, final, ritz = finish_kernel(slots, size, share, sectors)(
-        over_sector(sums), mine, state, *bases, *images
+    final, ritz = finish_kernel(slots, size, share, sectors)(
+        over_sector(sums), mine, state, *bases
     )
     return stacked, final, ritz
 

time: 220 us -> 219 us (level)
    ppermute x18 -> x9, starting transfers between devices: 29.3 us -> 13.3 us  [chip_shift(): return lax.ppermute(values, 'mpo', pairs)]
    ppermute x0 -> x9, starting transfers between devices: none -> 13.9 us  [chip_pair(): return lax.ppermute(values, 'mpo', pairs)]
    ppermute x0 -> x9, waiting for transfers between devices: none -> 12 us  [chip_pair(): return lax.ppermute(values, 'mpo', pairs)]
    ppermute x18 -> x9, waiting for transfers between devices: 28.7 us -> 17.3 us  [chip_shift(): return lax.ppermute(values, 'mpo', pairs)]
    pallas_call x1, Pallas kernels: 4.37 us -> 10.7 us  [per_device(): begin_kernel(edges, slots, size, share, group, chips)]
    pallas_call x3 -> x2, Pallas kernels: 16.7 us -> 11.2 us  [per_device(): couple_kernel(edges, slots, size, share, group, chips)]
  transfers between devices with their start and end apart: 24 -> 24, of which waited for: 24 -> 22; matrix products, arithmetic and copies ran while one was open for 0% -> 0% of each run, Pallas kernels for 0% -> 0%
where the time goes in v5:
time: 219 us
  blocking collectives  113 us (52%)
  waiting for transfers between devices  39.6 us (18%)
  Pallas kernels  36.5 us (17%)
  starting transfers between devices  28 us (13%)
    all_to_all x7, blocking collectives, over_sector(): return lax.all_to_all(values, 'sector', 0, 0, tiled=True)  113 us
    ppermute x9, waiting for transfers between devices, chip_shift(): return lax.ppermute(values, 'mpo', pairs)  17.3 us
    ppermute x9, starting transfers between devices, chip_pair(): return lax.ppermute(values, 'mpo', pairs)  13.9 us
    ppermute x9, starting transfers between devices, chip_shift(): return lax.ppermute(values, 'mpo', pairs)  13.3 us
    ppermute x9, waiting for transfers between devices, chip_pair(): return lax.ppermute(values, 'mpo', pairs)  12 us
    pallas_call x2, Pallas kernels, per_device(): couple_kernel(edges, slots, size, share, group, chips)  11.2 us
    pallas_call x1, Pallas kernels, per_device(): begin_kernel(edges, slots, size, share, group, chips)  10.7 us
    ppermute x3, waiting for transfers between devices, per_device(): received = lax.ppermute(send, 'mpo', core_swap)  5.69 us
  transfers between devices with their start and end apart: 24, of which 22 were waited for; matrix products, arithmetic and copies ran while one was open for 0% of the time, Pallas kernels for 0%

profile of v5, /device:TPU:4, one launch (start us, length us, event | category | flops | bytes accessed | tf_op | source)
XLA Modules:
  0.0 218.6 jit_solution(9144848545282358368)
XLA Ops:
  1.5 10.7 %begin.1 = (f32[16,128,128]{2,1,0:T(8,128)S(1)}, bf16[16,128,128]{2,1,0:T(8,128)(2,1)}, f32[16,16,128]{2,1,0:T(8,128)S(1)}, f32[8,128]{1,0:T(8,128)S(1)}, f32[24...) custom-call(s32[193]{0:T(256)S(1)} %concatenate.3.meta, ...), custom_call_target="tpu_custom_call" | custom-call | tf_op jit(solution)/shard_map/begin/pallas_call | solution.py:556
  12.3 1.9 collective-permute-done.received
  16.7 2.5 %collective-permute-start.3 = (bf16[32,16,128]{2,1,0:T(8,128)(2,1)S(1)}, bf16[32,16,128]{2,1,0:T(8,128)(2,1)S(1)}, u32[]{:S(2)}, u32[]{:S(2)}) collective-permute-start(bf16[32,16,128]{2,1,0:T(8,128)(2,1)S(1)} %get-tuple-element.73), channel_id=1, source_target_pairs={{0,6},{1,7},{2,0},{3,1},{4,2},{5,3},{6,4},{7,5},{8,14},{9,15},{10,... | collective-permute-start | bytes 393224 | tf_op jit(solution)/shard_map/ppermute | solution.py:551
  20.1 3.2 %collective-permute-done.2.third = bf16[32,16,128]{2,1,0:T(8,128)(2,1)S(1)} collective-permute-done((bf16[32,16,128]{2,1,0:T(8,128)(2,1)S(1)}, bf16[32,16,128]{2,1,0:T(8,128)(2,1)S(1)}, u32[]{:S(2)}, u32[]{:S(2)}) %collective-permute-start.2) | collective-permute-done | bytes 131104 | tf_op jit(solution)/shard_map/ppermute | solution.py:551
  25.4 24.7 %all_to_all.35.arrived = bf16[32,40,128]{2,1,0:T(8,128)(2,1)S(1)} all-to-all(bf16[32,40,128]{2,1,0:T(8,128)(2,1)S(1)} %pack.3), channel_id=1, replica_groups=mesh['sector'=32,'mpo'=8] {'sector'}, dimensions={0} | all-to-all | bytes 655360 | tf_op jit(solution)/shard_map/all_to_all | solution.py:543
  50.1 2.2 %image.3 = (f32[16,16,128]{2,1,0:T(8,128)S(1)}, f32[16,16,128]{2,1,0:T(8,128)S(1)}, bf16[16,16,128]{2,1,0:T(8,128)(2,1)S(1)}, f32[24,128]{1,0:T(8,128)S(1)}, s32[64]{0:T(128)S(1)}) custom-call(s32[193]{0:T(256)S(1)} %concatenate.3.meta, bf16[32,40,128]{2,1,0:T(8,128)(2,1)S(1)} %all_to_all.35.arrived, f32[16,16,128]{2,1,0:T(8,128)S(1)} %get-tuple-element.74.vector, ...), custom_call_target="tpu_custom_call" | custom-call | tf_op jit(solution)/shard_map/image/pallas_call | solution.py:570
  53.3 2.5 %collective-permute-start.5 = (bf16[16,16,128]{2,1,0:T(8,128)(2,1)S(1)}, bf16[16,16,128]{2,1,0:T(8,128)(2,1)S(1)}, u32[]{:S(2)}, u32[]{:S(2)}) collective-permute-start(bf16[16,16,128]{2,1,0:T(8,128)(2,1)S(1)} %get-tuple-element.76.refs_0_), channel_id=1, source_target_pairs={{0,4},{1,5},{2,6},{3,7},{4,0},{5,1},{6,2},{7,3},{8,12},{9,13},{10,... | collective-permute-start | bytes 196616 | tf_op jit(solution)/shard_map/ppermute | solution.py:547
  56.7 2.3 %collective-permute-done.5.refs_2_ = bf16[16,16,128]{2,1,0:T(8,128)(2,1)S(1)} collective-permute-done((bf16[16,16,128]{2,1,0:T(8,128)(2,1)S(1)}, bf16[16,16,128]{2,1,0:T(8,128)(2,1)S(1)}, u32[]{:S(2)}, u32[]{:S(2)}) %collective-permute-start.5) | collective-permute-done | bytes 65568 | tf_op jit(solution)/shard_map/ppermute | solution.py:547
  62.5 13.8 %all_to_all.36.thetas = f32[32,1,128]{2,1,0:T(1,128)S(1)} all-to-all(f32[32,1,128]{2,1,0:T(1,128)S(1)} %get-tuple-element.79), channel_id=1, replica_groups=mesh['sector'=32,'mpo'=8] {'sector'}, dimensions={0} | all-to-all | bytes 32768 | tf_op jit(solution)/shard_map/all_to_all | solution.py:543
  77.7 5.6 %couple.2 = (bf16[4,32,16,128]{3,2,1,0:T(8,128)(2,1)S(1)}, bf16[4,32,16,128]{3,2,1,0:T(8,128)(2,1)S(1)}, bf16[8,16,128,128]{3,2,1,0:T(8,128)(2,1)S(1)}, bf16[8,16,128,128]{3,2,1,0:T(8,128)(2,1)S(1)}) custom-call(s32[193]{0:T(256)S(1)} %concatenate.3.meta, ...), custom_call_target="tpu_custom_call", output_to_operand_aliasing={{2}: (2, {}), {3}: (3, {})} | custom-call | tf_op jit(solution)/shard_map/couple/pallas_call | solution.py:562
  83.6 1.9 collective-permute-done.8.received
  87.4 2.4 %collective-permute-start.11 = (bf16[32,16,128]{2,1,0:T(8,128)(2,1)S(1)}, bf16[32,16,128]{2,1,0:T(8,128)(2,1)S(1)}, u32[]{:S(2)}, u32[]{:S(2)}) collective-permute-start(bf16[32,16,128]{2,1,0:T(8,128)(2,1)S(1)} %get-tuple-element.93), channel_id=1, source_target_pairs={{0,6},{1,7},{2,0},{3,1},{4,2},{5,3},{6,4},{7,5},{8,14},{9,15},{10,... | collective-permute-start | bytes 393224 | tf_op jit(solution)/shard_map/ppermute | solution.py:551
  89.8 4.2 %collective-permute-done.9.second = bf16[32,16,128]{2,1,0:T(8,128)(2,1)S(1)} collective-permute-done((bf16[32,16,128]{2,1,0:T(8,128)(2,1)S(1)}, bf16[32,16,128]{2,1,0:T(8,128)(2,1)S(1)}, u32[]{:S(2)}, u32[]{:S(2)}) %collective-permute-start.9) | collective-permute-done | bytes 131104 | tf_op jit(solution)/shard_map/ppermute | solution.py:551
  94.0 1.8 collective-permute-done.11.fourth
  96.5 16.8 %all_to_all.37.arrived = bf16[32,40,128]{2,1,0:T(8,128)(2,1)S(1)} all-to-all(bf16[32,40,128]{2,1,0:T(8,128)(2,1)S(1)} %pack.4), channel_id=1, replica_groups=mesh['sector'=32,'mpo'=8] {'sector'}, dimensions={0} | all-to-all | bytes 655360 | tf_op jit(solution)/shard_map/all_to_all | solution.py:543
  114.2 2.3 %collective-permute-start.14 = (bf16[16,16,128]{2,1,0:T(8,128)(2,1)S(1)}, bf16[16,16,128]{2,1,0:T(8,128)(2,1)S(1)}, u32[]{:S(2)}, u32[]{:S(2)}) collective-permute-start(bf16[16,16,128]{2,1,0:T(8,128)(2,1)S(1)} %get-tuple-element.97.refs_0_), channel_id=1, source_target_pairs={{0,6},{1,7},{2,4},{3,5},{4,2},{5,3},{6,0},{7,1},{8,14},{9,15},{10,... | collective-permute-start | bytes 196616 | tf_op jit(solution)/shard_map/ppermute | solution.py:547
  116.6 2.5 %collective-permute-start.13 = (bf16[16,16,128]{2,1,0:T(8,128)(2,1)S(1)}, bf16[16,16,128]{2,1,0:T(8,128)(2,1)S(1)}, u32[]{:S(2)}, u32[]{:S(2)}) collective-permute-start(bf16[16,16,128]{2,1,0:T(8,128)(2,1)S(1)} %get-tuple-element.97.refs_0_), channel_id=1, source_target_pairs={{0,4},{1,5},{2,6},{3,7},{4,0},{5,1},{6,2},{7,3},{8,12},{9,13},{10,... | collective-permute-start | bytes 196616 | tf_op jit(solution)/shard_map/ppermute | solution.py:547
  119.5 2.8 %collective-permute-done.13.refs_2_ = bf16[16,16,128]{2,1,0:T(8,128)(2,1)S(1)} collective-permute-done((bf16[16,16,128]{2,1,0:T(8,128)(2,1)S(1)}, bf16[16,16,128]{2,1,0:T(8,128)(2,1)S(1)}, u32[]{:S(2)}, u32[]{:S(2)}) %collective-permute-start.13) | collective-permute-done | bytes 65568 | tf_op jit(solution)/shard_map/ppermute | solution.py:547
  126.0 13.5 %all_to_all.38.thetas = f32[32,1,128]{2,1,0:T(1,128)S(1)} all-to-all(f32[32,1,128]{2,1,0:T(1,128)S(1)} %get-tuple-element.100), channel_id=1, replica_groups=mesh['sector'=32,'mpo'=8] {'sector'}, dimensions={0} | all-to-all | bytes 32768 | tf_op jit(solution)/shard_map/all_to_all | solution.py:543
  140.9 5.6 %couple.3 = (bf16[4,32,16,128]{3,2,1,0:T(8,128)(2,1)S(1)}, bf16[4,32,16,128]{3,2,1,0:T(8,128)(2,1)S(1)}, bf16[8,16,128,128]{3,2,1,0:T(8,128)(2,1)S(1)}, bf16[8,16,128,128]{3,2,1,0:T(8,128)(2,1)S(1)}) custom-call(s32[193]{0:T(256)S(1)} %concatenate.3.meta, ...), custom_call_target="tpu_custom_call", output_to_operand_aliasing={{2}: (2, {}), {3}: (3, {})} | custom-call | tf_op jit(solution)/shard_map/couple/pallas_call | solution.py:562
  146.6 1.9 collective-permute-done.16.received
  150.4 2.4 %collective-permute-start.19 = (bf16[32,16,128]{2,1,0:T(8,128)(2,1)S(1)}, bf16[32,16,128]{2,1,0:T(8,128)(2,1)S(1)}, u32[]{:S(2)}, u32[]{:S(2)}) collective-permute-start(bf16[32,16,128]{2,1,0:T(8,128)(2,1)S(1)} %get-tuple-element.114), channel_id=1, source_target_pairs={{0,6},{1,7},{2,0},{3,1},{4,2},{5,3},{6,4},{7,5},{8,14},{9,15},{10,... | collective-permute-start | bytes 393224 | tf_op jit(solution)/shard_map/ppermute | solution.py:551
  152.8 4.2 %collective-permute-done.17.second = bf16[32,16,128]{2,1,0:T(8,128)(2,1)S(1)} collective-permute-done((bf16[32,16,128]{2,1,0:T(8,128)(2,1)S(1)}, bf16[32,16,128]{2,1,0:T(8,128)(2,1)S(1)}, u32[]{:S(2)}, u32[]{:S(2)}) %collective-permute-start.17) | collective-permute-done | bytes 131104 | tf_op jit(solution)/shard_map/ppermute | solution.py:551
  157.0 1.8 collective-permute-done.19.fourth
  159.5 16.8 %all_to_all.39.arrived = bf16[32,40,128]{2,1,0:T(8,128)(2,1)S(1)} all-to-all(bf16[32,40,128]{2,1,0:T(8,128)(2,1)S(1)} %pack.5), channel_id=1, replica_groups=mesh['sector'=32,'mpo'=8] {'sector'}, dimensions={0} | all-to-all | bytes 655360 | tf_op jit(solution)/shard_map/all_to_all | solution.py:543
  177.2 2.3 %collective-permute-start.22 = (bf16[16,16,128]{2,1,0:T(8,128)(2,1)S(1)}, bf16[16,16,128]{2,1,0:T(8,128)(2,1)S(1)}, u32[]{:S(2)}, u32[]{:S(2)}) collective-permute-start(bf16[16,16,128]{2,1,0:T(8,128)(2,1)S(1)} %get-tuple-element.117.refs_0_), channel_id=1, source_target_pairs={{0,6},{1,7},{2,4},{3,5},{4,2},{5,3},{6,0},{7,1},{8,14},{9,15},{10,... | collective-permute-start | bytes 196616 | tf_op jit(solution)/shard_map/ppermute | solution.py:547
  179.6 2.5 %collective-permute-start.21 = (bf16[16,16,128]{2,1,0:T(8,128)(2,1)S(1)}, bf16[16,16,128]{2,1,0:T(8,128)(2,1)S(1)}, u32[]{:S(2)}, u32[]{:S(2)}) collective-permute-start(bf16[16,16,128]{2,1,0:T(8,128)(2,1)S(1)} %get-tuple-element.117.refs_0_), channel_id=1, source_target_pairs={{0,4},{1,5},{2,6},{3,7},{4,0},{5,1},{6,2},{7,3},{8,12},{9,13},{10,... | collective-permute-start | bytes 196616 | tf_op jit(solution)/shard_map/ppermute | solution.py:547
  182.5 2.8 %collective-permute-done.21.refs_2_ = bf16[16,16,128]{2,1,0:T(8,128)(2,1)S(1)} collective-permute-done((bf16[16,16,128]{2,1,0:T(8,128)(2,1)S(1)}, bf16[16,16,128]{2,1,0:T(8,128)(2,1)S(1)}, u32[]{:S(2)}, u32[]{:S(2)}) %collective-permute-start.21) | collective-permute-done | bytes 65568 | tf_op jit(solution)/shard_map/ppermute | solution.py:547
  186.5 1.5 collective-permute-done.23.other
  189.1 13.5 %all_to_all.40.thetas = f32[32,1,128]{2,1,0:T(1,128)S(1)} all-to-all(f32[32,1,128]{2,1,0:T(1,128)S(1)} %get-tuple-element.120), channel_id=1, replica_groups=mesh['sector'=32,'mpo'=8] {'sector'}, dimensions={0} | all-to-all | bytes 32768 | tf_op jit(solution)/shard_map/all_to_all | solution.py:543
  202.6 1.6 correct.5
  204.2 13.5 %all_to_all.41.sums = f32[32,8,128]{2,1,0:T(8,128)S(1)} all-to-all(f32[32,8,128]{2,1,0:T(8,128)S(1)} %get-tuple-element.126), channel_id=1, replica_groups=mesh['sector'=32,'mpo'=8] {'sector'}, dimensions={0} | all-to-all | bytes 262144 | tf_op jit(solution)/shard_map/all_to_all | solution.py:543
  (48 shorter events, 29.2 us)
Async XLA Ops:
  12.2 64.2 %copy-start = (f32[16,128,128]{2,1,0:T(8,128)S(1)}, f32[16,128,128]{2,1,0:T(8,128)}, u32[]{:S(2)}) copy-start(f32[16,128,128]{2,1,0:T(8,128)} %shift.5) | copy-start | bytes 3145732
  12.2 2.0 collective-permute-start
  14.4 5.7 %collective-permute-start.1 = (bf16[32,16,128]{2,1,0:T(8,128)(2,1)S(1)}, bf16[32,16,128]{2,1,0:T(8,128)(2,1)S(1)}, u32[]{:S(2)}, u32[]{:S(2)}) collective-permute-start(bf16[32,16,128]{2,1,0:T(8,128)(2,1)S(1)} %get-tuple-element.71), channel_id=1, source_target_pairs={{0,2},{1,3},{2,4},{3,5},{4,6},{5,7},{6,0},{7,1},{8,10},{9,11},{10,... | collective-permute-start | bytes 393224 | tf_op jit(solution)/shard_map/ppermute | solution.py:551
  15.7 7.6 %collective-permute-start.2 = (bf16[32,16,128]{2,1,0:T(8,128)(2,1)S(1)}, bf16[32,16,128]{2,1,0:T(8,128)(2,1)S(1)}, u32[]{:S(2)}, u32[]{:S(2)}) collective-permute-start(bf16[32,16,128]{2,1,0:T(8,128)(2,1)S(1)} %get-tuple-element.72), channel_id=1, source_target_pairs={{0,4},{1,5},{2,6},{3,7},{4,0},{5,1},{6,2},{7,3},{8,12},{9,13},{10,... | collective-permute-start | bytes 393224 | tf_op jit(solution)/shard_map/ppermute | solution.py:551
  16.7 7.8 %collective-permute-start.3 = (bf16[32,16,128]{2,1,0:T(8,128)(2,1)S(1)}, bf16[32,16,128]{2,1,0:T(8,128)(2,1)S(1)}, u32[]{:S(2)}, u32[]{:S(2)}) collective-permute-start(bf16[32,16,128]{2,1,0:T(8,128)(2,1)S(1)} %get-tuple-element.73), channel_id=1, source_target_pairs={{0,6},{1,7},{2,0},{3,1},{4,2},{5,3},{6,4},{7,5},{8,14},{9,15},{10,... | collective-permute-start | bytes 393224 | tf_op jit(solution)/shard_map/ppermute | solution.py:551
  52.3 4.4 %collective-permute-start.6 = (bf16[16,16,128]{2,1,0:T(8,128)(2,1)S(1)}, bf16[16,16,128]{2,1,0:T(8,128)(2,1)S(1)}, u32[]{:S(2)}, u32[]{:S(2)}) collective-permute-start(bf16[16,16,128]{2,1,0:T(8,128)(2,1)S(1)} %get-tuple-element.76.refs_0_), channel_id=1, source_target_pairs={{0,6},{1,7},{2,4},{3,5},{4,2},{5,3},{6,0},{7,1},{8,14},{9,15},{10,... | collective-permute-start | bytes 196616 | tf_op jit(solution)/shard_map/ppermute | solution.py:547
  53.3 5.8 %collective-permute-start.5 = (bf16[16,16,128]{2,1,0:T(8,128)(2,1)S(1)}, bf16[16,16,128]{2,1,0:T(8,128)(2,1)S(1)}, u32[]{:S(2)}, u32[]{:S(2)}) collective-permute-start(bf16[16,16,128]{2,1,0:T(8,128)(2,1)S(1)} %get-tuple-element.76.refs_0_), channel_id=1, source_target_pairs={{0,4},{1,5},{2,6},{3,7},{4,0},{5,1},{6,2},{7,3},{8,12},{9,13},{10,... | collective-permute-start | bytes 196616 | tf_op jit(solution)/shard_map/ppermute | solution.py:547
  55.7 4.3 %collective-permute-start.4 = (bf16[16,16,128]{2,1,0:T(8,128)(2,1)S(1)}, bf16[16,16,128]{2,1,0:T(8,128)(2,1)S(1)}, u32[]{:S(2)}, u32[]{:S(2)}) collective-permute-start(bf16[16,16,128]{2,1,0:T(8,128)(2,1)S(1)} %get-tuple-element.76.refs_0_), channel_id=1, source_target_pairs={{0,2},{1,3},{2,0},{3,1},{4,6},{5,7},{6,4},{7,5},{8,10},{9,11},{10,... | collective-permute-start | bytes 196616 | tf_op jit(solution)/shard_map/ppermute | solution.py:547
  60.0 1.6 collective-permute-start.7
  83.3 2.2 collective-permute-start.8
  85.6 8.4 %collective-permute-start.9 = (bf16[32,16,128]{2,1,0:T(8,128)(2,1)S(1)}, bf16[32,16,128]{2,1,0:T(8,128)(2,1)S(1)}, u32[]{:S(2)}, u32[]{:S(2)}) collective-permute-start(bf16[32,16,128]{2,1,0:T(8,128)(2,1)S(1)} %get-tuple-element.91), channel_id=1, source_target_pairs={{0,2},{1,3},{2,4},{3,5},{4,6},{5,7},{6,0},{7,1},{8,10},{9,11},{10,... | collective-permute-start | bytes 393224 | tf_op jit(solution)/shard_map/ppermute | solution.py:551
  86.4 7.6 %collective-permute-start.10 = (bf16[32,16,128]{2,1,0:T(8,128)(2,1)S(1)}, bf16[32,16,128]{2,1,0:T(8,128)(2,1)S(1)}, u32[]{:S(2)}, u32[]{:S(2)}) collective-permute-start(bf16[32,16,128]{2,1,0:T(8,128)(2,1)S(1)} %get-tuple-element.92), channel_id=1, source_target_pairs={{0,4},{1,5},{2,6},{3,7},{4,0},{5,1},{6,2},{7,3},{8,12},{9,13},{10,... | collective-permute-start | bytes 393224 | tf_op jit(solution)/shard_map/ppermute | solution.py:551
  87.4 8.4 %collective-permute-start.11 = (bf16[32,16,128]{2,1,0:T(8,128)(2,1)S(1)}, bf16[32,16,128]{2,1,0:T(8,128)(2,1)S(1)}, u32[]{:S(2)}, u32[]{:S(2)}) collective-permute-start(bf16[32,16,128]{2,1,0:T(8,128)(2,1)S(1)} %get-tuple-element.93), channel_id=1, source_target_pairs={{0,6},{1,7},{2,0},{3,1},{4,2},{5,3},{6,4},{7,5},{8,14},{9,15},{10,... | collective-permute-start | bytes 393224 | tf_op jit(solution)/shard_map/ppermute | solution.py:551
  114.2 5.3 %collective-permute-start.14 = (bf16[16,16,128]{2,1,0:T(8,128)(2,1)S(1)}, bf16[16,16,128]{2,1,0:T(8,128)(2,1)S(1)}, u32[]{:S(2)}, u32[]{:S(2)}) collective-permute-start(bf16[16,16,128]{2,1,0:T(8,128)(2,1)S(1)} %get-tuple-element.97.refs_0_), channel_id=1, source_target_pairs={{0,6},{1,7},{2,4},{3,5},{4,2},{5,3},{6,0},{7,1},{8,14},{9,15},{10,... | collective-permute-start | bytes 196616 | tf_op jit(solution)/shard_map/ppermute | solution.py:547
  116.6 5.8 %collective-permute-start.13 = (bf16[16,16,128]{2,1,0:T(8,128)(2,1)S(1)}, bf16[16,16,128]{2,1,0:T(8,128)(2,1)S(1)}, u32[]{:S(2)}, u32[]{:S(2)}) collective-permute-start(bf16[16,16,128]{2,1,0:T(8,128)(2,1)S(1)} %get-tuple-element.97.refs_0_), channel_id=1, source_target_pairs={{0,4},{1,5},{2,6},{3,7},{4,0},{5,1},{6,2},{7,3},{8,12},{9,13},{10,... | collective-permute-start | bytes 196616 | tf_op jit(solution)/shard_map/ppermute | solution.py:547
  119.1 4.3 %collective-permute-start.12 = (bf16[16,16,128]{2,1,0:T(8,128)(2,1)S(1)}, bf16[16,16,128]{2,1,0:T(8,128)(2,1)S(1)}, u32[]{:S(2)}, u32[]{:S(2)}) collective-permute-start(bf16[16,16,128]{2,1,0:T(8,128)(2,1)S(1)} %get-tuple-element.97.refs_0_), channel_id=1, source_target_pairs={{0,2},{1,3},{2,0},{3,1},{4,6},{5,7},{6,4},{7,5},{8,10},{9,11},{10,... | collective-permute-start | bytes 196616 | tf_op jit(solution)/shard_map/ppermute | solution.py:547
  123.4 1.6 collective-permute-start.15
  146.5 2.0 collective-permute-start.16
  148.6 8.4 %collective-permute-start.17 = (bf16[32,16,128]{2,1,0:T(8,128)(2,1)S(1)}, bf16[32,16,128]{2,1,0:T(8,128)(2,1)S(1)}, u32[]{:S(2)}, u32[]{:S(2)}) collective-permute-start(bf16[32,16,128]{2,1,0:T(8,128)(2,1)S(1)} %get-tuple-element.112), channel_id=1, source_target_pairs={{0,2},{1,3},{2,4},{3,5},{4,6},{5,7},{6,0},{7,1},{8,10},{9,11},{10,... | collective-permute-start | bytes 393224 | tf_op jit(solution)/shard_map/ppermute | solution.py:551
  149.4 7.6 %collective-permute-start.18 = (bf16[32,16,128]{2,1,0:T(8,128)(2,1)S(1)}, bf16[32,16,128]{2,1,0:T(8,128)(2,1)S(1)}, u32[]{:S(2)}, u32[]{:S(2)}) collective-permute-start(bf16[32,16,128]{2,1,0:T(8,128)(2,1)S(1)} %get-tuple-element.113), channel_id=1, source_target_pairs={{0,4},{1,5},{2,6},{3,7},{4,0},{5,1},{6,2},{7,3},{8,12},{9,13},{10,... | collective-permute-start | bytes 393224 | tf_op jit(solution)/shard_map/ppermute | solution.py:551
  150.4 8.4 %collective-permute-start.19 = (bf16[32,16,128]{2,1,0:T(8,128)(2,1)S(1)}, bf16[32,16,128]{2,1,0:T(8,128)(2,1)S(1)}, u32[]{:S(2)}, u32[]{:S(2)}) collective-permute-start(bf16[32,16,128]{2,1,0:T(8,128)(2,1)S(1)} %get-tuple-element.114), channel_id=1, source_target_pairs={{0,6},{1,7},{2,0},{3,1},{4,2},{5,3},{6,4},{7,5},{8,14},{9,15},{10,... | collective-permute-start | bytes 393224 | tf_op jit(solution)/shard_map/ppermute | solution.py:551
  177.2 5.3 %collective-permute-start.22 = (bf16[16,16,128]{2,1,0:T(8,128)(2,1)S(1)}, bf16[16,16,128]{2,1,0:T(8,128)(2,1)S(1)}, u32[]{:S(2)}, u32[]{:S(2)}) collective-permute-start(bf16[16,16,128]{2,1,0:T(8,128)(2,1)S(1)} %get-tuple-element.117.refs_0_), channel_id=1, source_target_pairs={{0,6},{1,7},{2,4},{3,5},{4,2},{5,3},{6,0},{7,1},{8,14},{9,15},{10,... | collective-permute-start | bytes 196616 | tf_op jit(solution)/shard_map/ppermute | solution.py:547
  179.6 5.8 %collective-permute-start.21 = (bf16[16,16,128]{2,1,0:T(8,128)(2,1)S(1)}, bf16[16,16,128]{2,1,0:T(8,128)(2,1)S(1)}, u32[]{:S(2)}, u32[]{:S(2)}) collective-permute-start(bf16[16,16,128]{2,1,0:T(8,128)(2,1)S(1)} %get-tuple-element.117.refs_0_), channel_id=1, source_target_pairs={{0,4},{1,5},{2,6},{3,7},{4,0},{5,1},{6,2},{7,3},{8,12},{9,13},{10,... | collective-permute-start | bytes 196616 | tf_op jit(solution)/shard_map/ppermute | solution.py:547
  182.1 4.3 %collective-permute-start.20 = (bf16[16,16,128]{2,1,0:T(8,128)(2,1)S(1)}, bf16[16,16,128]{2,1,0:T(8,128)(2,1)S(1)}, u32[]{:S(2)}, u32[]{:S(2)}) collective-permute-start(bf16[16,16,128]{2,1,0:T(8,128)(2,1)S(1)} %get-tuple-element.117.refs_0_), channel_id=1, source_target_pairs={{0,2},{1,3},{2,0},{3,1},{4,6},{5,7},{6,4},{7,5},{8,10},{9,11},{10,... | collective-permute-start | bytes 196616 | tf_op jit(solution)/shard_map/ppermute | solution.py:547
  186.4 1.6 collective-permute-start.23

commit v6 on v5

--- a/solution.py
+++ b/solution.py
@@ -111,26 +111,21 @@
     lax.fori_loop(0, edges // UNROLL, step, 0)
 
 
-def begin_kernel(edges, slots, size, share, group, chips):
+def start_kernel(edges, slots, size, share, group):
     terms = group // PIECES
 
     def body(meta, far_guess, right, left, *refs):
         meta = Meta(meta, edges, slots)
-        vector, xin, mine, sums, state, right_near, left_near, own, send = refs[:9]
-        guess, acc, tmp, sems, guess_sem = refs[9:]
+        vector, xin, mine, sums, state, right_near, left_near, guess, sems, guess_sem = refs
         first = pltpu.make_async_copy(far_guess, guess, guess_sem)
         first.start()
         copies = []
-        for p in range(PIECES):
-            part = pl.ds(p * terms, terms)
-            copies.append(
-                [
-                    pltpu.make_async_copy(far.at[part], near.at[part], sems.at[i, p])
-                    for i, (far, near) in enumerate(((right, right_near), (left, left_near)))
-                ]
-            )
-            for copy in copies[p]:
-                copy.start()
+        for i, (far, near) in enumerate(((right, right_near), (left, left_near))):
+            for p in range(PIECES):
+                part = pl.ds(p * terms, terms)
+                copies.append(pltpu.make_async_copy(far.at[part], near.at[part], sems.at[i, p]))
+        for copy in copies:
+            copy.start()
         state[...] = jnp.zeros_like(state)
         first_row = pl.multiple_of(meta.place() * share, share)
         first.wait()
@@ -145,31 +140,13 @@
 
         squares = lax.fori_loop(0, slots, block, jnp.zeros((8, size), F32), unroll=4)
         sums[...] = three_parts(total(squares), 0, EXTRA)
-        half = PIECES // 2
-        for p in range(half):
-            for copy in copies[p]:
-                copy.wait()
-
-        def early(e, u):
-            acc[e] = add_terms(meta, xin, right_near, left_near, e, range(group // 2), None)
-
-        unrolled(edges, early)
-        for p in range(half, PIECES):
-            for copy in copies[p]:
-                copy.wait()
-
-        def late(e, u):
-            rest = range(group // 2, group)
-            value = add_terms(meta, xin, right_near, left_near, e, rest, acc[e])
-            couple_rows(meta, chips, share, own, send, tmp, e, u, value)
-
-        unrolled(edges, late)
+        for copy in copies:
+            copy.wait()
 
     near = pltpu.VMEM((group, slots, size, size), BF)
-    shape = out((chips, edges, share, size), BF)
-    return call(
-        body,
-        "begin",
+    return call(
+        body,
+        "start",
         [SMEM, FAR, FAR, FAR],
         (
             out((slots, size, size), F32),
@@ -179,13 +156,9 @@
             out((24, size), F32),
             near,
             near,
-            shape,
-            shape,
         ),
         [
             pltpu.VMEM((slots, size, size), F32),
-            pltpu.VMEM((edges, size, size), F32),
-            pltpu.VMEM((UNROLL, size, size), BF),
             pltpu.SemaphoreType.DMA((2, PIECES)),
             pltpu.SemaphoreType.DMA,
         ],
@@ -268,10 +241,9 @@
         images = refs[k - 1 : 2 * k - 2]
         if k == 1:
             image, basis, message, new_state, ids, acc, slot_lanes, wide_ids = refs
-            line = lax.broadcasted_iota(jnp.int32, (EXTRA, size), 0)
             for s in range(sectors):
                 tail = arrived[s, CAP * share :].astype(F32)
-                slot = jnp.sum(jnp.where(line == ID_ROW, tail, 0.0), axis=0, keepdims=True)
+                slot = tail[ID_ROW : ID_ROW + 1]
                 slot = jnp.where(slot < 0.0, float(slots), slot)
                 slot_lanes[s : s + 1] = slot.astype(jnp.int32)
             pltpu.sync_copy(slot_lanes, wide_ids)
@@ -553,15 +525,14 @@
     def far(values):
         return pltpu.with_memory_space_constraint(values, pltpu.HBM)
 
-    vector, xin, mine, sums, state, right_near, left_near, own, send = begin_kernel(
-        edges, slots, size, share, group, chips
+    vector, xin, mine, sums, state, right_near, left_near = start_kernel(
+        edges, slots, size, share, group
     )(meta, far(guess), far(right_env), far(left_env))
     bases, images, whole_bases, ids = [], [], [], []
     for k in range(1, APPLIES + 1):
-        if k > 1:
-            own, send, right_near, left_near = couple_kernel(
-                edges, slots, size, share, group, chips
-            )(meta, xin, right_near, left_near)
+        own, send, right_near, left_near = couple_kernel(edges, slots, size, share, group, chips)(
+            meta, xin, right_near, left_near
+        )
         received = lax.ppermute(send, "mpo", core_swap)
         parts = pair_kernel(edges, size, share, chips)(own, received)
         shifted = [parts[0]] + [chip_shift(parts[j], j) for j in range(1, chips)]

time: 219 us -> 218 us (level)
    pallas_call x1, Pallas kernels: 10.7 us -> 4.39 us  [per_device(): start_kernel(edges, slots, size, share, group)]
    pallas_call x2 -> x3, Pallas kernels: 11.2 us -> 16.7 us  [per_device(): couple_kernel(edges, slots, size, share, group, chips)]
where the time goes in v6:
time: 218 us
  blocking collectives  113 us (52%)
  waiting for transfers between devices  39.5 us (18%)
  Pallas kernels  35.7 us (16%)
  starting transfers between devices  28 us (13%)
    all_to_all x7, blocking collectives, over_sector(): return lax.all_to_all(values, 'sector', 0, 0, tiled=True)  113 us
    ppermute x9, waiting for transfers between devices, chip_shift(): return lax.ppermute(values, 'mpo', pairs)  17.3 us
    pallas_call x3, Pallas kernels, per_device(): couple_kernel(edges, slots, size, share, group, chips)  16.7 us
    ppermute x9, starting transfers between devices, chip_pair(): return lax.ppermute(values, 'mpo', pairs)  13.9 us
    ppermute x9, starting transfers between devices, chip_shift(): return lax.ppermute(values, 'mpo', pairs)  13.3 us
    ppermute x9, waiting for transfers between devices, chip_pair(): return lax.ppermute(values, 'mpo', pairs)  12 us
    ppermute x3, waiting for transfers between devices, per_device(): received = lax.ppermute(send, 'mpo', core_swap)  5.69 us
    ppermute x3, waiting for transfers between devices, per_device(): far_rows = lax.ppermute(near_rows, 'mpo', core_swap)  4.57 us
  transfers between devices with their start and end apart: 24, of which 22 were waited for; matrix products, arithmetic and copies ran while one was open for 0% of the time, Pallas kernels for 0%

profile of v6, /device:TPU:4, one launch (start us, length us, event | category | flops | bytes accessed | tf_op | source)
XLA Modules:
  0.0 217.8 jit_solution(8142561420559481367)
XLA Ops:
  1.5 4.4 %start.1 = (f32[16,128,128]{2,1,0:T(8,128)S(1)}, bf16[16,128,128]{2,1,0:T(8,128)(2,1)S(1)}, f32[16,16,128]{2,1,0:T(8,128)S(1)}, f32[8,128]{1,0:T(8,128)S(1)}, f3...) custom-call(s32[193]{0:T(256)S(1)} %concatenate.3.meta, ...), custom_call_target="tpu_custom_call" | custom-call | tf_op jit(solution)/shard_map/start/pallas_call | solution.py:528
  5.9 5.6 %couple.3 = (bf16[4,32,16,128]{3,2,1,0:T(8,128)(2,1)S(1)}, bf16[4,32,16,128]{3,2,1,0:T(8,128)(2,1)S(1)}, bf16[8,16,128,128]{3,2,1,0:T(8,128)(2,1)S(1)}, bf16[8,16,128,128]{3,2,1,0:T(8,128)(2,1)S(1)}) custom-call(s32[193]{0:T(256)S(1)} %concatenate.3.meta, ...), custom_call_target="tpu_custom_call", output_to_operand_aliasing={{2}: (2, {}), {3}: (3, {})} | custom-call | tf_op jit(solution)/shard_map/couple/pallas_call | solution.py:533
  11.5 1.9 collective-permute-done.received
  15.9 2.5 %collective-permute-start.3 = (bf16[32,16,128]{2,1,0:T(8,128)(2,1)S(1)}, bf16[32,16,128]{2,1,0:T(8,128)(2,1)S(1)}, u32[]{:S(2)}, u32[]{:S(2)}) collective-permute-start(bf16[32,16,128]{2,1,0:T(8,128)(2,1)S(1)} %get-tuple-element.79), channel_id=1, source_target_pairs={{0,6},{1,7},{2,0},{3,1},{4,2},{5,3},{6,4},{7,5},{8,14},{9,15},{10,... | collective-permute-start | bytes 393224 | tf_op jit(solution)/shard_map/ppermute | solution.py:523
  19.3 3.2 %collective-permute-done.2.third = bf16[32,16,128]{2,1,0:T(8,128)(2,1)S(1)} collective-permute-done((bf16[32,16,128]{2,1,0:T(8,128)(2,1)S(1)}, bf16[32,16,128]{2,1,0:T(8,128)(2,1)S(1)}, u32[]{:S(2)}, u32[]{:S(2)}) %collective-permute-start.2) | collective-permute-done | bytes 131104 | tf_op jit(solution)/shard_map/ppermute | solution.py:523
  24.6 24.7 %all_to_all.35.arrived = bf16[32,40,128]{2,1,0:T(8,128)(2,1)S(1)} all-to-all(bf16[32,40,128]{2,1,0:T(8,128)(2,1)S(1)} %pack.3), channel_id=1, replica_groups=mesh['sector'=32,'mpo'=8] {'sector'}, dimensions={0} | all-to-all | bytes 655360 | tf_op jit(solution)/shard_map/all_to_all | solution.py:515
  49.3 2.2 %image.3 = (f32[16,16,128]{2,1,0:T(8,128)S(1)}, f32[16,16,128]{2,1,0:T(8,128)S(1)}, bf16[16,16,128]{2,1,0:T(8,128)(2,1)S(1)}, f32[24,128]{1,0:T(8,128)S(1)}, s32[64]{0:T(128)S(1)}) custom-call(s32[193]{0:T(256)S(1)} %concatenate.3.meta, bf16[32,40,128]{2,1,0:T(8,128)(2,1)S(1)} %all_to_all.35.arrived, f32[16,16,128]{2,1,0:T(8,128)S(1)} %get-tuple-element.80.vector, ...), custom_call_target="tpu_custom_call" | custom-call | tf_op jit(solution)/shard_map/image/pallas_call | solution.py:541
  52.4 2.5 %collective-permute-start.5 = (bf16[16,16,128]{2,1,0:T(8,128)(2,1)S(1)}, bf16[16,16,128]{2,1,0:T(8,128)(2,1)S(1)}, u32[]{:S(2)}, u32[]{:S(2)}) collective-permute-start(bf16[16,16,128]{2,1,0:T(8,128)(2,1)S(1)} %get-tuple-element.82.refs_0_), channel_id=1, source_target_pairs={{0,4},{1,5},{2,6},{3,7},{4,0},{5,1},{6,2},{7,3},{8,12},{9,13},{10,... | collective-permute-start | bytes 196616 | tf_op jit(solution)/shard_map/ppermute | solution.py:519
  55.9 2.3 %collective-permute-done.5.refs_2_ = bf16[16,16,128]{2,1,0:T(8,128)(2,1)S(1)} collective-permute-done((bf16[16,16,128]{2,1,0:T(8,128)(2,1)S(1)}, bf16[16,16,128]{2,1,0:T(8,128)(2,1)S(1)}, u32[]{:S(2)}, u32[]{:S(2)}) %collective-permute-start.5) | collective-permute-done | bytes 65568 | tf_op jit(solution)/shard_map/ppermute | solution.py:519
  61.7 13.8 %all_to_all.36.thetas = f32[32,1,128]{2,1,0:T(1,128)S(1)} all-to-all(f32[32,1,128]{2,1,0:T(1,128)S(1)} %get-tuple-element.85), channel_id=1, replica_groups=mesh['sector'=32,'mpo'=8] {'sector'}, dimensions={0} | all-to-all | bytes 32768 | tf_op jit(solution)/shard_map/all_to_all | solution.py:515
  76.8 5.6 %couple.4 = (bf16[4,32,16,128]{3,2,1,0:T(8,128)(2,1)S(1)}, bf16[4,32,16,128]{3,2,1,0:T(8,128)(2,1)S(1)}, bf16[8,16,128,128]{3,2,1,0:T(8,128)(2,1)S(1)}, bf16[8,16,128,128]{3,2,1,0:T(8,128)(2,1)S(1)}) custom-call(s32[193]{0:T(256)S(1)} %concatenate.3.meta, ...), custom_call_target="tpu_custom_call", output_to_operand_aliasing={{2}: (2, {}), {3}: (3, {})} | custom-call | tf_op jit(solution)/shard_map/couple/pallas_call | solution.py:533
  82.7 1.9 collective-permute-done.8.received
  86.5 2.4 %collective-permute-start.11 = (bf16[32,16,128]{2,1,0:T(8,128)(2,1)S(1)}, bf16[32,16,128]{2,1,0:T(8,128)(2,1)S(1)}, u32[]{:S(2)}, u32[]{:S(2)}) collective-permute-start(bf16[32,16,128]{2,1,0:T(8,128)(2,1)S(1)} %get-tuple-element.99), channel_id=1, source_target_pairs={{0,6},{1,7},{2,0},{3,1},{4,2},{5,3},{6,4},{7,5},{8,14},{9,15},{10,... | collective-permute-start | bytes 393224 | tf_op jit(solution)/shard_map/ppermute | solution.py:523
  88.9 4.2 %collective-permute-done.9.second = bf16[32,16,128]{2,1,0:T(8,128)(2,1)S(1)} collective-permute-done((bf16[32,16,128]{2,1,0:T(8,128)(2,1)S(1)}, bf16[32,16,128]{2,1,0:T(8,128)(2,1)S(1)}, u32[]{:S(2)}, u32[]{:S(2)}) %collective-permute-start.9) | collective-permute-done | bytes 131104 | tf_op jit(solution)/shard_map/ppermute | solution.py:523
  93.2 1.8 collective-permute-done.11.fourth
  95.7 16.8 %all_to_all.37.arrived = bf16[32,40,128]{2,1,0:T(8,128)(2,1)S(1)} all-to-all(bf16[32,40,128]{2,1,0:T(8,128)(2,1)S(1)} %pack.4), channel_id=1, replica_groups=mesh['sector'=32,'mpo'=8] {'sector'}, dimensions={0} | all-to-all | bytes 655360 | tf_op jit(solution)/shard_map/all_to_all | solution.py:515
  113.4 2.3 %collective-permute-start.14 = (bf16[16,16,128]{2,1,0:T(8,128)(2,1)S(1)}, bf16[16,16,128]{2,1,0:T(8,128)(2,1)S(1)}, u32[]{:S(2)}, u32[]{:S(2)}) collective-permute-start(bf16[16,16,128]{2,1,0:T(8,128)(2,1)S(1)} %get-tuple-element.103.refs_0_), channel_id=1, source_target_pairs={{0,6},{1,7},{2,4},{3,5},{4,2},{5,3},{6,0},{7,1},{8,14},{9,15},{10,... | collective-permute-start | bytes 196616 | tf_op jit(solution)/shard_map/ppermute | solution.py:519
  115.7 2.5 %collective-permute-start.13 = (bf16[16,16,128]{2,1,0:T(8,128)(2,1)S(1)}, bf16[16,16,128]{2,1,0:T(8,128)(2,1)S(1)}, u32[]{:S(2)}, u32[]{:S(2)}) collective-permute-start(bf16[16,16,128]{2,1,0:T(8,128)(2,1)S(1)} %get-tuple-element.103.refs_0_), channel_id=1, source_target_pairs={{0,4},{1,5},{2,6},{3,7},{4,0},{5,1},{6,2},{7,3},{8,12},{9,13},{10,... | collective-permute-start | bytes 196616 | tf_op jit(solution)/shard_map/ppermute | solution.py:519
  118.7 2.8 %collective-permute-done.13.refs_2_ = bf16[16,16,128]{2,1,0:T(8,128)(2,1)S(1)} collective-permute-done((bf16[16,16,128]{2,1,0:T(8,128)(2,1)S(1)}, bf16[16,16,128]{2,1,0:T(8,128)(2,1)S(1)}, u32[]{:S(2)}, u32[]{:S(2)}) %collective-permute-start.13) | collective-permute-done | bytes 65568 | tf_op jit(solution)/shard_map/ppermute | solution.py:519
  125.1 13.5 %all_to_all.38.thetas = f32[32,1,128]{2,1,0:T(1,128)S(1)} all-to-all(f32[32,1,128]{2,1,0:T(1,128)S(1)} %get-tuple-element.106), channel_id=1, replica_groups=mesh['sector'=32,'mpo'=8] {'sector'}, dimensions={0} | all-to-all | bytes 32768 | tf_op jit(solution)/shard_map/all_to_all | solution.py:515
  140.0 5.6 %couple.5 = (bf16[4,32,16,128]{3,2,1,0:T(8,128)(2,1)S(1)}, bf16[4,32,16,128]{3,2,1,0:T(8,128)(2,1)S(1)}, bf16[8,16,128,128]{3,2,1,0:T(8,128)(2,1)S(1)}, bf16[8,16,128,128]{3,2,1,0:T(8,128)(2,1)S(1)}) custom-call(s32[193]{0:T(256)S(1)} %concatenate.3.meta, ...), custom_call_target="tpu_custom_call", output_to_operand_aliasing={{2}: (2, {}), {3}: (3, {})} | custom-call | tf_op jit(solution)/shard_map/couple/pallas_call | solution.py:533
  145.7 1.9 collective-permute-done.16.received
  149.5 2.4 %collective-permute-start.19 = (bf16[32,16,128]{2,1,0:T(8,128)(2,1)S(1)}, bf16[32,16,128]{2,1,0:T(8,128)(2,1)S(1)}, u32[]{:S(2)}, u32[]{:S(2)}) collective-permute-start(bf16[32,16,128]{2,1,0:T(8,128)(2,1)S(1)} %get-tuple-element.120), channel_id=1, source_target_pairs={{0,6},{1,7},{2,0},{3,1},{4,2},{5,3},{6,4},{7,5},{8,14},{9,15},{10,... | collective-permute-start | bytes 393224 | tf_op jit(solution)/shard_map/ppermute | solution.py:523
  151.9 4.2 %collective-permute-done.17.second = bf16[32,16,128]{2,1,0:T(8,128)(2,1)S(1)} collective-permute-done((bf16[32,16,128]{2,1,0:T(8,128)(2,1)S(1)}, bf16[32,16,128]{2,1,0:T(8,128)(2,1)S(1)}, u32[]{:S(2)}, u32[]{:S(2)}) %collective-permute-start.17) | collective-permute-done | bytes 131104 | tf_op jit(solution)/shard_map/ppermute | solution.py:523
  156.2 1.8 collective-permute-done.19.fourth
  158.7 16.8 %all_to_all.39.arrived = bf16[32,40,128]{2,1,0:T(8,128)(2,1)S(1)} all-to-all(bf16[32,40,128]{2,1,0:T(8,128)(2,1)S(1)} %pack.5), channel_id=1, replica_groups=mesh['sector'=32,'mpo'=8] {'sector'}, dimensions={0} | all-to-all | bytes 655360 | tf_op jit(solution)/shard_map/all_to_all | solution.py:515
  176.4 2.3 %collective-permute-start.22 = (bf16[16,16,128]{2,1,0:T(8,128)(2,1)S(1)}, bf16[16,16,128]{2,1,0:T(8,128)(2,1)S(1)}, u32[]{:S(2)}, u32[]{:S(2)}) collective-permute-start(bf16[16,16,128]{2,1,0:T(8,128)(2,1)S(1)} %get-tuple-element.123.refs_0_), channel_id=1, source_target_pairs={{0,6},{1,7},{2,4},{3,5},{4,2},{5,3},{6,0},{7,1},{8,14},{9,15},{10,... | collective-permute-start | bytes 196616 | tf_op jit(solution)/shard_map/ppermute | solution.py:519
  178.8 2.5 %collective-permute-start.21 = (bf16[16,16,128]{2,1,0:T(8,128)(2,1)S(1)}, bf16[16,16,128]{2,1,0:T(8,128)(2,1)S(1)}, u32[]{:S(2)}, u32[]{:S(2)}) collective-permute-start(bf16[16,16,128]{2,1,0:T(8,128)(2,1)S(1)} %get-tuple-element.123.refs_0_), channel_id=1, source_target_pairs={{0,4},{1,5},{2,6},{3,7},{4,0},{5,1},{6,2},{7,3},{8,12},{9,13},{10,... | collective-permute-start | bytes 196616 | tf_op jit(solution)/shard_map/ppermute | solution.py:519
  181.7 2.8 %collective-permute-done.21.refs_2_ = bf16[16,16,128]{2,1,0:T(8,128)(2,1)S(1)} collective-permute-done((bf16[16,16,128]{2,1,0:T(8,128)(2,1)S(1)}, bf16[16,16,128]{2,1,0:T(8,128)(2,1)S(1)}, u32[]{:S(2)}, u32[]{:S(2)}) %collective-permute-start.21) | collective-permute-done | bytes 65568 | tf_op jit(solution)/shard_map/ppermute | solution.py:519
  188.3 13.5 %all_to_all.40.thetas = f32[32,1,128]{2,1,0:T(1,128)S(1)} all-to-all(f32[32,1,128]{2,1,0:T(1,128)S(1)} %get-tuple-element.126), channel_id=1, replica_groups=mesh['sector'=32,'mpo'=8] {'sector'}, dimensions={0} | all-to-all | bytes 32768 | tf_op jit(solution)/shard_map/all_to_all | solution.py:515
  201.8 1.6 correct.5
  203.4 13.5 %all_to_all.41.sums = f32[32,8,128]{2,1,0:T(8,128)S(1)} all-to-all(f32[32,8,128]{2,1,0:T(8,128)S(1)} %get-tuple-element.132), channel_id=1, replica_groups=mesh['sector'=32,'mpo'=8] {'sector'}, dimensions={0} | all-to-all | bytes 262144 | tf_op jit(solution)/shard_map/all_to_all | solution.py:515
  (49 shorter events, 30.8 us)
Async XLA Ops:
  11.4 64.1 %copy-start = (f32[16,128,128]{2,1,0:T(8,128)S(1)}, f32[16,128,128]{2,1,0:T(8,128)}, u32[]{:S(2)}) copy-start(f32[16,128,128]{2,1,0:T(8,128)} %shift.5) | copy-start | bytes 3145732
  11.4 2.0 collective-permute-start
  13.6 5.7 %collective-permute-start.1 = (bf16[32,16,128]{2,1,0:T(8,128)(2,1)S(1)}, bf16[32,16,128]{2,1,0:T(8,128)(2,1)S(1)}, u32[]{:S(2)}, u32[]{:S(2)}) collective-permute-start(bf16[32,16,128]{2,1,0:T(8,128)(2,1)S(1)} %get-tuple-element.77), channel_id=1, source_target_pairs={{0,2},{1,3},{2,4},{3,5},{4,6},{5,7},{6,0},{7,1},{8,10},{9,11},{10,... | collective-permute-start | bytes 393224 | tf_op jit(solution)/shard_map/ppermute | solution.py:523
  14.9 7.6 %collective-permute-start.2 = (bf16[32,16,128]{2,1,0:T(8,128)(2,1)S(1)}, bf16[32,16,128]{2,1,0:T(8,128)(2,1)S(1)}, u32[]{:S(2)}, u32[]{:S(2)}) collective-permute-start(bf16[32,16,128]{2,1,0:T(8,128)(2,1)S(1)} %get-tuple-element.78), channel_id=1, source_target_pairs={{0,4},{1,5},{2,6},{3,7},{4,0},{5,1},{6,2},{7,3},{8,12},{9,13},{10,... | collective-permute-start | bytes 393224 | tf_op jit(solution)/shard_map/ppermute | solution.py:523
  15.9 7.8 %collective-permute-start.3 = (bf16[32,16,128]{2,1,0:T(8,128)(2,1)S(1)}, bf16[32,16,128]{2,1,0:T(8,128)(2,1)S(1)}, u32[]{:S(2)}, u32[]{:S(2)}) collective-permute-start(bf16[32,16,128]{2,1,0:T(8,128)(2,1)S(1)} %get-tuple-element.79), channel_id=1, source_target_pairs={{0,6},{1,7},{2,0},{3,1},{4,2},{5,3},{6,4},{7,5},{8,14},{9,15},{10,... | collective-permute-start | bytes 393224 | tf_op jit(solution)/shard_map/ppermute | solution.py:523
  51.5 4.4 %collective-permute-start.6 = (bf16[16,16,128]{2,1,0:T(8,128)(2,1)S(1)}, bf16[16,16,128]{2,1,0:T(8,128)(2,1)S(1)}, u32[]{:S(2)}, u32[]{:S(2)}) collective-permute-start(bf16[16,16,128]{2,1,0:T(8,128)(2,1)S(1)} %get-tuple-element.82.refs_0_), channel_id=1, source_target_pairs={{0,6},{1,7},{2,4},{3,5},{4,2},{5,3},{6,0},{7,1},{8,14},{9,15},{10,... | collective-permute-start | bytes 196616 | tf_op jit(solution)/shard_map/ppermute | solution.py:519
  52.4 5.8 %collective-permute-start.5 = (bf16[16,16,128]{2,1,0:T(8,128)(2,1)S(1)}, bf16[16,16,128]{2,1,0:T(8,128)(2,1)S(1)}, u32[]{:S(2)}, u32[]{:S(2)}) collective-permute-start(bf16[16,16,128]{2,1,0:T(8,128)(2,1)S(1)} %get-tuple-element.82.refs_0_), channel_id=1, source_target_pairs={{0,4},{1,5},{2,6},{3,7},{4,0},{5,1},{6,2},{7,3},{8,12},{9,13},{10,... | collective-permute-start | bytes 196616 | tf_op jit(solution)/shard_map/ppermute | solution.py:519
  54.9 4.3 %collective-permute-start.4 = (bf16[16,16,128]{2,1,0:T(8,128)(2,1)S(1)}, bf16[16,16,128]{2,1,0:T(8,128)(2,1)S(1)}, u32[]{:S(2)}, u32[]{:S(2)}) collective-permute-start(bf16[16,16,128]{2,1,0:T(8,128)(2,1)S(1)} %get-tuple-element.82.refs_0_), channel_id=1, source_target_pairs={{0,2},{1,3},{2,0},{3,1},{4,6},{5,7},{6,4},{7,5},{8,10},{9,11},{10,... | collective-permute-start | bytes 196616 | tf_op jit(solution)/shard_map/ppermute | solution.py:519
  59.2 1.6 collective-permute-start.7
  82.4 2.2 collective-permute-start.8
  84.7 8.4 %collective-permute-start.9 = (bf16[32,16,128]{2,1,0:T(8,128)(2,1)S(1)}, bf16[32,16,128]{2,1,0:T(8,128)(2,1)S(1)}, u32[]{:S(2)}, u32[]{:S(2)}) collective-permute-start(bf16[32,16,128]{2,1,0:T(8,128)(2,1)S(1)} %get-tuple-element.97), channel_id=1, source_target_pairs={{0,2},{1,3},{2,4},{3,5},{4,6},{5,7},{6,0},{7,1},{8,10},{9,11},{10,... | collective-permute-start | bytes 393224 | tf_op jit(solution)/shard_map/ppermute | solution.py:523
  85.5 7.6 %collective-permute-start.10 = (bf16[32,16,128]{2,1,0:T(8,128)(2,1)S(1)}, bf16[32,16,128]{2,1,0:T(8,128)(2,1)S(1)}, u32[]{:S(2)}, u32[]{:S(2)}) collective-permute-start(bf16[32,16,128]{2,1,0:T(8,128)(2,1)S(1)} %get-tuple-element.98), channel_id=1, source_target_pairs={{0,4},{1,5},{2,6},{3,7},{4,0},{5,1},{6,2},{7,3},{8,12},{9,13},{10,... | collective-permute-start | bytes 393224 | tf_op jit(solution)/shard_map/ppermute | solution.py:523
  86.5 8.4 %collective-permute-start.11 = (bf16[32,16,128]{2,1,0:T(8,128)(2,1)S(1)}, bf16[32,16,128]{2,1,0:T(8,128)(2,1)S(1)}, u32[]{:S(2)}, u32[]{:S(2)}) collective-permute-start(bf16[32,16,128]{2,1,0:T(8,128)(2,1)S(1)} %get-tuple-element.99), channel_id=1, source_target_pairs={{0,6},{1,7},{2,0},{3,1},{4,2},{5,3},{6,4},{7,5},{8,14},{9,15},{10,... | collective-permute-start | bytes 393224 | tf_op jit(solution)/shard_map/ppermute | solution.py:523
  113.4 5.3 %collective-permute-start.14 = (bf16[16,16,128]{2,1,0:T(8,128)(2,1)S(1)}, bf16[16,16,128]{2,1,0:T(8,128)(2,1)S(1)}, u32[]{:S(2)}, u32[]{:S(2)}) collective-permute-start(bf16[16,16,128]{2,1,0:T(8,128)(2,1)S(1)} %get-tuple-element.103.refs_0_), channel_id=1, source_target_pairs={{0,6},{1,7},{2,4},{3,5},{4,2},{5,3},{6,0},{7,1},{8,14},{9,15},{10,... | collective-permute-start | bytes 196616 | tf_op jit(solution)/shard_map/ppermute | solution.py:519
  115.7 5.8 %collective-permute-start.13 = (bf16[16,16,128]{2,1,0:T(8,128)(2,1)S(1)}, bf16[16,16,128]{2,1,0:T(8,128)(2,1)S(1)}, u32[]{:S(2)}, u32[]{:S(2)}) collective-permute-start(bf16[16,16,128]{2,1,0:T(8,128)(2,1)S(1)} %get-tuple-element.103.refs_0_), channel_id=1, source_target_pairs={{0,4},{1,5},{2,6},{3,7},{4,0},{5,1},{6,2},{7,3},{8,12},{9,13},{10,... | collective-permute-start | bytes 196616 | tf_op jit(solution)/shard_map/ppermute | solution.py:519
  118.3 4.3 %collective-permute-start.12 = (bf16[16,16,128]{2,1,0:T(8,128)(2,1)S(1)}, bf16[16,16,128]{2,1,0:T(8,128)(2,1)S(1)}, u32[]{:S(2)}, u32[]{:S(2)}) collective-permute-start(bf16[16,16,128]{2,1,0:T(8,128)(2,1)S(1)} %get-tuple-element.103.refs_0_), channel_id=1, source_target_pairs={{0,2},{1,3},{2,0},{3,1},{4,6},{5,7},{6,4},{7,5},{8,10},{9,11},{10,... | collective-permute-start | bytes 196616 | tf_op jit(solution)/shard_map/ppermute | solution.py:519
  122.6 1.6 collective-permute-start.15
  145.6 2.0 collective-permute-start.16
  147.7 8.4 %collective-permute-start.17 = (bf16[32,16,128]{2,1,0:T(8,128)(2,1)S(1)}, bf16[32,16,128]{2,1,0:T(8,128)(2,1)S(1)}, u32[]{:S(2)}, u32[]{:S(2)}) collective-permute-start(bf16[32,16,128]{2,1,0:T(8,128)(2,1)S(1)} %get-tuple-element.118), channel_id=1, source_target_pairs={{0,2},{1,3},{2,4},{3,5},{4,6},{5,7},{6,0},{7,1},{8,10},{9,11},{10,... | collective-permute-start | bytes 393224 | tf_op jit(solution)/shard_map/ppermute | solution.py:523
  148.6 7.6 %collective-permute-start.18 = (bf16[32,16,128]{2,1,0:T(8,128)(2,1)S(1)}, bf16[32,16,128]{2,1,0:T(8,128)(2,1)S(1)}, u32[]{:S(2)}, u32[]{:S(2)}) collective-permute-start(bf16[32,16,128]{2,1,0:T(8,128)(2,1)S(1)} %get-tuple-element.119), channel_id=1, source_target_pairs={{0,4},{1,5},{2,6},{3,7},{4,0},{5,1},{6,2},{7,3},{8,12},{9,13},{10,... | collective-permute-start | bytes 393224 | tf_op jit(solution)/shard_map/ppermute | solution.py:523
  149.5 8.4 %collective-permute-start.19 = (bf16[32,16,128]{2,1,0:T(8,128)(2,1)S(1)}, bf16[32,16,128]{2,1,0:T(8,128)(2,1)S(1)}, u32[]{:S(2)}, u32[]{:S(2)}) collective-permute-start(bf16[32,16,128]{2,1,0:T(8,128)(2,1)S(1)} %get-tuple-element.120), channel_id=1, source_target_pairs={{0,6},{1,7},{2,0},{3,1},{4,2},{5,3},{6,4},{7,5},{8,14},{9,15},{10,... | collective-permute-start | bytes 393224 | tf_op jit(solution)/shard_map/ppermute | solution.py:523
  176.4 5.3 %collective-permute-start.22 = (bf16[16,16,128]{2,1,0:T(8,128)(2,1)S(1)}, bf16[16,16,128]{2,1,0:T(8,128)(2,1)S(1)}, u32[]{:S(2)}, u32[]{:S(2)}) collective-permute-start(bf16[16,16,128]{2,1,0:T(8,128)(2,1)S(1)} %get-tuple-element.123.refs_0_), channel_id=1, source_target_pairs={{0,6},{1,7},{2,4},{3,5},{4,2},{5,3},{6,0},{7,1},{8,14},{9,15},{10,... | collective-permute-start | bytes 196616 | tf_op jit(solution)/shard_map/ppermute | solution.py:519
  178.8 5.8 %collective-permute-start.21 = (bf16[16,16,128]{2,1,0:T(8,128)(2,1)S(1)}, bf16[16,16,128]{2,1,0:T(8,128)(2,1)S(1)}, u32[]{:S(2)}, u32[]{:S(2)}) collective-permute-start(bf16[16,16,128]{2,1,0:T(8,128)(2,1)S(1)} %get-tuple-element.123.refs_0_), channel_id=1, source_target_pairs={{0,4},{1,5},{2,6},{3,7},{4,0},{5,1},{6,2},{7,3},{8,12},{9,13},{10,... | collective-permute-start | bytes 196616 | tf_op jit(solution)/shard_map/ppermute | solution.py:519
  181.3 4.3 %collective-permute-start.20 = (bf16[16,16,128]{2,1,0:T(8,128)(2,1)S(1)}, bf16[16,16,128]{2,1,0:T(8,128)(2,1)S(1)}, u32[]{:S(2)}, u32[]{:S(2)}) collective-permute-start(bf16[16,16,128]{2,1,0:T(8,128)(2,1)S(1)} %get-tuple-element.123.refs_0_), channel_id=1, source_target_pairs={{0,2},{1,3},{2,0},{3,1},{4,6},{5,7},{6,4},{7,5},{8,10},{9,11},{10,... | collective-permute-start | bytes 196616 | tf_op jit(solution)/shard_map/ppermute | solution.py:519
  185.6 1.6 collective-permute-start.23

commit v7 on v6

--- a/solution.py
+++ b/solution.py
@@ -350,7 +350,7 @@
             basis[b] = direction
             return acc + fold(direction * image[b].astype(F32))
 
-        acc = lax.fori_loop(0, slots, step, jnp.zeros((8, size), F32), unroll=2)
+        acc = lax.fori_loop(0, slots, step, jnp.zeros((8, size), F32), unroll=4)
         message[...] = jnp.broadcast_to(total(acc)[None], (sectors, 1, size))
 
     return call(
@@ -410,7 +410,7 @@
             return tuple(a + fold(value * o) for a, o in zip(carry, others))
 
         carry = lax.fori_loop(
-            0, slots, step, tuple(jnp.zeros((8, size), F32) for _ in range(k + 1)), unroll=2
+            0, slots, step, tuple(jnp.zeros((8, size), F32) for _ in range(k + 1)), unroll=4
         )
         if last:
             line = lax.broadcasted_iota(jnp.int32, (EXTRA, size), 0)

time: 218 us -> 218 us (level)
  no operation moved by 1% of the time
where the time goes in v7:
time: 218 us
  blocking collectives  113 us (52%)
  waiting for transfers between devices  39.5 us (18%)
  Pallas kernels  35.6 us (16%)
  starting transfers between devices  28 us (13%)
    all_to_all x7, blocking collectives, over_sector(): return lax.all_to_all(values, 'sector', 0, 0, tiled=True)  113 us
    ppermute x9, waiting for transfers between devices, chip_shift(): return lax.ppermute(values, 'mpo', pairs)  17.3 us
    pallas_call x3, Pallas kernels, per_device(): couple_kernel(edges, slots, size, share, group, chips)  16.7 us
    ppermute x9, starting transfers between devices, chip_pair(): return lax.ppermute(values, 'mpo', pairs)  13.9 us
    ppermute x9, starting transfers between devices, chip_shift(): return lax.ppermute(values, 'mpo', pairs)  13.3 us
    ppermute x9, waiting for transfers between devices, chip_pair(): return lax.ppermute(values, 'mpo', pairs)  12 us
    ppermute x3, waiting for transfers between devices, per_device(): received = lax.ppermute(send, 'mpo', core_swap)  5.69 us
    ppermute x3, waiting for transfers between devices, per_device(): far_rows = lax.ppermute(near_rows, 'mpo', core_swap)  4.57 us
  transfers between devices with their start and end apart: 24, of which 22 were waited for; matrix products, arithmetic and copies ran while one was open for 0% of the time, Pallas kernels for 0%

profile of v7, /device:TPU:4, one launch (start us, length us, event | category | flops | bytes accessed | tf_op | source)
XLA Modules:
  0.0 217.6 jit_solution(6857162205194508873)
XLA Ops:
  1.5 4.4 %start.1 = (f32[16,128,128]{2,1,0:T(8,128)S(1)}, bf16[16,128,128]{2,1,0:T(8,128)(2,1)S(1)}, f32[16,16,128]{2,1,0:T(8,128)S(1)}, f32[8,128]{1,0:T(8,128)S(1)}, f3...) custom-call(s32[193]{0:T(256)S(1)} %concatenate.3.meta, ...), custom_call_target="tpu_custom_call" | custom-call | tf_op jit(solution)/shard_map/start/pallas_call | solution.py:528
  5.9 5.6 %couple.3 = (bf16[4,32,16,128]{3,2,1,0:T(8,128)(2,1)S(1)}, bf16[4,32,16,128]{3,2,1,0:T(8,128)(2,1)S(1)}, bf16[8,16,128,128]{3,2,1,0:T(8,128)(2,1)S(1)}, bf16[8,16,128,128]{3,2,1,0:T(8,128)(2,1)S(1)}) custom-call(s32[193]{0:T(256)S(1)} %concatenate.3.meta, ...), custom_call_target="tpu_custom_call", output_to_operand_aliasing={{2}: (2, {}), {3}: (3, {})} | custom-call | tf_op jit(solution)/shard_map/couple/pallas_call | solution.py:533
  11.5 1.9 collective-permute-done.received
  15.9 2.5 %collective-permute-start.3 = (bf16[32,16,128]{2,1,0:T(8,128)(2,1)S(1)}, bf16[32,16,128]{2,1,0:T(8,128)(2,1)S(1)}, u32[]{:S(2)}, u32[]{:S(2)}) collective-permute-start(bf16[32,16,128]{2,1,0:T(8,128)(2,1)S(1)} %get-tuple-element.79), channel_id=1, source_target_pairs={{0,6},{1,7},{2,0},{3,1},{4,2},{5,3},{6,4},{7,5},{8,14},{9,15},{10,... | collective-permute-start | bytes 393224 | tf_op jit(solution)/shard_map/ppermute | solution.py:523
  19.3 3.2 %collective-permute-done.2.third = bf16[32,16,128]{2,1,0:T(8,128)(2,1)S(1)} collective-permute-done((bf16[32,16,128]{2,1,0:T(8,128)(2,1)S(1)}, bf16[32,16,128]{2,1,0:T(8,128)(2,1)S(1)}, u32[]{:S(2)}, u32[]{:S(2)}) %collective-permute-start.2) | collective-permute-done | bytes 131104 | tf_op jit(solution)/shard_map/ppermute | solution.py:523
  24.6 24.7 %all_to_all.35.arrived = bf16[32,40,128]{2,1,0:T(8,128)(2,1)S(1)} all-to-all(bf16[32,40,128]{2,1,0:T(8,128)(2,1)S(1)} %pack.3), channel_id=1, replica_groups=mesh['sector'=32,'mpo'=8] {'sector'}, dimensions={0} | all-to-all | bytes 655360 | tf_op jit(solution)/shard_map/all_to_all | solution.py:515
  49.3 2.2 %image.3 = (f32[16,16,128]{2,1,0:T(8,128)S(1)}, f32[16,16,128]{2,1,0:T(8,128)S(1)}, bf16[16,16,128]{2,1,0:T(8,128)(2,1)S(1)}, f32[24,128]{1,0:T(8,128)S(1)}, s32[64]{0:T(128)S(1)}) custom-call(s32[193]{0:T(256)S(1)} %concatenate.3.meta, bf16[32,40,128]{2,1,0:T(8,128)(2,1)S(1)} %all_to_all.35.arrived, f32[16,16,128]{2,1,0:T(8,128)S(1)} %get-tuple-element.80.vector, ...), custom_call_target="tpu_custom_call" | custom-call | tf_op jit(solution)/shard_map/image/pallas_call | solution.py:541
  52.4 2.5 %collective-permute-start.5 = (bf16[16,16,128]{2,1,0:T(8,128)(2,1)S(1)}, bf16[16,16,128]{2,1,0:T(8,128)(2,1)S(1)}, u32[]{:S(2)}, u32[]{:S(2)}) collective-permute-start(bf16[16,16,128]{2,1,0:T(8,128)(2,1)S(1)} %get-tuple-element.82.refs_0_), channel_id=1, source_target_pairs={{0,4},{1,5},{2,6},{3,7},{4,0},{5,1},{6,2},{7,3},{8,12},{9,13},{10,... | collective-permute-start | bytes 196616 | tf_op jit(solution)/shard_map/ppermute | solution.py:519
  55.9 2.3 %collective-permute-done.5.refs_2_ = bf16[16,16,128]{2,1,0:T(8,128)(2,1)S(1)} collective-permute-done((bf16[16,16,128]{2,1,0:T(8,128)(2,1)S(1)}, bf16[16,16,128]{2,1,0:T(8,128)(2,1)S(1)}, u32[]{:S(2)}, u32[]{:S(2)}) %collective-permute-start.5) | collective-permute-done | bytes 65568 | tf_op jit(solution)/shard_map/ppermute | solution.py:519
  61.7 13.8 %all_to_all.36.thetas = f32[32,1,128]{2,1,0:T(1,128)S(1)} all-to-all(f32[32,1,128]{2,1,0:T(1,128)S(1)} %get-tuple-element.85), channel_id=1, replica_groups=mesh['sector'=32,'mpo'=8] {'sector'}, dimensions={0} | all-to-all | bytes 32768 | tf_op jit(solution)/shard_map/all_to_all | solution.py:515
  76.8 5.6 %couple.4 = (bf16[4,32,16,128]{3,2,1,0:T(8,128)(2,1)S(1)}, bf16[4,32,16,128]{3,2,1,0:T(8,128)(2,1)S(1)}, bf16[8,16,128,128]{3,2,1,0:T(8,128)(2,1)S(1)}, bf16[8,16,128,128]{3,2,1,0:T(8,128)(2,1)S(1)}) custom-call(s32[193]{0:T(256)S(1)} %concatenate.3.meta, ...), custom_call_target="tpu_custom_call", output_to_operand_aliasing={{2}: (2, {}), {3}: (3, {})} | custom-call | tf_op jit(solution)/shard_map/couple/pallas_call | solution.py:533
  82.6 1.9 collective-permute-done.8.received
  86.5 2.4 %collective-permute-start.11 = (bf16[32,16,128]{2,1,0:T(8,128)(2,1)S(1)}, bf16[32,16,128]{2,1,0:T(8,128)(2,1)S(1)}, u32[]{:S(2)}, u32[]{:S(2)}) collective-permute-start(bf16[32,16,128]{2,1,0:T(8,128)(2,1)S(1)} %get-tuple-element.99), channel_id=1, source_target_pairs={{0,6},{1,7},{2,0},{3,1},{4,2},{5,3},{6,4},{7,5},{8,14},{9,15},{10,... | collective-permute-start | bytes 393224 | tf_op jit(solution)/shard_map/ppermute | solution.py:523
  88.9 4.2 %collective-permute-done.9.second = bf16[32,16,128]{2,1,0:T(8,128)(2,1)S(1)} collective-permute-done((bf16[32,16,128]{2,1,0:T(8,128)(2,1)S(1)}, bf16[32,16,128]{2,1,0:T(8,128)(2,1)S(1)}, u32[]{:S(2)}, u32[]{:S(2)}) %collective-permute-start.9) | collective-permute-done | bytes 131104 | tf_op jit(solution)/shard_map/ppermute | solution.py:523
  93.1 1.8 collective-permute-done.11.fourth
  95.6 16.8 %all_to_all.37.arrived = bf16[32,40,128]{2,1,0:T(8,128)(2,1)S(1)} all-to-all(bf16[32,40,128]{2,1,0:T(8,128)(2,1)S(1)} %pack.4), channel_id=1, replica_groups=mesh['sector'=32,'mpo'=8] {'sector'}, dimensions={0} | all-to-all | bytes 655360 | tf_op jit(solution)/shard_map/all_to_all | solution.py:515
  113.3 2.3 %collective-permute-start.14 = (bf16[16,16,128]{2,1,0:T(8,128)(2,1)S(1)}, bf16[16,16,128]{2,1,0:T(8,128)(2,1)S(1)}, u32[]{:S(2)}, u32[]{:S(2)}) collective-permute-start(bf16[16,16,128]{2,1,0:T(8,128)(2,1)S(1)} %get-tuple-element.103.refs_0_), channel_id=1, source_target_pairs={{0,6},{1,7},{2,4},{3,5},{4,2},{5,3},{6,0},{7,1},{8,14},{9,15},{10,... | collective-permute-start | bytes 196616 | tf_op jit(solution)/shard_map/ppermute | solution.py:519
  115.7 2.5 %collective-permute-start.13 = (bf16[16,16,128]{2,1,0:T(8,128)(2,1)S(1)}, bf16[16,16,128]{2,1,0:T(8,128)(2,1)S(1)}, u32[]{:S(2)}, u32[]{:S(2)}) collective-permute-start(bf16[16,16,128]{2,1,0:T(8,128)(2,1)S(1)} %get-tuple-element.103.refs_0_), channel_id=1, source_target_pairs={{0,4},{1,5},{2,6},{3,7},{4,0},{5,1},{6,2},{7,3},{8,12},{9,13},{10,... | collective-permute-start | bytes 196616 | tf_op jit(solution)/shard_map/ppermute | solution.py:519
  118.6 2.8 %collective-permute-done.13.refs_2_ = bf16[16,16,128]{2,1,0:T(8,128)(2,1)S(1)} collective-permute-done((bf16[16,16,128]{2,1,0:T(8,128)(2,1)S(1)}, bf16[16,16,128]{2,1,0:T(8,128)(2,1)S(1)}, u32[]{:S(2)}, u32[]{:S(2)}) %collective-permute-start.13) | collective-permute-done | bytes 65568 | tf_op jit(solution)/shard_map/ppermute | solution.py:519
  122.6 1.5 collective-permute-done.15.other
  125.1 13.5 %all_to_all.38.thetas = f32[32,1,128]{2,1,0:T(1,128)S(1)} all-to-all(f32[32,1,128]{2,1,0:T(1,128)S(1)} %get-tuple-element.106), channel_id=1, replica_groups=mesh['sector'=32,'mpo'=8] {'sector'}, dimensions={0} | all-to-all | bytes 32768 | tf_op jit(solution)/shard_map/all_to_all | solution.py:515
  139.9 5.6 %couple.5 = (bf16[4,32,16,128]{3,2,1,0:T(8,128)(2,1)S(1)}, bf16[4,32,16,128]{3,2,1,0:T(8,128)(2,1)S(1)}, bf16[8,16,128,128]{3,2,1,0:T(8,128)(2,1)S(1)}, bf16[8,16,128,128]{3,2,1,0:T(8,128)(2,1)S(1)}) custom-call(s32[193]{0:T(256)S(1)} %concatenate.3.meta, ...), custom_call_target="tpu_custom_call", output_to_operand_aliasing={{2}: (2, {}), {3}: (3, {})} | custom-call | tf_op jit(solution)/shard_map/couple/pallas_call | solution.py:533
  145.6 1.9 collective-permute-done.16.received
  149.4 2.4 %collective-permute-start.19 = (bf16[32,16,128]{2,1,0:T(8,128)(2,1)S(1)}, bf16[32,16,128]{2,1,0:T(8,128)(2,1)S(1)}, u32[]{:S(2)}, u32[]{:S(2)}) collective-permute-start(bf16[32,16,128]{2,1,0:T(8,128)(2,1)S(1)} %get-tuple-element.120), channel_id=1, source_target_pairs={{0,6},{1,7},{2,0},{3,1},{4,2},{5,3},{6,4},{7,5},{8,14},{9,15},{10,... | collective-permute-start | bytes 393224 | tf_op jit(solution)/shard_map/ppermute | solution.py:523
  151.9 4.2 %collective-permute-done.17.second = bf16[32,16,128]{2,1,0:T(8,128)(2,1)S(1)} collective-permute-done((bf16[32,16,128]{2,1,0:T(8,128)(2,1)S(1)}, bf16[32,16,128]{2,1,0:T(8,128)(2,1)S(1)}, u32[]{:S(2)}, u32[]{:S(2)}) %collective-permute-start.17) | collective-permute-done | bytes 131104 | tf_op jit(solution)/shard_map/ppermute | solution.py:523
  156.1 1.8 collective-permute-done.19.fourth
  158.6 16.8 %all_to_all.39.arrived = bf16[32,40,128]{2,1,0:T(8,128)(2,1)S(1)} all-to-all(bf16[32,40,128]{2,1,0:T(8,128)(2,1)S(1)} %pack.5), channel_id=1, replica_groups=mesh['sector'=32,'mpo'=8] {'sector'}, dimensions={0} | all-to-all | bytes 655360 | tf_op jit(solution)/shard_map/all_to_all | solution.py:515
  176.3 2.3 %collective-permute-start.22 = (bf16[16,16,128]{2,1,0:T(8,128)(2,1)S(1)}, bf16[16,16,128]{2,1,0:T(8,128)(2,1)S(1)}, u32[]{:S(2)}, u32[]{:S(2)}) collective-permute-start(bf16[16,16,128]{2,1,0:T(8,128)(2,1)S(1)} %get-tuple-element.123.refs_0_), channel_id=1, source_target_pairs={{0,6},{1,7},{2,4},{3,5},{4,2},{5,3},{6,0},{7,1},{8,14},{9,15},{10,... | collective-permute-start | bytes 196616 | tf_op jit(solution)/shard_map/ppermute | solution.py:519
  178.7 2.5 %collective-permute-start.21 = (bf16[16,16,128]{2,1,0:T(8,128)(2,1)S(1)}, bf16[16,16,128]{2,1,0:T(8,128)(2,1)S(1)}, u32[]{:S(2)}, u32[]{:S(2)}) collective-permute-start(bf16[16,16,128]{2,1,0:T(8,128)(2,1)S(1)} %get-tuple-element.123.refs_0_), channel_id=1, source_target_pairs={{0,4},{1,5},{2,6},{3,7},{4,0},{5,1},{6,2},{7,3},{8,12},{9,13},{10,... | collective-permute-start | bytes 196616 | tf_op jit(solution)/shard_map/ppermute | solution.py:519
  181.6 2.8 %collective-permute-done.21.refs_2_ = bf16[16,16,128]{2,1,0:T(8,128)(2,1)S(1)} collective-permute-done((bf16[16,16,128]{2,1,0:T(8,128)(2,1)S(1)}, bf16[16,16,128]{2,1,0:T(8,128)(2,1)S(1)}, u32[]{:S(2)}, u32[]{:S(2)}) %collective-permute-start.21) | collective-permute-done | bytes 65568 | tf_op jit(solution)/shard_map/ppermute | solution.py:519
  188.2 13.5 %all_to_all.40.thetas = f32[32,1,128]{2,1,0:T(1,128)S(1)} all-to-all(f32[32,1,128]{2,1,0:T(1,128)S(1)} %get-tuple-element.126), channel_id=1, replica_groups=mesh['sector'=32,'mpo'=8] {'sector'}, dimensions={0} | all-to-all | bytes 32768 | tf_op jit(solution)/shard_map/all_to_all | solution.py:515
  203.2 13.5 %all_to_all.41.sums = f32[32,8,128]{2,1,0:T(8,128)S(1)} all-to-all(f32[32,8,128]{2,1,0:T(8,128)S(1)} %get-tuple-element.132), channel_id=1, replica_groups=mesh['sector'=32,'mpo'=8] {'sector'}, dimensions={0} | all-to-all | bytes 262144 | tf_op jit(solution)/shard_map/all_to_all | solution.py:515
  (49 shorter events, 30.7 us)
Async XLA Ops:
  11.4 64.1 %copy-start = (f32[16,128,128]{2,1,0:T(8,128)S(1)}, f32[16,128,128]{2,1,0:T(8,128)}, u32[]{:S(2)}) copy-start(f32[16,128,128]{2,1,0:T(8,128)} %shift.5) | copy-start | bytes 3145732
  11.4 2.0 collective-permute-start
  13.6 5.7 %collective-permute-start.1 = (bf16[32,16,128]{2,1,0:T(8,128)(2,1)S(1)}, bf16[32,16,128]{2,1,0:T(8,128)(2,1)S(1)}, u32[]{:S(2)}, u32[]{:S(2)}) collective-permute-start(bf16[32,16,128]{2,1,0:T(8,128)(2,1)S(1)} %get-tuple-element.77), channel_id=1, source_target_pairs={{0,2},{1,3},{2,4},{3,5},{4,6},{5,7},{6,0},{7,1},{8,10},{9,11},{10,... | collective-permute-start | bytes 393224 | tf_op jit(solution)/shard_map/ppermute | solution.py:523
  14.9 7.6 %collective-permute-start.2 = (bf16[32,16,128]{2,1,0:T(8,128)(2,1)S(1)}, bf16[32,16,128]{2,1,0:T(8,128)(2,1)S(1)}, u32[]{:S(2)}, u32[]{:S(2)}) collective-permute-start(bf16[32,16,128]{2,1,0:T(8,128)(2,1)S(1)} %get-tuple-element.78), channel_id=1, source_target_pairs={{0,4},{1,5},{2,6},{3,7},{4,0},{5,1},{6,2},{7,3},{8,12},{9,13},{10,... | collective-permute-start | bytes 393224 | tf_op jit(solution)/shard_map/ppermute | solution.py:523
  15.9 7.8 %collective-permute-start.3 = (bf16[32,16,128]{2,1,0:T(8,128)(2,1)S(1)}, bf16[32,16,128]{2,1,0:T(8,128)(2,1)S(1)}, u32[]{:S(2)}, u32[]{:S(2)}) collective-permute-start(bf16[32,16,128]{2,1,0:T(8,128)(2,1)S(1)} %get-tuple-element.79), channel_id=1, source_target_pairs={{0,6},{1,7},{2,0},{3,1},{4,2},{5,3},{6,4},{7,5},{8,14},{9,15},{10,... | collective-permute-start | bytes 393224 | tf_op jit(solution)/shard_map/ppermute | solution.py:523
  51.5 4.4 %collective-permute-start.6 = (bf16[16,16,128]{2,1,0:T(8,128)(2,1)S(1)}, bf16[16,16,128]{2,1,0:T(8,128)(2,1)S(1)}, u32[]{:S(2)}, u32[]{:S(2)}) collective-permute-start(bf16[16,16,128]{2,1,0:T(8,128)(2,1)S(1)} %get-tuple-element.82.refs_0_), channel_id=1, source_target_pairs={{0,6},{1,7},{2,4},{3,5},{4,2},{5,3},{6,0},{7,1},{8,14},{9,15},{10,... | collective-permute-start | bytes 196616 | tf_op jit(solution)/shard_map/ppermute | solution.py:519
  52.4 5.8 %collective-permute-start.5 = (bf16[16,16,128]{2,1,0:T(8,128)(2,1)S(1)}, bf16[16,16,128]{2,1,0:T(8,128)(2,1)S(1)}, u32[]{:S(2)}, u32[]{:S(2)}) collective-permute-start(bf16[16,16,128]{2,1,0:T(8,128)(2,1)S(1)} %get-tuple-element.82.refs_0_), channel_id=1, source_target_pairs={{0,4},{1,5},{2,6},{3,7},{4,0},{5,1},{6,2},{7,3},{8,12},{9,13},{10,... | collective-permute-start | bytes 196616 | tf_op jit(solution)/shard_map/ppermute | solution.py:519
  54.9 4.3 %collective-permute-start.4 = (bf16[16,16,128]{2,1,0:T(8,128)(2,1)S(1)}, bf16[16,16,128]{2,1,0:T(8,128)(2,1)S(1)}, u32[]{:S(2)}, u32[]{:S(2)}) collective-permute-start(bf16[16,16,128]{2,1,0:T(8,128)(2,1)S(1)} %get-tuple-element.82.refs_0_), channel_id=1, source_target_pairs={{0,2},{1,3},{2,0},{3,1},{4,6},{5,7},{6,4},{7,5},{8,10},{9,11},{10,... | collective-permute-start | bytes 196616 | tf_op jit(solution)/shard_map/ppermute | solution.py:519
  59.2 1.6 collective-permute-start.7
  82.4 2.2 %collective-permute-start.8 = (bf16[4,32,16,128]{3,2,1,0:T(8,128)(2,1)S(1)}, bf16[4,32,16,128]{3,2,1,0:T(8,128)(2,1)S(1)}, u32[]{:S(2)}, u32[]{:S(2)}) collective-permute-start(bf16[4,32,16,128]{3,2,1,0:T(8,128)(2,1)S(1)} %get-tuple-element.95), channel_id=1, source_target_pairs={{0,1},{1,0},{2,3},{3,2},{4,5},{5,4},{6,7},{7,6},{8,9},{9,8},{10,11... | collective-permute-start | bytes 1572872 | tf_op jit(solution)/shard_map/ppermute | solution.py:536
  84.7 8.4 %collective-permute-start.9 = (bf16[32,16,128]{2,1,0:T(8,128)(2,1)S(1)}, bf16[32,16,128]{2,1,0:T(8,128)(2,1)S(1)}, u32[]{:S(2)}, u32[]{:S(2)}) collective-permute-start(bf16[32,16,128]{2,1,0:T(8,128)(2,1)S(1)} %get-tuple-element.97), channel_id=1, source_target_pairs={{0,2},{1,3},{2,4},{3,5},{4,6},{5,7},{6,0},{7,1},{8,10},{9,11},{10,... | collective-permute-start | bytes 393224 | tf_op jit(solution)/shard_map/ppermute | solution.py:523
  85.5 7.6 %collective-permute-start.10 = (bf16[32,16,128]{2,1,0:T(8,128)(2,1)S(1)}, bf16[32,16,128]{2,1,0:T(8,128)(2,1)S(1)}, u32[]{:S(2)}, u32[]{:S(2)}) collective-permute-start(bf16[32,16,128]{2,1,0:T(8,128)(2,1)S(1)} %get-tuple-element.98), channel_id=1, source_target_pairs={{0,4},{1,5},{2,6},{3,7},{4,0},{5,1},{6,2},{7,3},{8,12},{9,13},{10,... | collective-permute-start | bytes 393224 | tf_op jit(solution)/shard_map/ppermute | solution.py:523
  86.5 8.4 %collective-permute-start.11 = (bf16[32,16,128]{2,1,0:T(8,128)(2,1)S(1)}, bf16[32,16,128]{2,1,0:T(8,128)(2,1)S(1)}, u32[]{:S(2)}, u32[]{:S(2)}) collective-permute-start(bf16[32,16,128]{2,1,0:T(8,128)(2,1)S(1)} %get-tuple-element.99), channel_id=1, source_target_pairs={{0,6},{1,7},{2,0},{3,1},{4,2},{5,3},{6,4},{7,5},{8,14},{9,15},{10,... | collective-permute-start | bytes 393224 | tf_op jit(solution)/shard_map/ppermute | solution.py:523
  113.3 5.3 %collective-permute-start.14 = (bf16[16,16,128]{2,1,0:T(8,128)(2,1)S(1)}, bf16[16,16,128]{2,1,0:T(8,128)(2,1)S(1)}, u32[]{:S(2)}, u32[]{:S(2)}) collective-permute-start(bf16[16,16,128]{2,1,0:T(8,128)(2,1)S(1)} %get-tuple-element.103.refs_0_), channel_id=1, source_target_pairs={{0,6},{1,7},{2,4},{3,5},{4,2},{5,3},{6,0},{7,1},{8,14},{9,15},{10,... | collective-permute-start | bytes 196616 | tf_op jit(solution)/shard_map/ppermute | solution.py:519
  115.7 5.8 %collective-permute-start.13 = (bf16[16,16,128]{2,1,0:T(8,128)(2,1)S(1)}, bf16[16,16,128]{2,1,0:T(8,128)(2,1)S(1)}, u32[]{:S(2)}, u32[]{:S(2)}) collective-permute-start(bf16[16,16,128]{2,1,0:T(8,128)(2,1)S(1)} %get-tuple-element.103.refs_0_), channel_id=1, source_target_pairs={{0,4},{1,5},{2,6},{3,7},{4,0},{5,1},{6,2},{7,3},{8,12},{9,13},{10,... | collective-permute-start | bytes 196616 | tf_op jit(solution)/shard_map/ppermute | solution.py:519
  118.2 4.3 %collective-permute-start.12 = (bf16[16,16,128]{2,1,0:T(8,128)(2,1)S(1)}, bf16[16,16,128]{2,1,0:T(8,128)(2,1)S(1)}, u32[]{:S(2)}, u32[]{:S(2)}) collective-permute-start(bf16[16,16,128]{2,1,0:T(8,128)(2,1)S(1)} %get-tuple-element.103.refs_0_), channel_id=1, source_target_pairs={{0,2},{1,3},{2,0},{3,1},{4,6},{5,7},{6,4},{7,5},{8,10},{9,11},{10,... | collective-permute-start | bytes 196616 | tf_op jit(solution)/shard_map/ppermute | solution.py:519
  122.5 1.6 collective-permute-start.15
  145.5 2.0 collective-permute-start.16
  147.7 8.4 %collective-permute-start.17 = (bf16[32,16,128]{2,1,0:T(8,128)(2,1)S(1)}, bf16[32,16,128]{2,1,0:T(8,128)(2,1)S(1)}, u32[]{:S(2)}, u32[]{:S(2)}) collective-permute-start(bf16[32,16,128]{2,1,0:T(8,128)(2,1)S(1)} %get-tuple-element.118), channel_id=1, source_target_pairs={{0,2},{1,3},{2,4},{3,5},{4,6},{5,7},{6,0},{7,1},{8,10},{9,11},{10,... | collective-permute-start | bytes 393224 | tf_op jit(solution)/shard_map/ppermute | solution.py:523
  148.5 7.6 %collective-permute-start.18 = (bf16[32,16,128]{2,1,0:T(8,128)(2,1)S(1)}, bf16[32,16,128]{2,1,0:T(8,128)(2,1)S(1)}, u32[]{:S(2)}, u32[]{:S(2)}) collective-permute-start(bf16[32,16,128]{2,1,0:T(8,128)(2,1)S(1)} %get-tuple-element.119), channel_id=1, source_target_pairs={{0,4},{1,5},{2,6},{3,7},{4,0},{5,1},{6,2},{7,3},{8,12},{9,13},{10,... | collective-permute-start | bytes 393224 | tf_op jit(solution)/shard_map/ppermute | solution.py:523
  149.4 8.4 %collective-permute-start.19 = (bf16[32,16,128]{2,1,0:T(8,128)(2,1)S(1)}, bf16[32,16,128]{2,1,0:T(8,128)(2,1)S(1)}, u32[]{:S(2)}, u32[]{:S(2)}) collective-permute-start(bf16[32,16,128]{2,1,0:T(8,128)(2,1)S(1)} %get-tuple-element.120), channel_id=1, source_target_pairs={{0,6},{1,7},{2,0},{3,1},{4,2},{5,3},{6,4},{7,5},{8,14},{9,15},{10,... | collective-permute-start | bytes 393224 | tf_op jit(solution)/shard_map/ppermute | solution.py:523
  176.3 5.3 %collective-permute-start.22 = (bf16[16,16,128]{2,1,0:T(8,128)(2,1)S(1)}, bf16[16,16,128]{2,1,0:T(8,128)(2,1)S(1)}, u32[]{:S(2)}, u32[]{:S(2)}) collective-permute-start(bf16[16,16,128]{2,1,0:T(8,128)(2,1)S(1)} %get-tuple-element.123.refs_0_), channel_id=1, source_target_pairs={{0,6},{1,7},{2,4},{3,5},{4,2},{5,3},{6,0},{7,1},{8,14},{9,15},{10,... | collective-permute-start | bytes 196616 | tf_op jit(solution)/shard_map/ppermute | solution.py:519
  178.7 5.8 %collective-permute-start.21 = (bf16[16,16,128]{2,1,0:T(8,128)(2,1)S(1)}, bf16[16,16,128]{2,1,0:T(8,128)(2,1)S(1)}, u32[]{:S(2)}, u32[]{:S(2)}) collective-permute-start(bf16[16,16,128]{2,1,0:T(8,128)(2,1)S(1)} %get-tuple-element.123.refs_0_), channel_id=1, source_target_pairs={{0,4},{1,5},{2,6},{3,7},{4,0},{5,1},{6,2},{7,3},{8,12},{9,13},{10,... | collective-permute-start | bytes 196616 | tf_op jit(solution)/shard_map/ppermute | solution.py:519
  181.2 4.3 %collective-permute-start.20 = (bf16[16,16,128]{2,1,0:T(8,128)(2,1)S(1)}, bf16[16,16,128]{2,1,0:T(8,128)(2,1)S(1)}, u32[]{:S(2)}, u32[]{:S(2)}) collective-permute-start(bf16[16,16,128]{2,1,0:T(8,128)(2,1)S(1)} %get-tuple-element.123.refs_0_), channel_id=1, source_target_pairs={{0,2},{1,3},{2,0},{3,1},{4,6},{5,7},{6,4},{7,5},{8,10},{9,11},{10,... | collective-permute-start | bytes 196616 | tf_op jit(solution)/shard_map/ppermute | solution.py:519
  185.5 1.6 collective-permute-start.23
